TPU v7x, 32 devices: a whole 2x2x4 slice. The times are simulated.
32 devices in a mesh: ax: 16 (over z, x, core), az: 2 (over y).
Axes of the slice: x: 2, y: 2, z: 4, core: 2. Of those that a mesh axis runs over, the one named last changes fastest.
Arguments:
- conserved: float32 [64, 5, 32, 512], P('ax', None, None, 'az'), may hold values from -1.1 to 6.2, as said below
- cycle_modes: int32 [32], replicated, may hold values from 1 to 64, as said below
- filtered_cycles: int32 [64], P('ax'), may hold values from 1 to 32, as said below
Outputs:
- stepped: float32 [64, 5, 32, 512], P('ax', None, None, 'az')
Inputs may be any that keep to these rules, and one draw needn't show every extreme that they name: `conserved`: density is at least 0.3 and pressure at least 0.02 in every cell. `cycle_modes`: 64 and 1 both occur. `filtered_cycles`: 32 and 1 both occur.
All inputs are finite; a program needn't handle non-finite values.
Results may differ from a plain program's by a relative error of at most 0.0003.
Values sent between devices are 32-bit elements; how exact they have to be, the bound alone decides.
No kernel may reach another device: no remote copies, remote signals or barrier semaphores. Data moves between devices by JAX's collectives and lax.ppermute only.
A program may use at most 64 MiB of HBM per device.

v0:
```python
import math

import jax
import jax.numpy as jnp
from jax import lax
from jax.sharding import PartitionSpec as P

NT = 512
NRF = 32
MODE_MOST = 64


STENCIL = (0.8, -0.2, 4.0 / 105.0, -1.0 / 280.0)
GAS_FACTOR = 0.4
TIME_STEP = 0.1


def extended(cells, sides, width, closed):
    for axis, dim in sides:
        count = lax.axis_size(axis)
        ends = count if closed else count - 1
        head = lax.slice_in_dim(cells, 0, width, axis=dim)
        tail = lax.slice_in_dim(cells, cells.shape[dim] - width, cells.shape[dim], axis=dim)
        cells = jnp.concatenate(
            [
                lax.ppermute(tail, axis, [(i, (i + 1) % count) for i in range(ends)]),
                cells,
                lax.ppermute(head, axis, [((i + 1) % count, i) for i in range(ends)]),
            ],
            axis=dim,
        )
    return cells


def partner(block, axis, distance):
    count = lax.axis_size(axis)
    route = []
    for low in range(count):
        high = low | 1 << distance
        if high != low and high < count:
            route += [(low, high), (high, low)]
    return lax.ppermute(block, axis, route)


def velocities(fields):
    density = fields[:, 0]
    axial_vel = fields[:, 1] / density
    radial_vel = fields[:, 2] / density
    swirl_vel = fields[:, 3] / density
    kinetic = fields[:, 1] * axial_vel + fields[:, 2] * radial_vel + fields[:, 3] * swirl_vel
    pressure = GAS_FACTOR * (fields[:, 4] - 0.5 * kinetic)
    return (axial_vel, radial_vel, swirl_vel, pressure)


def axial_flux(fields):
    axial_vel, radial_vel, swirl_vel, pressure = velocities(fields)
    return jnp.stack(
        [
            fields[:, 1],
            fields[:, 1] * axial_vel + pressure,
            fields[:, 2] * axial_vel,
            fields[:, 3] * axial_vel,
            axial_vel * (fields[:, 4] + pressure),
        ],
        axis=1,
    )


def radial_flux(fields):
    axial_vel, radial_vel, swirl_vel, pressure = velocities(fields)
    return jnp.stack(
        [
            fields[:, 2],
            fields[:, 1] * radial_vel,
            fields[:, 2] * radial_vel + pressure,
            fields[:, 3] * radial_vel,
            radial_vel * (fields[:, 4] + pressure),
        ],
        axis=1,
    )


def swirl_flux(fields):
    axial_vel, radial_vel, swirl_vel, pressure = velocities(fields)
    return jnp.stack(
        [
            fields[:, 3],
            fields[:, 1] * swirl_vel,
            fields[:, 2] * swirl_vel,
            fields[:, 3] * swirl_vel + pressure,
            swirl_vel * (fields[:, 4] + pressure),
        ],
        axis=1,
    )


def central_difference(values, along, extent):
    result = None
    for offset, weight in zip((1, 2, 3, 4), STENCIL):
        forward_part = lax.slice_in_dim(values, 4 + offset, 4 + offset + extent, axis=along)
        backward_part = lax.slice_in_dim(values, 4 - offset, 4 - offset + extent, axis=along)
        contribution = weight * (forward_part - backward_part)
        result = contribution if result is None else result + contribution
    return result


def section_update(axial_padded, theta_padded, opposite, fields):
    stations = fields.shape[0]
    radial = fields.shape[2]
    width = fields.shape[3]
    axial_term = central_difference(axial_flux(axial_padded), 0, stations)
    flips = jnp.array([1.0, 1.0, -1.0, -1.0, 1.0], jnp.float32).reshape(1, 5, 1, 1)
    mirrored = opposite[:, :, ::-1, :] * flips
    outer_rows = jnp.broadcast_to(fields[:, :, -1:, :], (stations, 5, 4, width))
    radial_padded = jnp.concatenate([mirrored, fields, outer_rows], axis=2)
    signed_radius = (jnp.arange(radial + 8, dtype=jnp.float32) - 3.5).reshape(1, 1, -1, 1)
    radial_term = central_difference(radial_flux(radial_padded) * signed_radius, 2, radial)
    swirl_term = central_difference(swirl_flux(theta_padded), 3, width) * (NT / (2.0 * math.pi))
    axial_vel, radial_vel, swirl_vel, pressure = velocities(fields)
    nothing = jnp.zeros_like(pressure)
    source = jnp.stack(
        [nothing, nothing, fields[:, 3] * swirl_vel + pressure, -fields[:, 2] * swirl_vel, nothing],
        axis=1,
    )
    radius = (jnp.arange(radial, dtype=jnp.float32) + 0.5).reshape(1, 1, -1, 1)
    tendency = -axial_term - (radial_term + swirl_term - source) / radius
    return fields + TIME_STEP * tendency


def fourier_basis(columns):
    harmonic = jnp.arange(2 * MODE_MOST, dtype=jnp.int32) % MODE_MOST
    product = columns[:, None] * harmonic[None, :] % NT
    angle = product.astype(jnp.float32) * (2.0 * math.pi / NT)
    cosine_side = (jnp.arange(2 * MODE_MOST, dtype=jnp.int32) < MODE_MOST)[None, :]
    return jnp.where(cosine_side, jnp.cos(angle), jnp.sin(angle))


def mode_weights(cycle_modes):
    harmonic = jnp.arange(2 * MODE_MOST, dtype=jnp.int32) % MODE_MOST
    base_weight = jnp.where(harmonic == 0, 1.0 / NT, 2.0 / NT).astype(jnp.float32)
    keep = harmonic[None, :] < cycle_modes[:, None]
    return jnp.where(keep, base_weight[None, :], 0.0)


def per_device(conserved, cycle_modes, filtered_cycles):
    axial_padded = extended(conserved, (("ax", 0),), 4, False)
    theta_padded = extended(conserved, (("az", 3),), 4, True)
    position = lax.axis_index("ax")
    last_index = lax.axis_size("ax") - 1
    low_edge = jnp.broadcast_to(conserved[:1], (4,) + conserved.shape[1:])
    high_edge = jnp.broadcast_to(conserved[-1:], (4,) + conserved.shape[1:])
    axial_padded = jnp.concatenate(
        [
            jnp.where(position == 0, low_edge, axial_padded[:4]),
            axial_padded[4:-4],
            jnp.where(position == last_index, high_edge, axial_padded[-4:]),
        ],
        axis=0,
    )
    partner_bit = lax.axis_size("az").bit_length() - 2
    opposite = partner(conserved[:, :, :4, :], "az", partner_bit)
    section = section_update(axial_padded, theta_padded, opposite, conserved)
    kept_weights = mode_weights(cycle_modes)
    sector = lax.axis_index("az")
    per_sector = NRF // lax.axis_size("az")
    lines = lax.all_to_all(section, "az", split_axis=2, concat_axis=3, tiled=True)
    full_basis = fourier_basis(jnp.arange(NT, dtype=jnp.int32))
    local_weights = lax.dynamic_slice_in_dim(kept_weights, sector * per_sector, per_sector, 0)
    coefficients = jnp.einsum("afrt,tc->afrc", lines, full_basis, precision=lax.Precision.HIGHEST)
    smoothed = jnp.einsum(
        "afrc,tc->afrt",
        coefficients * local_weights[None, None],
        full_basis,
        precision=lax.Precision.HIGHEST,
    )
    local_ids = sector * per_sector + jnp.arange(per_sector, dtype=jnp.int32)
    chosen = jnp.where(
        local_ids[None, None, :, None] < filtered_cycles[:, None, None, None], smoothed, lines
    )
    result_cycles = lax.all_to_all(chosen, "az", split_axis=3, concat_axis=2, tiled=True)
    return jnp.concatenate([result_cycles, section[:, :, NRF:, :]], axis=2)


def solution(mesh):
    placed = (P("ax", None, None, "az"), P(), P("ax"))
    return jax.shard_map(
        per_device, mesh=mesh, in_specs=placed, out_specs=P("ax", None, None, "az"), check_vma=False
    )
```

profile of v0, /device:TPU:0, one launch (start us, length us, event | category | flops | bytes accessed | tf_op | source)
XLA Modules:
  0.0 92.6 jit_solution(8275054431332127691)
XLA Ops:
  0.0 1.4 %collective-permute-start.1 = (f32[4,5,32,256]{3,2,1,0:T(8,128)}, f32[4,5,32,256]{3,2,1,0:T(8,128)S(1)}, u32[]{:S(2)}, u32[]{:S(2)}) collective-permute-start(f32[4,5,32,256]{3,2,1,0:T(8,128)} %param.4), channel_id=1, source_target_pairs={{2,0},{4,2},{6,4},{8,6},{10,8},{12,10},{14,12},{16,14},{18,16},{20... | collective-permute-start | bytes 1966088 | tf_op jit(solution)/shard_map/ppermute | solution.py:28
  1.4 3.1 %collective-permute-start = (f32[4,5,32,256]{3,2,1,0:T(8,128)}, f32[4,5,32,256]{3,2,1,0:T(8,128)S(1)}, u32[]{:S(2)}, u32[]{:S(2)}) collective-permute-start(f32[4,5,32,256]{3,2,1,0:T(8,128)} %param.4), channel_id=1, source_target_pairs={{0,2},{2,4},{4,6},{6,8},{8,10},{10,12},{12,14},{14,16},{16,18},{18... | collective-permute-start | bytes 1966088 | tf_op jit(solution)/shard_map/ppermute | solution.py:26
  4.5 1.2 %fusion.67 = (f32[4,5,32,4]{3,2,1,0:T(8,128)S(1)}, f32[4,5,32,4]{3,2,1,0:T(8,128)S(1)}) fusion(f32[4,5,32,256]{3,2,1,0:T(8,128)} %param.4), kind=kLoop, calls=%fused_computation.133 | loop fusion | bytes 40960 | tf_op jit(solution)/shard_map/slice | solution.py:23
  5.7 3.1 %collective-permute-start.3 = (f32[4,5,32,4]{3,2,1,0:T(8,128)S(1)}, f32[4,5,32,4]{3,2,1,0:T(8,128)S(1)}, u32[]{:S(2)}, u32[]{:S(2)}) collective-permute-start(f32[4,5,32,4]{3,2,1,0:T(8,128)S(1)} %get-tuple-element.18), channel_id=1, source_target_pairs={{0,1},{1,0},{2,3},{3,2},{4,5},{5,4},{6,7},{7,6},{8,9},{9,8},{10,11... | collective-permute-start | bytes 30728 | tf_op jit(solution)/shard_map/ppermute | solution.py:26
  8.8 0.1 collective-permute-start.4
  8.9 1.6 %slice.194 = f32[4,5,4,256]{3,2,1,0:T(4,128)} slice(f32[4,5,32,256]{3,2,1,0:T(8,128)} %param.4), slice={[0:4], [0:5], [0:4], [0:256]} | slice | bytes 163840 | tf_op jit(solution)/shard_map/slice | solution.py:161
  10.4 1.9 %collective-permute-start.2 = (f32[4,5,4,256]{3,2,1,0:T(4,128)}, f32[4,5,4,256]{3,2,1,0:T(4,128)}, u32[]{:S(2)}, u32[]{:S(2)}) collective-permute-start(f32[4,5,4,256]{3,2,1,0:T(4,128)} %slice.194), channel_id=1, source_target_pairs={{0,1},{1,0},{2,3},{3,2},{4,5},{5,4},{6,7},{7,6},{8,9},{9,8},{10,11... | collective-permute-start | bytes 245768 | tf_op jit(solution)/shard_map/ppermute | solution.py:42
  12.4 1.0 %slice_bitcast_fusion.1 = (f32[5,32,256]{2,1,0:T(8,128)S(1)}, f32[5,32,256]{2,1,0:T(8,128)S(1)}) fusion(f32[4,5,32,256]{3,2,1,0:T(8,128)} %param.4), kind=kLoop, calls=%fused_computation.103 | loop fusion | bytes 655360 | tf_op jit(solution)/shard_map/broadcast_in_dim | solution.py:150
  13.4 0.6 iota_add_fusion.1
  14.0 0.0 copy-done
  14.0 0.1 fusion.55
  14.1 0.5 and_select_fusion
  14.6 0.0 copy-done.6
  14.6 0.6 broadcast_compare_fusion
  15.2 0.6 compare_select_fusion.1
  15.8 0.6 slice.195
  16.4 0.7 copy.42
  17.1 0.6 copy.33
  17.8 0.1 pad.3.clone
  17.8 1.3 %dynamic-slice = s32[16]{0:T(128)} dynamic-slice(s32[32]{0:T(128)} %param.5, s32[]{:T(128)S(6)} %select_n.78), dynamic_slice_sizes={16} | dynamic-slice | bytes 132 | tf_op jit(solution)/shard_map/dynamic_slice | solution.py:168
  19.1 0.0 collective-permute-done.3
  19.1 4.8 %collective-permute-done.4 = f32[4,5,32,4]{3,2,1,0:T(8,128)} collective-permute-done((f32[4,5,32,4]{3,2,1,0:T(8,128)S(1)}, f32[4,5,32,4]{3,2,1,0:T(8,128)}, u32[]{:S(2)}, u32[]{:S(2)}) %collective-permute-start.4) | collective-permute-done | bytes 10272 | tf_op jit(solution)/shard_map/ppermute | solution.py:28
  23.9 1.4 %pad_maximum_fusion.1 = f32[4,5,32,264]{3,2,1,0:T(8,128)S(1)} fusion(f32[4,5,32,4]{3,2,1,0:T(8,128)} %collective-permute-done.4, f32[4,5,32,256]{3,2,1,0:T(8,128)S(1)} %copy-done, f32[4,5,32,4]{3,2,1,0:T(8,128)S(1)} %collective-permute-done.3), kind=kLoop, calls=%fused_computation.3 | loop fusion | flops 337920 | bytes 1351680 | tf_op jit(solution)/shard_map/concatenate | solution.py:24
  25.3 0.0 copy-start.1
  25.4 0.1 add_dynamic-update-slice_fusion.1
  25.5 0.1 collective-permute-done.2
  25.7 1.5 %rev.3 = f32[4,5,4,256]{3,2,1,0:T(4,128)} reverse(f32[4,5,4,256]{3,2,1,0:T(4,128)} %collective-permute-done.2), dimensions={2} | reverse | bytes 163840 | tf_op jit(solution)/shard_map/rev | solution.py:113
  27.2 0.0 copy-done.1
  27.2 1.0 %broadcast_multiply_fusion.1 = f32[4,5,4,256]{3,2,1,0:T(4,128)S(1)} fusion(f32[4,5,4,256]{3,2,1,0:T(4,128)} %rev.3, f32[5]{0:T(128)S(1)} %copy-done.1), kind=kLoop, calls=%fused_computation.115 | loop fusion | flops 20480 | bytes 163860 | tf_op jit(solution)/shard_map/mul | solution.py:113
  28.1 0.8 broadcast_in_dim.74
  28.9 0.1 pad_maximum_fusion.2
  29.0 0.0 copy-start.2
  29.1 0.1 add_dynamic-update-slice_fusion.2
  29.3 0.4 copy-done.2
  29.7 0.1 broadcast_multiply_fusion
  29.8 0.0 collective-permute-done.1
  29.8 0.1 broadcast_select_fusion
  29.9 0.0 collective-permute-done
  29.9 0.1 broadcast_select_fusion.1
  30.0 0.2 pad_maximum_fusion
  30.3 0.2 add_dynamic-update-slice_fusion
  30.5 0.1 multiply_dynamic-update-slice_fusion.2
  30.5 0.1 multiply_dynamic-update-slice_fusion.1
  30.6 0.1 multiply_dynamic-update-slice_fusion
  30.7 1.5 %multiply_add_fusion = f32[4,5,32,256]{3,2,1,0:T(8,128)S(1)} fusion(f32[4,5,32,256]{3,2,1,0:T(8,128)S(1)} %copy-done, f32[4,1,32,256]{3,2,1,0:T(8,128)S(1)} %get-tuple-element.21, f32[4,1,32,256]{3,2,1,0:T(8,128)S(1)} %get-tuple-element.20, f32[4,5,32,264]{3,2,1,0:T(8,128)S(1)} %multiply_dynamic-update-slice_fusion.3, ...), kind=kLoop, calls=%fused_computation.45 | loop fusion | flops 7208960 | bytes 17301672 | tf_op jit(solution)/shard_map/add | solution.py:127
  32.3 0.0 copy-start.3
  32.3 0.0 copy-start.4
  32.3 0.0 copy-start.5
  32.3 1.4 %copy.34 = f32[4,5,32,256]{3,1,0,2:T(8,128)} copy(f32[4,5,32,256]{3,2,1,0:T(8,128)S(1)} %multiply_add_fusion) | data formatting | bytes 1310720 | tf_op jit(solution)/shard_map/add | solution.py:127
  33.7 3.7 %all-to-all-start = ((f32[4,5,32,256]{3,1,0,2:T(8,128)}), f32[4,5,32,256]{3,1,0,2:T(8,128)S(1)}, u32[]{:S(2)}, u32[]{:S(2)}) async-start(f32[4,5,32,256]{3,1,0,2:T(8,128)} %copy.34), calls=%async_computation | async-start | bytes 2097152 | tf_op jit(solution)/shard_map/all_to_all | solution.py:166
  37.5 0.1 compare_select_fusion
  37.5 15.0 %all-to-all-done = f32[4,5,32,256]{3,1,0,2:T(8,128)S(1)} async-done(((f32[4,5,32,256]{3,1,0,2:T(8,128)}), f32[4,5,32,256]{3,1,0,2:T(8,128)S(1)}, u32[]{:S(2)}, u32[]{:S(2)}) %all-to-all-start) | async-done | bytes 655392 | tf_op jit(solution)/shard_map/all_to_all | solution.py:166
  52.5 0.5 copy.41
  53.0 0.5 all_to_all.29
  53.5 1.7 %convolution_multiply_fusion = f32[4,5,16,128]{3,2,1,0:T(8,128)S(1)} fusion(f32[4,5,16,512]{3,2,1,0:T(8,128)S(1)} %all_to_all.29, s32[128]{0:T(128)S(1)} %copy-done.3, pred[128]{0:T(512)(128)(4,1)S(1)} %iota_compare_fusion, f32[16,128]{1,0:T(8,128)S(1)} %compare_select_fusion), kind=kOutput, calls=%fused_computation.2 | convolution fusion | flops 252682240 | bytes 828032 | tf_op jit(solution)/shard_map/afrt,tc->afrc/dot_general | solution.py:169
  55.2 0.0 copy-done.7
  55.3 1.7 %convolution_select_fusion = f32[4,5,16,512]{3,2,1,0:T(8,128)S(1)} fusion(f32[4,5,16,512]{3,2,1,0:T(8,128)S(1)} %all_to_all.29, f32[4,5,16,128]{3,2,1,0:T(8,128)S(1)} %convolution_multiply_fusion, pred[4,16]{1,0:T(4,128)(4,1)S(1)} %copy-done.7, s32[128]{0:T(128)S(1)} %copy-done.3, pred[128]{0:T(512)(128)(4,1)S(1)} %iota_compare_fusion), kind=kOutput, calls=%fused_computation.1 | convolution fusion | flops 252805120 | bytes 1475264 | tf_op jit(solution)/shard_map/afrc,tc->afrt/dot_general | solution.py:170
  57.0 3.5 %copy.36 = f32[4,5,16,512]{2,0,1,3:T(4,128)} copy(f32[4,5,16,512]{3,2,1,0:T(8,128)S(1)} %convolution_select_fusion) | data formatting | bytes 1310720 | tf_op jit(solution)/shard_map/jit(_where)/select_n | solution.py:177
  60.5 5.7 %reshape.69 = f32[2,1,81920]{2,1,0:T(1,128)S(1)} reshape(f32[512,5,4,16]{3,2,1,0:T(4,128)} %bitcast.27) | data formatting | bytes 1310720
  66.2 12.1 %all_to_all.36 = f32[2,1,81920]{2,1,0:T(1,128)S(1)} all-to-all(f32[2,1,81920]{2,1,0:T(1,128)S(1)} %reshape.69), channel_id=1, replica_groups=mesh['ax'=16,'az'=2] {'az'}, dimensions={0} | all-to-all | bytes 1310720 | tf_op jit(solution)/shard_map/all_to_all | solution.py:180
  78.3 0.5 broadcast.144
  78.8 2.7 %reduce = f32[2,81920]{1,0:T(2,128)S(1)} reduce(f32[2,1,81920]{2,1,0:T(1,128)S(1)} %all_to_all.36, f32[]{:T(128)} %broadcast.144), dimensions={1}, to_apply=%all_to_all.30.reduce_sub_computation | reduce | bytes 1310724 | tf_op jit(solution)/shard_map/all_to_all | solution.py:180
  81.5 6.3 %reshape.70 = f32[512,5,4,16]{3,2,1,0:T(4,128)} reshape(f32[2,81920]{1,0:T(2,128)S(1)} %reduce) | data formatting | bytes 1310720
  87.8 4.8 %copy.37 = f32[4,5,2,16,256]{4,3,2,1,0:T(8,128)} copy(f32[4,5,2,16,256]{3,0,1,4,2:T(4,128)} %bitcast.28) | data formatting | bytes 1310720 | tf_op jit(solution)/shard_map/all_to_all | solution.py:180
  (20 shorter events, 0.3 us)
Async XLA Ops:
  0.0 14.0 %copy-start = (f32[4,5,32,256]{3,2,1,0:T(8,128)S(1)}, f32[4,5,32,256]{3,2,1,0:T(8,128)}, u32[]{:S(2)}) copy-start(f32[4,5,32,256]{3,2,1,0:T(8,128)} %param.4) | copy-start | bytes 1966084
  0.0 14.6 %copy-start.6 = (s32[4]{0:T(128)S(1)}, s32[4]{0:T(128)}, u32[]{:S(2)}) copy-start(s32[4]{0:T(128)} %param.6) | copy-start | bytes 52
  0.0 29.8 %collective-permute-start.1 = (f32[4,5,32,256]{3,2,1,0:T(8,128)}, f32[4,5,32,256]{3,2,1,0:T(8,128)S(1)}, u32[]{:S(2)}, u32[]{:S(2)}) collective-permute-start(f32[4,5,32,256]{3,2,1,0:T(8,128)} %param.4), channel_id=1, source_target_pairs={{2,0},{4,2},{6,4},{8,6},{10,8},{12,10},{14,12},{16,14},{18,16},{20... | collective-permute-start | bytes 1966088 | tf_op jit(solution)/shard_map/ppermute | solution.py:28
  1.4 28.5 %collective-permute-start = (f32[4,5,32,256]{3,2,1,0:T(8,128)}, f32[4,5,32,256]{3,2,1,0:T(8,128)S(1)}, u32[]{:S(2)}, u32[]{:S(2)}) collective-permute-start(f32[4,5,32,256]{3,2,1,0:T(8,128)} %param.4), channel_id=1, source_target_pairs={{0,2},{2,4},{4,6},{6,8},{8,10},{10,12},{12,14},{14,16},{16,18},{18... | collective-permute-start | bytes 1966088 | tf_op jit(solution)/shard_map/ppermute | solution.py:26
  5.7 13.4 %collective-permute-start.3 = (f32[4,5,32,4]{3,2,1,0:T(8,128)S(1)}, f32[4,5,32,4]{3,2,1,0:T(8,128)S(1)}, u32[]{:S(2)}, u32[]{:S(2)}) collective-permute-start(f32[4,5,32,4]{3,2,1,0:T(8,128)S(1)} %get-tuple-element.18), channel_id=1, source_target_pairs={{0,1},{1,0},{2,3},{3,2},{4,5},{5,4},{6,7},{7,6},{8,9},{9,8},{10,11... | collective-permute-start | bytes 30728 | tf_op jit(solution)/shard_map/ppermute | solution.py:26
  8.8 15.1 %collective-permute-start.4 = (f32[4,5,32,4]{3,2,1,0:T(8,128)S(1)}, f32[4,5,32,4]{3,2,1,0:T(8,128)}, u32[]{:S(2)}, u32[]{:S(2)}) collective-permute-start(f32[4,5,32,4]{3,2,1,0:T(8,128)S(1)} %get-tuple-element.19), channel_id=1, source_target_pairs={{1,0},{0,1},{3,2},{2,3},{5,4},{4,5},{7,6},{6,7},{9,8},{8,9},{11,10... | collective-permute-start | bytes 30728 | tf_op jit(solution)/shard_map/ppermute | solution.py:28
  10.4 15.2 %collective-permute-start.2 = (f32[4,5,4,256]{3,2,1,0:T(4,128)}, f32[4,5,4,256]{3,2,1,0:T(4,128)}, u32[]{:S(2)}, u32[]{:S(2)}) collective-permute-start(f32[4,5,4,256]{3,2,1,0:T(4,128)} %slice.194), channel_id=1, source_target_pairs={{0,1},{1,0},{2,3},{3,2},{4,5},{5,4},{6,7},{7,6},{8,9},{9,8},{10,11... | collective-permute-start | bytes 245768 | tf_op jit(solution)/shard_map/ppermute | solution.py:42
  25.3 1.9 %copy-start.1 = (f32[5]{0:T(128)S(1)}, f32[5]{0:T(128)}, u32[]{:S(2)}) copy-start(f32[5]{0:T(128)} %constant.88.clone) | copy-start | bytes 64
  29.0 0.7 copy-start.2
  32.3 5.2 %copy-start.3 = (s32[128]{0:T(128)S(1)}, s32[128]{0:T(128)}, u32[]{:S(2)}) copy-start(s32[128]{0:T(128)} %and_select_fusion) | copy-start | bytes 1540
  32.3 5.2 %copy-start.4 = (f32[128]{0:T(128)S(1)}, f32[128]{0:T(128)}, u32[]{:S(2)}) copy-start(f32[128]{0:T(128)} %compare_select_fusion.1) | copy-start | bytes 1540
  32.3 5.2 %copy-start.5 = (s32[16]{0:T(128)S(1)}, s32[16]{0:T(128)}, u32[]{:S(2)}) copy-start(s32[16]{0:T(128)} %dynamic-slice) | copy-start | bytes 196
  33.7 18.8 %all-to-all-start = ((f32[4,5,32,256]{3,1,0,2:T(8,128)}), f32[4,5,32,256]{3,1,0,2:T(8,128)S(1)}, u32[]{:S(2)}, u32[]{:S(2)}) async-start(f32[4,5,32,256]{3,1,0,2:T(8,128)} %copy.34), calls=%async_computation | async-start | bytes 2097152 | tf_op jit(solution)/shard_map/all_to_all | solution.py:166
  52.5 2.8 %copy-start.7 = (pred[4,16]{1,0:T(4,128)(4,1)S(1)}, pred[4,16]{1,0:T(4,128)(4,1)}, u32[]{:S(2)}) copy-start(pred[4,16]{1,0:T(4,128)(4,1)} %broadcast_compare_fusion) | copy-start | bytes 196
where the time goes:
time: 93.3 us; the launch traced here: 92.6 us
  local copies, waits for them, and re-layouts  33.1 us (35%)
  waiting for transfers between devices  19.9 us (21%)
  starting transfers between devices  13.3 us (14%)
  blocking collectives  12.1 us (13%)
  other arithmetic  10.5 us (11%)
  matrix products  3.43 us (4%)
    all_to_all x1, waiting for transfers between devices, per_device(): lax.all_to_all(section, 'az', split_axis=2, concat_axis=3, tiled=True)  15 us
    unnamed x21, local copies, waits for them, and re-layouts  12.5 us
    all_to_all x1, blocking collectives, per_device(): lax.all_to_all(chosen, 'az', split_axis=3, concat_axis=2, tiled=True)  12.1 us
    ppermute x2, starting transfers between devices, extended(): lax.ppermute(tail, axis, [(i, (i + 1) % count) for i in range(ends)])  6.14 us
    all_to_all x2, local copies, waits for them, and re-layouts, per_device(): lax.all_to_all(chosen, 'az', split_axis=3, concat_axis=2, tiled=True)  5.32 us
    ppermute x2, waiting for transfers between devices, extended(): lax.ppermute(head, axis, [((i + 1) % count, i) for i in range(ends)])  4.79 us
    all_to_all x1, starting transfers between devices, per_device(): lax.all_to_all(section, 'az', split_axis=2, concat_axis=3, tiled=True)  3.75 us
    select_n x1, local copies, waits for them, and re-layouts, per_device(): jnp.where(local_ids[None, None, :, None] < filtered_cycles[:, None, None,...  3.52 us
  transfers between devices with their start and end apart: 6, of which 3 were waited for; matrix products, arithmetic and copies ran while one was open for 16% of the time, Pallas kernels for 0%

commit v1 on v0

v1 whole, which is shorter than its diff:
```python
import functools
import math

import jax
import jax.numpy as jnp
import numpy as np
from jax import lax
from jax.experimental import pallas as pl
from jax.experimental.pallas import tpu as pltpu
from jax.sharding import PartitionSpec as P

MODE_MOST = 64
STENCIL = (0.8, -0.2, 4.0 / 105.0, -1.0 / 280.0)
REACH = len(STENCIL)
GAS_FACTOR = 0.4
TIME_STEP = 0.1
COMPONENTS = 5
TILE = 8
LANES = 128
CHUNKS = ((0, 2), (2, 1), (3, 1))

VMEM = pl.BlockSpec(memory_space=pltpu.VMEM)
SMEM = pl.BlockSpec(memory_space=pltpu.SMEM)
ANY = pl.BlockSpec(memory_space=pl.ANY)
PARAMS = dict(vmem_limit_bytes=8 << 20)


def primitives(s):
    inverse = 1.0 / s[0]
    a, b, c = s[1] * inverse, s[2] * inverse, s[3] * inverse
    p = GAS_FACTOR * (s[4] - 0.5 * (s[1] * a + s[2] * b + s[3] * c))
    return a, b, c, p


def flux(s, vel, p, along):
    out = [s[along]] + [s[i] * vel for i in (1, 2, 3)] + [vel * (s[4] + p)]
    out[along] = out[along] + p
    return out


def axial_flux(s):
    inverse = 1.0 / s[0]
    a = s[1] * inverse
    p = GAS_FACTOR * (s[4] - 0.5 * ((s[1] * s[1] + s[2] * s[2] + s[3] * s[3]) * inverse))
    return flux(s, a, p, 1)


def halo_terms(x_ref, stores, base, step, forward, rows):
    scale = jnp.where(forward, -TIME_STEP, TIME_STEP)
    for r in range(0, rows, TILE):
        near = []
        for h in range(REACH):
            at = base + step * h
            near.append(axial_flux([x_ref[at, c, r : r + TILE, :] for c in range(COMPONENTS)]))
        for i in range(REACH):
            for c in range(COMPONENTS):
                total = None
                for h in range(i + 1):
                    part = STENCIL[REACH + h - i - 1] * near[h][c]
                    total = part if total is None else total + part
                stores(i, c, r, scale * total)


def outer_kernel(last, x_ref, t_ref):
    me = lax.axis_index("ax")
    even = lax.rem(me, 2) == 0
    end = (me == 0) | (me == last)
    base = jnp.where(even, 0, REACH - 1)
    step = jnp.where(end, 0, jnp.where(even, 1, -1))
    forward = even != end

    def store(i, c, r, value):
        t_ref[jnp.where(forward, i, REACH - 1 - i), c, r : r + TILE, :] = value

    halo_terms(x_ref, store, base, step, forward, x_ref.shape[2])


def inner_kernel(x_ref, t_ref, pack_ref):
    me = lax.axis_index("ax")
    forward = lax.rem(me, 2) == 1
    base = jnp.where(forward, 0, REACH - 1)
    step = jnp.where(forward, 1, -1)
    stations, _, rows, width = x_ref.shape

    def store(i, c, r, value):
        t_ref[jnp.where(forward, i, REACH - 1 - i), c, r : r + TILE, :] = value

    halo_terms(x_ref, store, base, step, forward, rows)
    groups = rows // TILE
    lane = lax.broadcasted_iota(jnp.int32, (TILE, LANES), 1)
    for c in range(COMPONENTS):
        edge = jnp.zeros((TILE, LANES), jnp.float32)
        for s in range(stations):
            pack_ref[c, s * REACH : (s + 1) * REACH, :] = x_ref[s, c, 0:REACH, :]
            for g in range(groups):
                place = (s * groups + g) * 2 * REACH
                first = x_ref[s, c, g * TILE : (g + 1) * TILE, 0:LANES]
                final = x_ref[s, c, g * TILE : (g + 1) * TILE, width - LANES : width]
                both = pltpu.roll(jnp.where(lane < REACH, first, final), (place + REACH) % LANES, 1)
                edge = jnp.where((lane >= place) & (lane < place + 2 * REACH), both, edge)
        pack_ref[c, stations * REACH : stations * REACH + TILE, 0:LANES] = edge
        if width > LANES:
            pack_ref[c, stations * REACH : stations * REACH + TILE, LANES:width] = jnp.zeros(
                (TILE, width - LANES), jnp.float32
            )


def base_kernel(
    turn, x_ref, inner_ref, own_ref, left_ref, right_ref, across_ref, modes_ref,
    base_ref, weight_ref, scratch,
):
    stations, _, rows, width = x_ref.shape
    points = int(round(turn))
    groups = rows // TILE
    lane = lax.broadcasted_iota(jnp.int32, (TILE, LANES), 1)
    edge_rows = pl.ds(stations * REACH, TILE)
    per_angle = turn / (2.0 * math.pi)

    slot = lane % (2 * REACH)
    from_left = slot < REACH

    def edge_flux(s):
        _, _, vel, p = primitives(s)
        return flux(s, vel, p, 3)

    own = edge_flux([own_ref[c, edge_rows, 0:LANES] for c in range(COMPONENTS)])
    other = edge_flux(
        [
            jnp.where(from_left, left_ref[c, edge_rows, 0:LANES], right_ref[c, edge_rows, 0:LANES])
            for c in range(COMPONENTS)
        ]
    )
    fixes = []
    for c in range(COMPONENTS):
        change = other[c] - own[c]
        fix = jnp.zeros((TILE, LANES), jnp.float32)
        for k in range(1, REACH + 1):
            ahead = pltpu.roll(change, LANES - k, 1)
            behind = pltpu.roll(change, k, 1)
            fix = fix + STENCIL[k - 1] * jnp.where(
                from_left,
                jnp.where(slot + k >= REACH, ahead, 0.0),
                jnp.where(slot - k < REACH, -behind, 0.0),
            )
        fixes.append(fix)

    for s in range(stations):
        cross = [across_ref[c, s * REACH : (s + 1) * REACH, :] for c in range(COMPONENTS)]
        _, vel, _, p = primitives(cross)
        far = flux(cross, vel, p, 2)
        for c in range(COMPONENTS):
            sign = -1.0 if c in (2, 3) else 1.0
            for i in range(REACH):
                scratch[c, TILE - 1 - i : TILE - i, :] = (sign * (i + 0.5)) * far[c][i : i + 1, :]
        for g in range(groups):
            at = slice(g * TILE, (g + 1) * TILE)
            state = [x_ref[s, c, at, :] for c in range(COMPONENTS)]
            _, vel, _, p = primitives(state)
            out = flux(state, vel, p, 2)
            radius = (
                lax.broadcasted_iota(jnp.int32, (TILE, width), 0).astype(jnp.float32) + (g * TILE + 0.5)
            )
            for c in range(COMPONENTS):
                scratch[c, TILE + g * TILE : TILE + (g + 1) * TILE, :] = radius * out[c]
                if g == groups - 1:
                    edge = out[c][TILE - 1 : TILE, :]
                    for m in range(1, REACH + 1):
                        scratch[c, TILE + rows + m - 1 : TILE + rows + m, :] = (rows - 0.5 + m) * edge
        for g in range(groups):
            at = slice(g * TILE, (g + 1) * TILE)
            state = [x_ref[s, c, at, :] for c in range(COMPONENTS)]
            _, _, vel, p = primitives(state)
            swirl = flux(state, vel, p, 3)
            radius = (
                lax.broadcasted_iota(jnp.int32, (TILE, width), 0).astype(jnp.float32) + (g * TILE + 0.5)
            )
            scale = TIME_STEP / radius
            place = (s * groups + g) * 2 * REACH
            source = {2: state[3] * vel + p, 3: -(state[2] * vel)}
            for c in range(COMPONENTS):
                turned = None
                radial = None
                for k in range(1, REACH + 1):
                    part = STENCIL[k - 1] * (
                        pltpu.roll(swirl[c], width - k, 1) - pltpu.roll(swirl[c], k, 1)
                    )
                    turned = part if turned is None else turned + part
                    start = TILE + g * TILE
                    part = STENCIL[k - 1] * (
                        scratch[c, start + k : start + k + TILE, :]
                        - scratch[c, start - k : start - k + TILE, :]
                    )
                    radial = part if radial is None else radial + part
                fix = pltpu.roll(fixes[c], (LANES - REACH - place) % LANES, 1)
                head = jnp.where(lane < REACH, fix, 0.0)
                tail = jnp.where(lane >= LANES - REACH, fix, 0.0)
                if width == LANES:
                    turned = turned + (head + tail)
                else:
                    middle = [jnp.zeros((TILE, width - 2 * LANES), jnp.float32)] if width > 2 * LANES else []
                    turned = turned + jnp.concatenate([head] + middle + [tail], axis=1)
                total = radial + per_angle * turned
                if c in source:
                    total = total - source[c]
                base_ref[s, c, at, :] = state[c] + inner_ref[s, c, at, :] - scale * total

    for r in range(0, rows, TILE):
        near = [
            axial_flux([x_ref[h, c, r : r + TILE, :] for c in range(COMPONENTS)]) for h in range(stations)
        ]
        for s in range(stations):
            for c in range(COMPONENTS):
                total = None
                for h in range(stations):
                    if h == s:
                        continue
                    weight = STENCIL[abs(h - s) - 1] * (-TIME_STEP if h > s else TIME_STEP)
                    part = weight * near[h][c]
                    total = part if total is None else total + part
                base_ref[s, c, r : r + TILE, :] += total

    columns = 2 * MODE_MOST
    harmonic = lax.broadcasted_iota(jnp.int32, (rows, columns), 1) % MODE_MOST
    row = lax.broadcasted_iota(jnp.int32, (rows, columns), 0)
    kept = jnp.zeros((rows, columns), jnp.int32)
    for j in range(rows):
        kept = jnp.where(row == j, modes_ref[j], kept)
    weight = jnp.where(harmonic == 0, 1.0 / points, 2.0 / points).astype(jnp.float32)
    weight_ref[...] = jnp.where(harmonic < kept, weight, 0.0)


def forward_kernel(first, count, base_ref, t_ref, basis_ref, section_ref, coeff_ref):
    section = base_ref[first : first + count] + t_ref[...]
    section_ref[...] = section
    lines = section.reshape(-1, section.shape[-1])
    basis = basis_ref[lax.axis_index("az")]
    coeff_ref[...] = lax.dot_general(
        lines, basis, (((1,), (0,)), ((), ())),
        precision=lax.Precision.HIGHEST, preferred_element_type=jnp.float32,
    )


def inverse_kernel(first, count, section_ref, mine_ref, other_ref, weight_ref, basis_ref, limit_ref, *rest):
    out_ref, buffer, sem = rest[-3:]
    _, _, rows, width = section_ref.shape
    basis = basis_ref[lax.axis_index("az")]
    lines = COMPONENTS * rows
    weight = weight_ref[...]
    row = lax.broadcasted_iota(jnp.int32, (rows, width), 0)
    copies = []
    for s in range(count):
        part = pl.ds(s * lines, lines)
        total = mine_ref[part, :] + other_ref[part, :]
        total = (total.reshape(COMPONENTS, rows, -1) * weight[None]).reshape(lines, -1)
        smooth = lax.dot_general(
            total, basis, (((1,), (1,)), ((), ())),
            precision=lax.Precision.HIGHEST, preferred_element_type=jnp.float32,
        ).reshape(COMPONENTS, rows, width)
        inside = (row < limit_ref[first + s])[None]
        buffer[s] = jnp.where(inside, smooth, section_ref[s])
        copy = pltpu.make_async_copy(buffer.at[s], out_ref.at[first + s], sem.at[s])
        copy.start()
        copies.append(copy)
    for copy in copies:
        copy.wait()


def fourier_tables(sectors, width):
    points = sectors * width
    harmonic = np.arange(2 * MODE_MOST) % MODE_MOST
    angle = (np.arange(points)[:, None] * harmonic[None, :] % points) * (2.0 * np.pi / points)
    table = np.where(np.arange(2 * MODE_MOST)[None, :] < MODE_MOST, np.cos(angle), np.sin(angle))
    return table.astype(np.float32).reshape(sectors, width, 2 * MODE_MOST)


def per_device(conserved, cycle_modes, filtered_cycles):
    line = lax.axis_size("ax")
    sectors = lax.axis_size("az")
    stations, components, rows, width = conserved.shape
    if stations != REACH or components != COMPONENTS or line % 2 or sectors % 2:
        raise ValueError("unsupported shape")
    if (stations * rows // TILE) * 2 * REACH > LANES or width % LANES or rows % TILE:
        raise ValueError("unsupported shape")
    block = jax.ShapeDtypeStruct(conserved.shape, jnp.float32)
    params = pltpu.CompilerParams(**PARAMS)

    terms = pl.pallas_call(
        functools.partial(outer_kernel, line - 1),
        out_shape=block, in_specs=[VMEM], out_specs=VMEM, compiler_params=params, name="outer",
    )(conserved)
    ends = [(0, 0), (line - 1, line - 1)]
    pairs = [(i, i + 1) for i in range(1, line - 1, 2)]
    outer_route = ends + pairs + [(j, i) for i, j in pairs]
    outer = [
        lax.ppermute(lax.slice_in_dim(terms, a, a + n, axis=0), "ax", outer_route) for a, n in CHUNKS
    ]
    inner, pack = pl.pallas_call(
        inner_kernel,
        out_shape=(block, jax.ShapeDtypeStruct((COMPONENTS, stations * REACH + TILE, width), jnp.float32)),
        in_specs=[VMEM], out_specs=(VMEM, VMEM), compiler_params=params, name="inner",
    )(conserved)
    inner = lax.ppermute(inner, "ax", [(i, i ^ 1) for i in range(line)])

    def turned(value, by):
        return lax.ppermute(value, "az", [(i, (i + by) % sectors) for i in range(sectors)])

    across = turned(pack, sectors // 2)
    left, right = (across, across) if sectors == 2 else (turned(pack, 1), turned(pack, -1))
    base, weight = pl.pallas_call(
        functools.partial(base_kernel, float(width * sectors)),
        out_shape=(block, jax.ShapeDtypeStruct((rows, 2 * MODE_MOST), jnp.float32)),
        in_specs=[VMEM] * 6 + [SMEM], out_specs=(VMEM, VMEM),
        scratch_shapes=[pltpu.VMEM((COMPONENTS, rows + 2 * TILE, width), jnp.float32)],
        compiler_params=params, name="base",
    )(conserved, inner, pack, left, right, across, cycle_modes)
    basis = jnp.asarray(fourier_tables(sectors, width))
    out = None
    for (first, count), arrived in zip(CHUNKS, outer):
        section, mine = pl.pallas_call(
            functools.partial(forward_kernel, first, count),
            out_shape=(
                jax.ShapeDtypeStruct((count,) + conserved.shape[1:], jnp.float32),
                jax.ShapeDtypeStruct((count * components * rows, 2 * MODE_MOST), jnp.float32),
            ),
            in_specs=[VMEM] * 3, out_specs=(VMEM, VMEM), compiler_params=params, name="forward%d" % first,
        )(base, arrived, basis)
        other = turned(mine, 1) if sectors == 2 else lax.psum(mine, "az") - mine
        more = () if out is None else (out,)
        out = pl.pallas_call(
            functools.partial(inverse_kernel, first, count),
            out_shape=block,
            in_specs=[VMEM] * 5 + [SMEM] + [ANY] * len(more), out_specs=ANY,
            scratch_shapes=[
                pltpu.VMEM((count,) + conserved.shape[1:], jnp.float32),
                pltpu.SemaphoreType.DMA((count,)),
            ],
            input_output_aliases={6: 0} if more else {},
            compiler_params=params, name="inverse%d" % first,
        )(section, mine, other, weight, basis, filtered_cycles, *more)
    return out


def solution(mesh):
    placed = (P("ax", None, None, "az"), P(), P("ax"))
    return jax.shard_map(
        per_device, mesh=mesh, in_specs=placed, out_specs=P("ax", None, None, "az"), check_vma=False
    )
```

time: 93.3 us -> 30.3 us (0.32)
  the two profiles are of different devices: /device:TPU:0 before, /device:TPU:9 now
where the time goes in v1:
time: 30.3 us; the launch traced here: 30.1 us
  starting transfers between devices  15.1 us (50%)
  Pallas kernels  9.25 us (31%)
  waiting for transfers between devices  3.73 us (12%)
  local copies, waits for them, and re-layouts  1.81 us (6%)
    ppermute x3, starting transfers between devices, per_device(): lax.ppermute(lax.slice_in_dim(terms, a, a + n, axis=0), 'ax', outer_route)  8.86 us
    ppermute x4, starting transfers between devices, turned(): lax.ppermute(value, 'az', [(i, (i + by) % sectors) for i in range(sectors)])  5.51 us
    pallas_call x3, Pallas kernels, per_device(): pl.pallas_call(functools.partial(inverse_kernel, first, count), out_shape...  4.77 us
    pallas_call x1, Pallas kernels, per_device(): pl.pallas_call(functools.partial(base_kernel, float(width * sectors)), ou...  2.99 us
    ppermute x3, waiting for transfers between devices, per_device(): lax.ppermute(lax.slice_in_dim(terms, a, a + n, axis=0), 'ax', outer_route)  2.41 us
    unnamed x10, local copies, waits for them, and re-layouts  1.76 us
    ppermute x4, waiting for transfers between devices, turned(): lax.ppermute(value, 'az', [(i, (i + by) % sectors) for i in range(sectors)])  1.32 us
    pallas_call x3, Pallas kernels, per_device(): pl.pallas_call(functools.partial(forward_kernel, first, count), out_shape...  1.04 us
  transfers between devices with their start and end apart: 8, of which 3 were waited for; matrix products, arithmetic and copies ran while one was open for 0% of the time, Pallas kernels for 25%

profile of v1, /device:TPU:9, one launch (start us, length us, event | category | flops | bytes accessed | tf_op | source)
XLA Modules:
  0.0 30.1 jit_solution(13832662988668725187)
XLA Ops:
  0.0 0.0 copy-start.1
  0.0 1.1 %copy-done.1 = f32[4,5,32,256]{3,2,1,0:T(8,128)S(1)} copy-done((f32[4,5,32,256]{3,2,1,0:T(8,128)S(1)}, f32[4,5,32,256]{3,2,1,0:T(8,128)}, u32[]{:S(2)}) %copy-start.1) | copy-done | bytes 655384
  1.1 0.3 inner.1
  1.4 0.7 %collective-permute-start = (f32[4,5,32,256]{3,2,1,0:T(8,128)S(1)}, f32[4,5,32,256]{3,2,1,0:T(8,128)S(1)}, u32[]{:S(2)}, u32[]{:S(2)}) collective-permute-start(f32[4,5,32,256]{3,2,1,0:T(8,128)S(1)} %get-tuple-element.15), channel_id=1, source_target_pairs={{0,2},{2,0},{4,6},{6,4},{8,10},{10,8},{12,14},{14,12},{16,18},{18,... | collective-permute-start | bytes 1966088 | tf_op jit(solution)/shard_map/ppermute | solution.py:302
  2.1 0.2 outer.1
  2.3 0.0 copy-start.2
  2.3 3.2 %collective-permute-start.6 = (f32[2,5,32,256]{3,2,1,0:T(8,128)S(1)}, f32[2,5,32,256]{3,2,1,0:T(8,128)S(1)}, u32[]{:S(2)}, u32[]{:S(2)}) collective-permute-start(f32[2,5,32,256]{3,2,1,0:T(8,128)S(1)} %slice.14), channel_id=1, source_target_pairs={{0,0},{30,30},{2,4},{6,8},{10,12},{14,16},{18,20},{22,24},{26,28},... | collective-permute-start | bytes 983048 | tf_op jit(solution)/shard_map/ppermute | solution.py:295
  5.5 1.3 %collective-permute-start.1 = (f32[5,24,256]{2,1,0:T(8,128)S(1)}, f32[5,24,256]{2,1,0:T(8,128)S(1)}, u32[]{:S(2)}, u32[]{:S(2)}) collective-permute-start(f32[5,24,256]{2,1,0:T(8,128)S(1)} %get-tuple-element.16.own_ref), channel_id=1, source_target_pairs={{0,1},{1,0},{2,3},{3,2},{4,5},{5,4},{6,7},{7,6},{8,9},{9,8},{10,11... | collective-permute-start | bytes 368648 | tf_op jit(solution)/shard_map/ppermute | solution.py:305
  6.8 0.0 copy-start.4
  6.9 2.8 %collective-permute-start.4 = (f32[1,5,32,256]{3,2,1,0:T(8,128)S(1)}, f32[1,5,32,256]{3,2,1,0:T(8,128)S(1)}, u32[]{:S(2)}, u32[]{:S(2)}) collective-permute-start(f32[1,5,32,256]{3,2,1,0:T(8,128)S(1)} %get-tuple-element.25), channel_id=1, source_target_pairs={{0,0},{30,30},{2,4},{6,8},{10,12},{14,16},{18,20},{22,24},{26,28},... | collective-permute-start | bytes 491528 | tf_op jit(solution)/shard_map/ppermute | solution.py:295
  9.7 0.0 copy-start
  9.7 2.9 %collective-permute-start.2 = (f32[1,5,32,256]{3,2,1,0:T(8,128)S(1)}, f32[1,5,32,256]{3,2,1,0:T(8,128)S(1)}, u32[]{:S(2)}, u32[]{:S(2)}) collective-permute-start(f32[1,5,32,256]{3,2,1,0:T(8,128)S(1)} %get-tuple-element.26), channel_id=1, source_target_pairs={{0,0},{30,30},{2,4},{6,8},{10,12},{14,16},{18,20},{22,24},{26,28},... | collective-permute-start | bytes 491528 | tf_op jit(solution)/shard_map/ppermute | solution.py:295
  12.6 0.0 collective-permute-done.1.left_ref.right_ref.across_ref
  12.6 0.0 collective-permute-done.inner_ref
  12.6 0.0 copy-done.2
  12.6 0.0 copy-done.4
  12.6 3.0 %base.1 = (f32[4,5,32,256]{3,2,1,0:T(8,128)S(1)}, f32[32,128]{1,0:T(8,128)S(1)}) custom-call(f32[4,5,32,256]{3,2,1,0:T(8,128)S(1)} %copy-done.2, f32[4,5,32,256]{3,2,1,0:T(8,128)S(1)} %collective-permute-done.inner_ref, f32[5,24,256]{2,1,0:T(8,128)S(1)} %get-tuple-element.16.own_ref, f32[5,24,256]{2,1,0:T(8,128)S(1)} %collective-permute-done.1.left_ref.right_ref.across_ref, ...), custom_call_target="tpu_custom_call" | custom-call | tf_op jit(solution)/shard_map/base/pallas_call | solution.py:309
  15.6 2.3 %collective-permute-done.6.t_ref = f32[2,5,32,256]{3,2,1,0:T(8,128)S(1)} collective-permute-done((f32[2,5,32,256]{3,2,1,0:T(8,128)S(1)}, f32[2,5,32,256]{3,2,1,0:T(8,128)S(1)}, u32[]{:S(2)}, u32[]{:S(2)}) %collective-permute-start.6) | collective-permute-done | bytes 327712 | tf_op jit(solution)/shard_map/ppermute | solution.py:295
  17.9 0.0 copy-done
  17.9 0.4 %forward0.1 = (f32[2,5,32,256]{3,2,1,0:T(8,128)S(1)}, f32[320,128]{1,0:T(8,128)S(1)}) custom-call(f32[4,5,32,256]{3,2,1,0:T(8,128)S(1)} %get-tuple-element.17.base_ref, f32[2,5,32,256]{3,2,1,0:T(8,128)S(1)} %collective-permute-done.6.t_ref, f32[2,256,128]{2,1,0:T(8,128)S(1)} %copy-done), custom_call_target="tpu_custom_call" | custom-call | tf_op jit(solution)/shard_map/forward0/pallas_call | solution.py:319
  18.3 1.3 %collective-permute-start.7 = (f32[320,128]{1,0:T(8,128)S(1)}, f32[320,128]{1,0:T(8,128)S(1)}, u32[]{:S(2)}, u32[]{:S(2)}) collective-permute-start(f32[320,128]{1,0:T(8,128)S(1)} %get-tuple-element.24.mine_ref), channel_id=1, source_target_pairs={{0,1},{1,0},{2,3},{3,2},{4,5},{5,4},{6,7},{7,6},{8,9},{9,8},{10,11... | collective-permute-start | bytes 491528 | tf_op jit(solution)/shard_map/ppermute | solution.py:305
  19.6 0.0 collective-permute-done.4.t_ref
  19.6 0.3 %forward2.1 = (f32[1,5,32,256]{3,2,1,0:T(8,128)S(1)}, f32[160,128]{1,0:T(8,128)S(1)}) custom-call(f32[4,5,32,256]{3,2,1,0:T(8,128)S(1)} %get-tuple-element.17.base_ref, f32[1,5,32,256]{3,2,1,0:T(8,128)S(1)} %collective-permute-done.4.t_ref, f32[2,256,128]{2,1,0:T(8,128)S(1)} %copy-done), custom_call_target="tpu_custom_call" | custom-call | tf_op jit(solution)/shard_map/forward2/pallas_call | solution.py:319
  19.9 1.6 %collective-permute-start.5 = (f32[160,128]{1,0:T(8,128)S(1)}, f32[160,128]{1,0:T(8,128)S(1)}, u32[]{:S(2)}, u32[]{:S(2)}) collective-permute-start(f32[160,128]{1,0:T(8,128)S(1)} %get-tuple-element.22.mine_ref), channel_id=1, source_target_pairs={{0,1},{1,0},{2,3},{3,2},{4,5},{5,4},{6,7},{7,6},{8,9},{9,8},{10,11... | collective-permute-start | bytes 245768 | tf_op jit(solution)/shard_map/ppermute | solution.py:305
  21.5 0.1 collective-permute-done.2.t_ref
  21.7 0.3 %forward3.1 = (f32[1,5,32,256]{3,2,1,0:T(8,128)S(1)}, f32[160,128]{1,0:T(8,128)S(1)}) custom-call(f32[4,5,32,256]{3,2,1,0:T(8,128)S(1)} %get-tuple-element.17.base_ref, f32[1,5,32,256]{3,2,1,0:T(8,128)S(1)} %collective-permute-done.2.t_ref, f32[2,256,128]{2,1,0:T(8,128)S(1)} %copy-done), custom_call_target="tpu_custom_call" | custom-call | tf_op jit(solution)/shard_map/forward3/pallas_call | solution.py:319
  22.0 1.3 %collective-permute-start.3 = (f32[160,128]{1,0:T(8,128)S(1)}, f32[160,128]{1,0:T(8,128)S(1)}, u32[]{:S(2)}, u32[]{:S(2)}) collective-permute-start(f32[160,128]{1,0:T(8,128)S(1)} %get-tuple-element.19.mine_ref), channel_id=1, source_target_pairs={{0,1},{1,0},{2,3},{3,2},{4,5},{5,4},{6,7},{7,6},{8,9},{9,8},{10,11... | collective-permute-start | bytes 245768 | tf_op jit(solution)/shard_map/ppermute | solution.py:305
  23.3 1.3 %collective-permute-done.7.other_ref = f32[320,128]{1,0:T(8,128)S(1)} collective-permute-done((f32[320,128]{1,0:T(8,128)S(1)}, f32[320,128]{1,0:T(8,128)S(1)}, u32[]{:S(2)}, u32[]{:S(2)}) %collective-permute-start.7) | collective-permute-done | bytes 163872 | tf_op jit(solution)/shard_map/ppermute | solution.py:305
  24.6 0.0 copy-start.3
  24.6 0.7 %copy-done.3 = s32[4]{0:T(128)S(1)} copy-done((s32[4]{0:T(128)S(1)}, s32[4]{0:T(128)}, u32[]{:S(2)}) %copy-start.3) | copy-done | bytes 40
  25.3 1.7 %inverse0.1.rest_0_ = f32[4,5,32,256]{3,2,1,0:T(8,128)} custom-call(f32[2,5,32,256]{3,2,1,0:T(8,128)S(1)} %get-tuple-element.23.section_ref, f32[320,128]{1,0:T(8,128)S(1)} %get-tuple-element.24.mine_ref, f32[320,128]{1,0:T(8,128)S(1)} %collective-permute-done.7.other_ref, f32[32,128]{1,0:T(8,128)S(1)} %get-tuple-element.20.weight_ref, ...), custom_call_target="tpu_custom_call" | custom-call | tf_op jit(solution)/shard_map/inverse0/pallas_call | solution.py:329
  27.0 0.0 collective-permute-done.5.other_ref
  27.0 1.5 %inverse2.1.rest_0_ = f32[4,5,32,256]{3,2,1,0:T(8,128)} custom-call(f32[1,5,32,256]{3,2,1,0:T(8,128)S(1)} %get-tuple-element.21.section_ref, f32[160,128]{1,0:T(8,128)S(1)} %get-tuple-element.22.mine_ref, f32[160,128]{1,0:T(8,128)S(1)} %collective-permute-done.5.other_ref, ...), custom_call_target="tpu_custom_call", output_to_operand_aliasing={{}: (6, {})} | custom-call | tf_op jit(solution)/shard_map/inverse2/pallas_call | solution.py:329
  28.5 0.0 collective-permute-done.3.other_ref
  28.5 1.5 %inverse3.1 = f32[4,5,32,256]{3,2,1,0:T(8,128)} custom-call(f32[1,5,32,256]{3,2,1,0:T(8,128)S(1)} %get-tuple-element.18.section_ref, f32[160,128]{1,0:T(8,128)S(1)} %get-tuple-element.19.mine_ref, f32[160,128]{1,0:T(8,128)S(1)} %collective-permute-done.3.other_ref, f32[32,128]{1,0:T(8,128)S(1)} %get-tuple-element.20.weight_ref, ...), custom_call_target="tpu_custom_call", output_to_operand_aliasing={{}: (6, {})} | custom-call | tf_op jit(solution)/shard_map/inverse3/pallas_call | solution.py:329
  (2 shorter events, 0.0 us)
Async XLA Ops:
  0.0 1.1 %copy-start.1 = (f32[4,5,32,256]{3,2,1,0:T(8,128)S(1)}, f32[4,5,32,256]{3,2,1,0:T(8,128)}, u32[]{:S(2)}) copy-start(f32[4,5,32,256]{3,2,1,0:T(8,128)} %x_ref.5) | copy-start | bytes 1966084
  1.4 11.2 %collective-permute-start = (f32[4,5,32,256]{3,2,1,0:T(8,128)S(1)}, f32[4,5,32,256]{3,2,1,0:T(8,128)S(1)}, u32[]{:S(2)}, u32[]{:S(2)}) collective-permute-start(f32[4,5,32,256]{3,2,1,0:T(8,128)S(1)} %get-tuple-element.15), channel_id=1, source_target_pairs={{0,2},{2,0},{4,6},{6,4},{8,10},{10,8},{12,14},{14,12},{16,18},{18,... | collective-permute-start | bytes 1966088 | tf_op jit(solution)/shard_map/ppermute | solution.py:302
  2.3 10.3 %copy-start.2 = (f32[4,5,32,256]{3,2,1,0:T(8,128)S(1)}, f32[4,5,32,256]{3,2,1,0:T(8,128)}, u32[]{:S(2)}) copy-start(f32[4,5,32,256]{3,2,1,0:T(8,128)} %x_ref.5) | copy-start | bytes 1966084
  2.3 15.5 %collective-permute-start.6 = (f32[2,5,32,256]{3,2,1,0:T(8,128)S(1)}, f32[2,5,32,256]{3,2,1,0:T(8,128)S(1)}, u32[]{:S(2)}, u32[]{:S(2)}) collective-permute-start(f32[2,5,32,256]{3,2,1,0:T(8,128)S(1)} %slice.14), channel_id=1, source_target_pairs={{0,0},{30,30},{2,4},{6,8},{10,12},{14,16},{18,20},{22,24},{26,28},... | collective-permute-start | bytes 983048 | tf_op jit(solution)/shard_map/ppermute | solution.py:295
  5.5 7.1 %collective-permute-start.1 = (f32[5,24,256]{2,1,0:T(8,128)S(1)}, f32[5,24,256]{2,1,0:T(8,128)S(1)}, u32[]{:S(2)}, u32[]{:S(2)}) collective-permute-start(f32[5,24,256]{2,1,0:T(8,128)S(1)} %get-tuple-element.16.own_ref), channel_id=1, source_target_pairs={{0,1},{1,0},{2,3},{3,2},{4,5},{5,4},{6,7},{7,6},{8,9},{9,8},{10,11... | collective-permute-start | bytes 368648 | tf_op jit(solution)/shard_map/ppermute | solution.py:305
  6.8 5.8 %copy-start.4 = (s32[32]{0:T(128)S(1)}, s32[32]{0:T(128)}, u32[]{:S(2)}) copy-start(s32[32]{0:T(128)} %modes_ref.1) | copy-start | bytes 388
  6.9 12.8 %collective-permute-start.4 = (f32[1,5,32,256]{3,2,1,0:T(8,128)S(1)}, f32[1,5,32,256]{3,2,1,0:T(8,128)S(1)}, u32[]{:S(2)}, u32[]{:S(2)}) collective-permute-start(f32[1,5,32,256]{3,2,1,0:T(8,128)S(1)} %get-tuple-element.25), channel_id=1, source_target_pairs={{0,0},{30,30},{2,4},{6,8},{10,12},{14,16},{18,20},{22,24},{26,28},... | collective-permute-start | bytes 491528 | tf_op jit(solution)/shard_map/ppermute | solution.py:295
  9.7 8.2 %copy-start = (f32[2,256,128]{2,1,0:T(8,128)S(1)}, f32[2,256,128]{2,1,0:T(8,128)}, u32[]{:S(2)}) copy-start(f32[2,256,128]{2,1,0:T(8,128)} %constant.2.clone.basis_ref) | copy-start | bytes 786436
  9.7 12.0 %collective-permute-start.2 = (f32[1,5,32,256]{3,2,1,0:T(8,128)S(1)}, f32[1,5,32,256]{3,2,1,0:T(8,128)S(1)}, u32[]{:S(2)}, u32[]{:S(2)}) collective-permute-start(f32[1,5,32,256]{3,2,1,0:T(8,128)S(1)} %get-tuple-element.26), channel_id=1, source_target_pairs={{0,0},{30,30},{2,4},{6,8},{10,12},{14,16},{18,20},{22,24},{26,28},... | collective-permute-start | bytes 491528 | tf_op jit(solution)/shard_map/ppermute | solution.py:295
  18.3 6.3 %collective-permute-start.7 = (f32[320,128]{1,0:T(8,128)S(1)}, f32[320,128]{1,0:T(8,128)S(1)}, u32[]{:S(2)}, u32[]{:S(2)}) collective-permute-start(f32[320,128]{1,0:T(8,128)S(1)} %get-tuple-element.24.mine_ref), channel_id=1, source_target_pairs={{0,1},{1,0},{2,3},{3,2},{4,5},{5,4},{6,7},{7,6},{8,9},{9,8},{10,11... | collective-permute-start | bytes 491528 | tf_op jit(solution)/shard_map/ppermute | solution.py:305
  19.9 7.0 %collective-permute-start.5 = (f32[160,128]{1,0:T(8,128)S(1)}, f32[160,128]{1,0:T(8,128)S(1)}, u32[]{:S(2)}, u32[]{:S(2)}) collective-permute-start(f32[160,128]{1,0:T(8,128)S(1)} %get-tuple-element.22.mine_ref), channel_id=1, source_target_pairs={{0,1},{1,0},{2,3},{3,2},{4,5},{5,4},{6,7},{7,6},{8,9},{9,8},{10,11... | collective-permute-start | bytes 245768 | tf_op jit(solution)/shard_map/ppermute | solution.py:305
  22.0 6.5 %collective-permute-start.3 = (f32[160,128]{1,0:T(8,128)S(1)}, f32[160,128]{1,0:T(8,128)S(1)}, u32[]{:S(2)}, u32[]{:S(2)}) collective-permute-start(f32[160,128]{1,0:T(8,128)S(1)} %get-tuple-element.19.mine_ref), channel_id=1, source_target_pairs={{0,1},{1,0},{2,3},{3,2},{4,5},{5,4},{6,7},{7,6},{8,9},{9,8},{10,11... | collective-permute-start | bytes 245768 | tf_op jit(solution)/shard_map/ppermute | solution.py:305
  24.6 0.7 %copy-start.3 = (s32[4]{0:T(128)S(1)}, s32[4]{0:T(128)}, u32[]{:S(2)}) copy-start(s32[4]{0:T(128)} %limit_ref.5) | copy-start | bytes 52

commit v2 on v1

v2 whole, which is shorter than its diff:
```python
import functools
import math

import jax
import jax.numpy as jnp
import numpy as np
from jax import lax
from jax.experimental import pallas as pl
from jax.experimental.pallas import tpu as pltpu
from jax.sharding import PartitionSpec as P


MODE_MOST = 64
STENCIL = (0.8, -0.2, 4.0 / 105.0, -1.0 / 280.0)
REACH = len(STENCIL)
GAS_FACTOR = 0.4
TIME_STEP = 0.1
COMPONENTS = 5
TILE = 8
LANES = 128
SENDS = ((0, 1), (1, 1), (2, 1), (3, 1))
GROUPS = ((0, 2), (2, 1), (3, 1))
LAST = len(GROUPS) - 1

VMEM = pl.BlockSpec(memory_space=pltpu.VMEM)
SMEM = pl.BlockSpec(memory_space=pltpu.SMEM)
ANY = pl.BlockSpec(memory_space=pl.ANY)
PARAMS = dict(vmem_limit_bytes=8 << 20)


def exact_dot(a, b):
    return lax.dot_general(
        a, b, (((1,), (0,)), ((), ())), precision=lax.Precision.HIGHEST, preferred_element_type=jnp.float32
    )


def primitives(s):
    inverse = 1.0 / s[0]
    a, b, c = s[1] * inverse, s[2] * inverse, s[3] * inverse
    p = GAS_FACTOR * (s[4] - 0.5 * (s[1] * a + s[2] * b + s[3] * c))
    return a, b, c, p


def flux(s, vel, p, along):
    out = [s[along]] + [s[i] * vel for i in (1, 2, 3)] + [vel * (s[4] + p)]
    out[along] = out[along] + p
    return out


def axial_flux(s):
    inverse = 1.0 / s[0]
    a = s[1] * inverse
    p = GAS_FACTOR * (s[4] - 0.5 * ((s[1] * s[1] + s[2] * s[2] + s[3] * s[3]) * inverse))
    return flux(s, a, p, 1)


def halo_terms(x_ref, base, step, forward, chunks, outs):
    rows = x_ref.shape[2]
    scale = jnp.where(forward, -TIME_STEP, TIME_STEP)
    after = [[STENCIL[REACH + h - i - 1] if h <= i else 0.0 for h in range(REACH)] for i in range(REACH)]
    before = [[STENCIL[i + h] if i + h < REACH else 0.0 for h in range(REACH)] for i in range(REACH)]
    for r in range(0, rows, TILE):
        at = slice(r, r + TILE)
        near = []
        for h in range(REACH):
            near.append(axial_flux([x_ref[base + step * h, c, at, :] for c in range(COMPONENTS)]))
        for (first, count), out in zip(chunks, outs):
            for n in range(count):
                i = first + n
                weights = [scale * jnp.where(forward, after[i][h], before[i][h]) for h in range(REACH)]
                for c in range(COMPONENTS):
                    out[n, c, at, :] = sum(w * near[h][c] for h, w in enumerate(weights))


def toward(me, last):
    even = lax.rem(me, 2) == 0
    end = (me == 0) | (me == last)
    base = jnp.where(even, 0, REACH - 1)
    step = jnp.where(end, 0, jnp.where(even, 1, -1))
    return base, step, even != end


def outer_kernel(last, x_ref, *outs):
    base, step, forward = toward(lax.axis_index("ax"), last)
    halo_terms(x_ref, base, step, forward, SENDS, outs)


def inner_kernel(x_ref, t_ref, pack_ref):
    stations, _, rows, width = x_ref.shape
    forward = lax.rem(lax.axis_index("ax"), 2) == 1
    base = jnp.where(forward, 0, REACH - 1)
    step = jnp.where(forward, 1, -1)
    halo_terms(x_ref, base, step, forward, [(0, stations)], [t_ref])
    groups = rows // TILE
    lane = lax.broadcasted_iota(jnp.int32, (TILE, LANES), 1)
    for c in range(COMPONENTS):
        edge = jnp.zeros((TILE, LANES), jnp.float32)
        for s in range(stations):
            pack_ref[c, s * REACH : (s + 1) * REACH, :] = x_ref[s, c, 0:REACH, :]
            for g in range(groups):
                place = (s * groups + g) * 2 * REACH
                first = x_ref[s, c, g * TILE : (g + 1) * TILE, 0:LANES]
                final = x_ref[s, c, g * TILE : (g + 1) * TILE, width - LANES : width]
                both = pltpu.roll(jnp.where(lane < REACH, first, final), (place + REACH) % LANES, 1)
                edge = jnp.where((lane >= place) & (lane < place + 2 * REACH), both, edge)
        pack_ref[c, stations * REACH : stations * REACH + TILE, 0:LANES] = edge
        if width > LANES:
            pack_ref[c, stations * REACH : stations * REACH + TILE, LANES:width] = jnp.zeros(
                (TILE, width - LANES), jnp.float32
            )


def base_kernel(
    turn, x_ref, inner_ref, own_ref, left_ref, right_ref, across_ref, table_ref, back_ref, modes_ref, limit_ref,
    base_ref, weight_ref, inside_ref, basis_ref, unbasis_ref, radial_ref, axial_ref,
):
    stations, _, rows, width = x_ref.shape
    points = int(round(turn))
    groups = rows // TILE
    lane = lax.broadcasted_iota(jnp.int32, (TILE, LANES), 1)
    edge_rows = pl.ds(stations * REACH, TILE)
    per_angle = turn / (2.0 * math.pi)

    slot = lane % (2 * REACH)
    from_left = slot < REACH

    def edge_flux(s):
        _, _, vel, p = primitives(s)
        return flux(s, vel, p, 3)

    own = edge_flux([own_ref[c, edge_rows, 0:LANES] for c in range(COMPONENTS)])
    other = edge_flux(
        [
            jnp.where(from_left, left_ref[c, edge_rows, 0:LANES], right_ref[c, edge_rows, 0:LANES])
            for c in range(COMPONENTS)
        ]
    )
    fixes = []
    for c in range(COMPONENTS):
        change = other[c] - own[c]
        fix = jnp.zeros((TILE, LANES), jnp.float32)
        for k in range(1, REACH + 1):
            ahead = pltpu.roll(change, LANES - k, 1)
            behind = pltpu.roll(change, k, 1)
            fix = fix + STENCIL[k - 1] * jnp.where(
                from_left,
                jnp.where(slot + k >= REACH, ahead, 0.0),
                jnp.where(slot - k < REACH, -behind, 0.0),
            )
        fixes.append(fix)

    for s in range(stations):
        cross = [across_ref[c, s * REACH : (s + 1) * REACH, :] for c in range(COMPONENTS)]
        _, vel, _, p = primitives(cross)
        far = flux(cross, vel, p, 2)
        for c in range(COMPONENTS):
            sign = -1.0 if c in (2, 3) else 1.0
            for i in range(REACH):
                radial_ref[s, c, TILE - 1 - i : TILE - i, :] = (sign * (i + 0.5)) * far[c][i : i + 1, :]
        for g in range(groups):
            at = slice(g * TILE, (g + 1) * TILE)
            state = [x_ref[s, c, at, :] for c in range(COMPONENTS)]
            a, b, vel, p = primitives(state)
            ahead = flux(state, a, p, 1)
            out = flux(state, b, p, 2)
            swirl = flux(state, vel, p, 3)
            radius = (
                lax.broadcasted_iota(jnp.int32, (TILE, width), 0).astype(jnp.float32) + (g * TILE + 0.5)
            )
            for c in range(COMPONENTS):
                axial_ref[s, c, at, :] = TIME_STEP * ahead[c]
                radial_ref[s, c, TILE + g * TILE : TILE + (g + 1) * TILE, :] = radius * out[c]
                if g == groups - 1:
                    edge = out[c][TILE - 1 : TILE, :]
                    for m in range(1, REACH + 1):
                        radial_ref[s, c, TILE + rows + m - 1 : TILE + rows + m, :] = (rows - 0.5 + m) * edge
            place = (s * groups + g) * 2 * REACH
            source = {2: state[3] * vel + p, 3: -(state[2] * vel)}
            for c in range(COMPONENTS):
                turned = None
                for k in range(1, REACH + 1):
                    part = STENCIL[k - 1] * (
                        pltpu.roll(swirl[c], width - k, 1) - pltpu.roll(swirl[c], k, 1)
                    )
                    turned = part if turned is None else turned + part
                fix = pltpu.roll(fixes[c], (LANES - REACH - place) % LANES, 1)
                head = jnp.where(lane < REACH, fix, 0.0)
                tail = jnp.where(lane >= LANES - REACH, fix, 0.0)
                if width == LANES:
                    turned = turned + (head + tail)
                else:
                    middle = [jnp.zeros((TILE, width - 2 * LANES), jnp.float32)] if width > 2 * LANES else []
                    turned = turned + jnp.concatenate([head] + middle + [tail], axis=1)
                total = per_angle * turned
                if c in source:
                    total = total - source[c]
                base_ref[s, c, at, :] = total
    for g in range(groups):
        at = slice(g * TILE, (g + 1) * TILE)
        start = TILE + g * TILE
        radius = lax.broadcasted_iota(jnp.int32, (TILE, width), 0).astype(jnp.float32) + (g * TILE + 0.5)
        scale = TIME_STEP / radius
        for c in range(COMPONENTS):
            near = [axial_ref[h, c, at, :] for h in range(stations)]
            for s in range(stations):
                total = base_ref[s, c, at, :]
                for k in range(1, REACH + 1):
                    total = total + STENCIL[k - 1] * (
                        radial_ref[s, c, start + k : start + k + TILE, :]
                        - radial_ref[s, c, start - k : start - k + TILE, :]
                    )
                total = x_ref[s, c, at, :] + inner_ref[s, c, at, :] - scale * total
                for h in range(stations):
                    if h != s:
                        total = total + (STENCIL[abs(h - s) - 1] * (-1.0 if h > s else 1.0)) * near[h]
                base_ref[s, c, at, :] = total

    sector = lax.axis_index("az")
    basis_ref[...] = table_ref[sector]
    unbasis_ref[...] = back_ref[sector]
    line = lax.broadcasted_iota(jnp.int32, (rows, LANES), 0)
    for s in range(stations):
        inside_ref[s] = (line < limit_ref[s]).astype(jnp.float32)
    columns = 2 * MODE_MOST
    harmonic = lax.broadcasted_iota(jnp.int32, (rows, columns), 1) % MODE_MOST
    row = lax.broadcasted_iota(jnp.int32, (rows, columns), 0)
    kept = jnp.zeros((rows, columns), jnp.int32)
    for j in range(rows):
        kept = jnp.where(row == j, modes_ref[j], kept)
    weight = jnp.where(harmonic == 0, 1.0 / points, 2.0 / points).astype(jnp.float32)
    weight_ref[...] = jnp.where(harmonic < kept, weight, 0.0)


def forward_kernel(n, last, base_ref, basis_ref, *refs):
    section_ref, coeff_ref = refs[-2:]
    first, count = GROUPS[n]
    width = base_ref.shape[-1]
    me = lax.axis_index("ax")
    end = (me == 0) | (me == last)
    inside = [(a, m) for a, m in SENDS if first <= a < first + count]
    for i, (a, m) in enumerate(inside):
        terms = jnp.where(end, refs[2 * i][...], refs[2 * i + 1][...])
        section_ref[a - first : a - first + m] = base_ref[a : a + m] + terms
    coeff_ref[...] = exact_dot(section_ref[...].reshape(-1, width), basis_ref[...])


def smooth(total, section, weight, unbasis, inside):
    _, rows, width = section.shape
    kept = (total.reshape(COMPONENTS, rows, -1) * weight[None]).reshape(COMPONENTS * rows, -1)
    value = exact_dot(kept, unbasis).reshape(section.shape)
    pick = (inside > 0.5)[None]
    return [
        jnp.where(pick, value[:, :, t : t + LANES], section[:, :, t : t + LANES]) for t in range(0, width, LANES)
    ]


def inverse_kernel(n, section_ref, mine_ref, other_ref, weight_ref, unbasis_ref, inside_ref, *refs):
    first, count = GROUPS[n]
    copies = []
    if n == LAST:
        done, (out_ref, target, sem) = refs[:LAST], refs[LAST:]
        for i, ref in enumerate(done):
            a, m = GROUPS[i]
            copies.append(pltpu.make_async_copy(ref, out_ref.at[a : a + m], sem.at[i]))
        for copy in copies:
            copy.start()
    else:
        (target,) = refs
    lines = COMPONENTS * section_ref.shape[2]
    for s in range(count):
        part = slice(s * lines, (s + 1) * lines)
        total = mine_ref[part, :] + other_ref[part, :]
        parts = smooth(total, section_ref[s], weight_ref[...], unbasis_ref[...], inside_ref[first + s])
        for i, value in enumerate(parts):
            target[s, :, :, i * LANES : (i + 1) * LANES] = value
    if n == LAST:
        copies.append(pltpu.make_async_copy(target, out_ref.at[first : first + count], sem.at[LAST]))
        copies[-1].start()
        for copy in copies:
            copy.wait()


def fourier_tables(sectors, width):
    points = sectors * width
    harmonic = np.arange(2 * MODE_MOST) % MODE_MOST
    angle = (np.arange(points)[:, None] * harmonic[None, :] % points) * (2.0 * np.pi / points)
    table = np.where(np.arange(2 * MODE_MOST)[None, :] < MODE_MOST, np.cos(angle), np.sin(angle))
    return table.astype(np.float32).reshape(sectors, width, 2 * MODE_MOST)


def per_device_inner(conserved, cycle_modes, filtered_cycles):
    line = lax.axis_size("ax")
    sectors = lax.axis_size("az")
    stations, components, rows, width = conserved.shape
    if stations != REACH or components != COMPONENTS or line % 2 or sectors % 2:
        raise ValueError("unsupported shape")
    if (stations * rows // TILE) * 2 * REACH > LANES or width % LANES or rows % TILE:
        raise ValueError("unsupported shape")
    struct = lambda *shape: jax.ShapeDtypeStruct(shape, jnp.float32)
    block = struct(*conserved.shape)
    params = pltpu.CompilerParams(**PARAMS)
    columns = 2 * MODE_MOST

    def turned(value, by):
        return lax.ppermute(value, "az", [(i, (i + by) % sectors) for i in range(sectors)])

    def others(value):
        return turned(value, 1) if sectors == 2 else lax.psum(value, "az") - value

    def call(kernel, outs, ins, out_specs=None, scratch=(), scalars=0):
        many = isinstance(outs, tuple)
        return pl.pallas_call(
            kernel, out_shape=outs, in_specs=[VMEM] * (len(ins) - scalars) + [SMEM] * scalars,
            out_specs=out_specs or ((VMEM,) * len(outs) if many else VMEM),
            scratch_shapes=scratch, compiler_params=params,
        )(*ins)

    shapes = [struct(count, components, rows, width) for _, count in GROUPS]
    lines = components * rows
    table = fourier_tables(sectors, width)
    forth, back = jnp.asarray(table), jnp.asarray(np.ascontiguousarray(table.transpose(0, 2, 1)))

    pairs = [(i, i + 1) for i in range(1, line - 1, 2)]
    pairs += [(j, i) for i, j in pairs]
    route = [(i * sectors + a, j * sectors + a) for i, j in pairs for a in range(sectors)]
    route += [(i * sectors + a, i * sectors + (a + 1) % sectors) for i in (0, line - 1) for a in range(sectors)]
    terms = call(
        functools.partial(outer_kernel, line - 1),
        tuple(struct(m, components, rows, width) for _, m in SENDS), [conserved],
    )
    inner, pack = call(inner_kernel, (block, struct(components, stations * REACH + TILE, width)), [conserved])
    across = turned(pack, sectors // 2)
    left, right = (across, across) if sectors == 2 else (turned(pack, 1), turned(pack, -1))
    arrived = []
    for value in terms:
        arrived.append(lax.ppermute(value, ("ax", "az"), route))
    inner = lax.ppermute(inner, "ax", [(i, i ^ 1) for i in range(line)])
    base, weight, inside, basis, unbasis = call(
        functools.partial(base_kernel, float(width * sectors)),
        (block, struct(rows, columns), struct(stations, rows, LANES), struct(width, columns), struct(columns, width)),
        [conserved, inner, pack, left, right, across, forth, back, cycle_modes, filtered_cycles],
        scalars=2,
        scratch=[
            pltpu.VMEM((stations, COMPONENTS, rows + 2 * TILE, width), jnp.float32),
            pltpu.VMEM(conserved.shape, jnp.float32),
        ],
    )
    done = []
    for n, (first, count) in enumerate(GROUPS):
        both = []
        for (a, m), own, got in zip(SENDS, terms, arrived):
            if first <= a < first + count:
                both += [own, got]
        section, mine = call(
            functools.partial(forward_kernel, n, line - 1), (shapes[n], struct(count * lines, columns)),
            [base, basis, *both],
        )
        other = others(mine)
        operands = [section, mine, other, weight, unbasis, inside]
        if n < LAST:
            done.append(call(functools.partial(inverse_kernel, n), shapes[n], operands))
    return call(
        functools.partial(inverse_kernel, LAST), block, operands + done, out_specs=ANY,
        scratch=[pltpu.VMEM(shapes[LAST].shape, jnp.float32), pltpu.SemaphoreType.DMA((len(GROUPS),))],
    )


def solution(mesh):
    placed = (P("ax", None, None, "az"), P(), P("ax"))
    return jax.shard_map(
        per_device_inner, mesh=mesh, in_specs=placed, out_specs=P("ax", None, None, "az"), check_vma=False
    )
```

time: 30.3 us -> 26.4 us (0.87)
  the two profiles are of different devices: /device:TPU:9 before, /device:TPU:10 now
where the time goes in v2:
time: 26.4 us; the launch traced here: 26.2 us
  waiting for transfers between devices  13.1 us (50%)
  Pallas kernels  5.98 us (23%)
  starting transfers between devices  5.88 us (22%)
  local copies, waits for them, and re-layouts  1.11 us (4%)
    ppermute x4, waiting for transfers between devices, per_device_inner(): arrived.append(lax.ppermute(value, ('ax', 'az'), route))  8.23 us
    pallas_call x9, Pallas kernels, call(): pl.pallas_call(kernel, out_shape=outs, in_specs=[VMEM] * (len(ins) - scal...  5.98 us
    ppermute x4, waiting for transfers between devices, turned(): lax.ppermute(value, 'az', [(i, (i + by) % sectors) for i in range(sectors)])  4.89 us
    ppermute x4, starting transfers between devices, turned(): lax.ppermute(value, 'az', [(i, (i + by) % sectors) for i in range(sectors)])  3.72 us
    ppermute x4, starting transfers between devices, per_device_inner(): arrived.append(lax.ppermute(value, ('ax', 'az'), route))  2.08 us
    unnamed x10, local copies, waits for them, and re-layouts  1.11 us
  transfers between devices with their start and end apart: 9, of which 7 were waited for; matrix products, arithmetic and copies ran while one was open for 0% of the time, Pallas kernels for 18%

profile of v2, /device:TPU:10, one launch (start us, length us, event | category | flops | bytes accessed | tf_op | source)
XLA Modules:
  0.0 26.2 jit_solution(4420199666327706217)
XLA Ops:
  0.0 0.0 copy-start
  0.0 1.1 %copy-done = f32[4,5,32,256]{3,2,1,0:T(8,128)S(1)} copy-done((f32[4,5,32,256]{3,2,1,0:T(8,128)S(1)}, f32[4,5,32,256]{3,2,1,0:T(8,128)}, u32[]{:S(2)}) %copy-start) | copy-done | bytes 655384
  1.1 0.3 %shard_map.55 = (f32[4,5,32,256]{3,2,1,0:T(8,128)S(1)}, f32[5,24,256]{2,1,0:T(8,128)S(1)}) custom-call(f32[4,5,32,256]{3,2,1,0:T(8,128)S(1)} %copy-done), custom_call_target="tpu_custom_call" | custom-call | tf_op jit(solution)/shard_map/pallas_call | solution.py:312
  1.4 0.1 collective-permute-start
  1.5 0.0 copy-start.1
  1.5 0.0 copy-start.2
  1.5 1.6 %collective-permute-start.1 = (f32[5,24,256]{2,1,0:T(8,128)S(1)}, f32[5,24,256]{2,1,0:T(8,128)S(1)}, u32[]{:S(2)}, u32[]{:S(2)}) collective-permute-start(f32[5,24,256]{2,1,0:T(8,128)S(1)} %get-tuple-element.23.own_ref), channel_id=1, source_target_pairs={{0,1},{1,0},{2,3},{3,2},{4,5},{5,4},{6,7},{7,6},{8,9},{9,8},{10,11... | collective-permute-start | bytes 368648 | tf_op jit(solution)/shard_map/ppermute | solution.py:305
  3.1 0.2 shard_map.57
  3.3 0.3 %collective-permute-start.4 = (f32[1,5,32,256]{3,2,1,0:T(8,128)S(1)}, f32[1,5,32,256]{3,2,1,0:T(8,128)S(1)}, u32[]{:S(2)}, u32[]{:S(2)}) collective-permute-start(f32[1,5,32,256]{3,2,1,0:T(8,128)S(1)} %get-tuple-element.32.refs_0_), channel_id=1, source_target_pairs={{2,4},{3,5},{6,8},{7,9},{10,12},{11,13},{14,16},{15,17},{18,20},{1... | collective-permute-start | bytes 491528 | tf_op jit(solution)/shard_map/ppermute | solution.py:336
  3.7 1.5 %collective-permute-start.5 = (f32[1,5,32,256]{3,2,1,0:T(8,128)S(1)}, f32[1,5,32,256]{3,2,1,0:T(8,128)S(1)}, u32[]{:S(2)}, u32[]{:S(2)}) collective-permute-start(f32[1,5,32,256]{3,2,1,0:T(8,128)S(1)} %get-tuple-element.33.refs_2_), channel_id=1, source_target_pairs={{2,4},{3,5},{6,8},{7,9},{10,12},{11,13},{14,16},{15,17},{18,20},{1... | collective-permute-start | bytes 491528 | tf_op jit(solution)/shard_map/ppermute | solution.py:336
  5.1 0.0 copy-start.3
  5.1 0.0 copy-start.4
  5.1 0.3 %collective-permute-start.7 = (f32[1,5,32,256]{3,2,1,0:T(8,128)S(1)}, f32[1,5,32,256]{3,2,1,0:T(8,128)S(1)}, u32[]{:S(2)}, u32[]{:S(2)}) collective-permute-start(f32[1,5,32,256]{3,2,1,0:T(8,128)S(1)} %get-tuple-element.36.refs_0_), channel_id=1, source_target_pairs={{2,4},{3,5},{6,8},{7,9},{10,12},{11,13},{14,16},{15,17},{18,20},{1... | collective-permute-start | bytes 491528 | tf_op jit(solution)/shard_map/ppermute | solution.py:336
  5.4 1.8 %collective-permute-done.1.left_ref.right_ref.across_ref = f32[5,24,256]{2,1,0:T(8,128)S(1)} collective-permute-done((f32[5,24,256]{2,1,0:T(8,128)S(1)}, f32[5,24,256]{2,1,0:T(8,128)S(1)}, u32[]{:S(2)}, u32[]{:S(2)}) %collective-permute-start.1) | collective-permute-done | bytes 122912 | tf_op jit(solution)/shard_map/ppermute | solution.py:305
  7.2 0.0 collective-permute-start.2
  7.2 0.0 collective-permute-done.inner_ref
  7.2 0.0 copy-done.1
  7.2 0.0 copy-done.2
  7.2 0.0 copy-done.3
  7.2 0.0 copy-done.4
  7.2 2.8 %shard_map.56 = (f32[4,5,32,256]{3,2,1,0:T(8,128)S(1)}, f32[32,128]{1,0:T(8,128)S(1)}, f32[4,32,128]{2,1,0:T(8,128)S(1)}, f32[256,128]{1,0:T(8,128)S(1)}, f32[128,256]{1,0:T(8,128)S(1)}) custom-call(f32[4,5,32,256]{3,2,1,0:T(8,128)S(1)} %copy-done, f32[4,5,32,256]{3,2,1,0:T(8,128)S(1)} %collective-permute-done.inner_ref, ...), custom_call_target="tpu_custom_call" | custom-call | tf_op jit(solution)/shard_map/pallas_call | solution.py:312
  10.0 5.1 %collective-permute-done.4.refs_1_ = f32[1,5,32,256]{3,2,1,0:T(8,128)S(1)} collective-permute-done((f32[1,5,32,256]{3,2,1,0:T(8,128)S(1)}, f32[1,5,32,256]{3,2,1,0:T(8,128)S(1)}, u32[]{:S(2)}, u32[]{:S(2)}) %collective-permute-start.4) | collective-permute-done | bytes 163872 | tf_op jit(solution)/shard_map/ppermute | solution.py:336
  15.1 1.8 %collective-permute-done.5.refs_3_ = f32[1,5,32,256]{3,2,1,0:T(8,128)S(1)} collective-permute-done((f32[1,5,32,256]{3,2,1,0:T(8,128)S(1)}, f32[1,5,32,256]{3,2,1,0:T(8,128)S(1)}, u32[]{:S(2)}, u32[]{:S(2)}) %collective-permute-start.5) | collective-permute-done | bytes 163872 | tf_op jit(solution)/shard_map/ppermute | solution.py:336
  16.9 0.4 %shard_map.59 = (f32[2,5,32,256]{3,2,1,0:T(8,128)S(1)}, f32[320,128]{1,0:T(8,128)S(1)}) custom-call(f32[4,5,32,256]{3,2,1,0:T(8,128)S(1)} %get-tuple-element.24.base_ref, f32[256,128]{1,0:T(8,128)S(1)} %get-tuple-element.25.basis_ref, f32[1,5,32,256]{3,2,1,0:T(8,128)S(1)} %get-tuple-element.32.refs_0_, f32[1,5,32,256]{3,2,1,0:T(8,128)S(1)} %collective-permute-done.4.refs_1_, ...), custom_call_target="tpu_custom_call" | custom-call | tf_op jit(solution)/shard_map/pallas_call | solution.py:312
  17.3 0.6 %collective-permute-start.6 = (f32[320,128]{1,0:T(8,128)S(1)}, f32[320,128]{1,0:T(8,128)S(1)}, u32[]{:S(2)}, u32[]{:S(2)}) collective-permute-start(f32[320,128]{1,0:T(8,128)S(1)} %get-tuple-element.35.mine_ref), channel_id=1, source_target_pairs={{0,1},{1,0},{2,3},{3,2},{4,5},{5,4},{6,7},{7,6},{8,9},{9,8},{10,11... | collective-permute-start | bytes 491528 | tf_op jit(solution)/shard_map/ppermute | solution.py:305
  17.9 0.7 %collective-permute-done.7.refs_1_ = f32[1,5,32,256]{3,2,1,0:T(8,128)S(1)} collective-permute-done((f32[1,5,32,256]{3,2,1,0:T(8,128)S(1)}, f32[1,5,32,256]{3,2,1,0:T(8,128)S(1)}, u32[]{:S(2)}, u32[]{:S(2)}) %collective-permute-start.7) | collective-permute-done | bytes 163872 | tf_op jit(solution)/shard_map/ppermute | solution.py:336
  18.7 0.3 %shard_map.61 = (f32[1,5,32,256]{3,2,1,0:T(8,128)S(1)}, f32[160,128]{1,0:T(8,128)S(1)}) custom-call(f32[4,5,32,256]{3,2,1,0:T(8,128)S(1)} %get-tuple-element.24.base_ref, f32[256,128]{1,0:T(8,128)S(1)} %get-tuple-element.25.basis_ref, f32[1,5,32,256]{3,2,1,0:T(8,128)S(1)} %get-tuple-element.36.refs_0_, f32[1,5,32,256]{3,2,1,0:T(8,128)S(1)} %collective-permute-done.7.refs_1_), custom_call_target="tpu_custom_call" | custom-call | tf_op jit(solution)/shard_map/pallas_call | solution.py:312
  19.0 0.9 %collective-permute-start.8 = (f32[160,128]{1,0:T(8,128)S(1)}, f32[160,128]{1,0:T(8,128)S(1)}, u32[]{:S(2)}, u32[]{:S(2)}) collective-permute-start(f32[160,128]{1,0:T(8,128)S(1)} %get-tuple-element.38.mine_ref), channel_id=1, source_target_pairs={{0,1},{1,0},{2,3},{3,2},{4,5},{5,4},{6,7},{7,6},{8,9},{9,8},{10,11... | collective-permute-start | bytes 245768 | tf_op jit(solution)/shard_map/ppermute | solution.py:305
  19.8 0.6 %collective-permute-done.2.refs_1_ = f32[1,5,32,256]{3,2,1,0:T(8,128)S(1)} collective-permute-done((f32[1,5,32,256]{3,2,1,0:T(8,128)S(1)}, f32[1,5,32,256]{3,2,1,0:T(8,128)S(1)}, u32[]{:S(2)}, u32[]{:S(2)}) %collective-permute-start.2) | collective-permute-done | bytes 163872 | tf_op jit(solution)/shard_map/ppermute | solution.py:336
  20.4 0.3 %shard_map.58 = (f32[1,5,32,256]{3,2,1,0:T(8,128)S(1)}, f32[160,128]{1,0:T(8,128)S(1)}) custom-call(f32[4,5,32,256]{3,2,1,0:T(8,128)S(1)} %get-tuple-element.24.base_ref, f32[256,128]{1,0:T(8,128)S(1)} %get-tuple-element.25.basis_ref, f32[1,5,32,256]{3,2,1,0:T(8,128)S(1)} %get-tuple-element.26.refs_0_, f32[1,5,32,256]{3,2,1,0:T(8,128)S(1)} %collective-permute-done.2.refs_1_), custom_call_target="tpu_custom_call" | custom-call | tf_op jit(solution)/shard_map/pallas_call | solution.py:312
  20.7 0.7 %collective-permute-start.3 = (f32[160,128]{1,0:T(8,128)S(1)}, f32[160,128]{1,0:T(8,128)S(1)}, u32[]{:S(2)}, u32[]{:S(2)}) collective-permute-start(f32[160,128]{1,0:T(8,128)S(1)} %get-tuple-element.28.mine_ref), channel_id=1, source_target_pairs={{0,1},{1,0},{2,3},{3,2},{4,5},{5,4},{6,7},{7,6},{8,9},{9,8},{10,11... | collective-permute-start | bytes 245768 | tf_op jit(solution)/shard_map/ppermute | solution.py:305
  21.4 2.2 %collective-permute-done.8.other_ref = f32[160,128]{1,0:T(8,128)S(1)} collective-permute-done((f32[160,128]{1,0:T(8,128)S(1)}, f32[160,128]{1,0:T(8,128)S(1)}, u32[]{:S(2)}, u32[]{:S(2)}) %collective-permute-start.8) | collective-permute-done | bytes 81952 | tf_op jit(solution)/shard_map/ppermute | solution.py:305
  23.6 0.3 %shard_map.62.refs_1_ = f32[1,5,32,256]{3,2,1,0:T(8,128)S(1)} custom-call(f32[1,5,32,256]{3,2,1,0:T(8,128)S(1)} %get-tuple-element.37.section_ref, f32[160,128]{1,0:T(8,128)S(1)} %get-tuple-element.38.mine_ref, f32[160,128]{1,0:T(8,128)S(1)} %collective-permute-done.8.other_ref, f32[32,128]{1,0:T(8,128)S(1)} %get-tuple-element.29.weight_ref, ...), custom_call_target="tpu_custom_call" | custom-call | tf_op jit(solution)/shard_map/pallas_call | solution.py:312
  23.9 0.0 collective-permute-done.6.other_ref
  23.9 0.4 %shard_map.60.refs_0_ = f32[2,5,32,256]{3,2,1,0:T(8,128)S(1)} custom-call(f32[2,5,32,256]{3,2,1,0:T(8,128)S(1)} %get-tuple-element.34.section_ref, f32[320,128]{1,0:T(8,128)S(1)} %get-tuple-element.35.mine_ref, f32[320,128]{1,0:T(8,128)S(1)} %collective-permute-done.6.other_ref, f32[32,128]{1,0:T(8,128)S(1)} %get-tuple-element.29.weight_ref, ...), custom_call_target="tpu_custom_call" | custom-call | tf_op jit(solution)/shard_map/pallas_call | solution.py:312
  24.3 0.9 %collective-permute-done.3.other_ref = f32[160,128]{1,0:T(8,128)S(1)} collective-permute-done((f32[160,128]{1,0:T(8,128)S(1)}, f32[160,128]{1,0:T(8,128)S(1)}, u32[]{:S(2)}, u32[]{:S(2)}) %collective-permute-start.3) | collective-permute-done | bytes 81952 | tf_op jit(solution)/shard_map/ppermute | solution.py:305
  25.2 1.0 %shard_map.63 = f32[4,5,32,256]{3,2,1,0:T(8,128)} custom-call(f32[1,5,32,256]{3,2,1,0:T(8,128)S(1)} %get-tuple-element.27.section_ref, f32[160,128]{1,0:T(8,128)S(1)} %get-tuple-element.28.mine_ref, f32[160,128]{1,0:T(8,128)S(1)} %collective-permute-done.3.other_ref, f32[32,128]{1,0:T(8,128)S(1)} %get-tuple-element.29.weight_ref, ...), custom_call_target="tpu_custom_call" | custom-call | tf_op jit(solution)/shard_map/pallas_call | solution.py:312
Async XLA Ops:
  0.0 1.1 %copy-start = (f32[4,5,32,256]{3,2,1,0:T(8,128)S(1)}, f32[4,5,32,256]{3,2,1,0:T(8,128)}, u32[]{:S(2)}) copy-start(f32[4,5,32,256]{3,2,1,0:T(8,128)} %x_ref.5) | copy-start | bytes 1966084
  1.4 5.8 %collective-permute-start = (f32[4,5,32,256]{3,2,1,0:T(8,128)S(1)}, f32[4,5,32,256]{3,2,1,0:T(8,128)S(1)}, u32[]{:S(2)}, u32[]{:S(2)}) collective-permute-start(f32[4,5,32,256]{3,2,1,0:T(8,128)S(1)} %get-tuple-element.22), channel_id=1, source_target_pairs={{0,2},{2,0},{4,6},{6,4},{8,10},{10,8},{12,14},{14,12},{16,18},{18,... | collective-permute-start | bytes 1966088 | tf_op jit(solution)/shard_map/ppermute | solution.py:337
  1.5 5.7 %copy-start.1 = (f32[2,256,128]{2,1,0:T(8,128)S(1)}, f32[2,256,128]{2,1,0:T(8,128)}, u32[]{:S(2)}) copy-start(f32[2,256,128]{2,1,0:T(8,128)} %constant.4.clone.table_ref) | copy-start | bytes 786436
  1.5 5.7 %copy-start.2 = (f32[2,128,256]{2,1,0:T(8,128)S(1)}, f32[2,128,256]{2,1,0:T(8,128)}, u32[]{:S(2)}) copy-start(f32[2,128,256]{2,1,0:T(8,128)} %constant.5.clone.back_ref) | copy-start | bytes 786436
  1.5 5.7 %collective-permute-start.1 = (f32[5,24,256]{2,1,0:T(8,128)S(1)}, f32[5,24,256]{2,1,0:T(8,128)S(1)}, u32[]{:S(2)}, u32[]{:S(2)}) collective-permute-start(f32[5,24,256]{2,1,0:T(8,128)S(1)} %get-tuple-element.23.own_ref), channel_id=1, source_target_pairs={{0,1},{1,0},{2,3},{3,2},{4,5},{5,4},{6,7},{7,6},{8,9},{9,8},{10,11... | collective-permute-start | bytes 368648 | tf_op jit(solution)/shard_map/ppermute | solution.py:305
  3.3 11.8 %collective-permute-start.4 = (f32[1,5,32,256]{3,2,1,0:T(8,128)S(1)}, f32[1,5,32,256]{3,2,1,0:T(8,128)S(1)}, u32[]{:S(2)}, u32[]{:S(2)}) collective-permute-start(f32[1,5,32,256]{3,2,1,0:T(8,128)S(1)} %get-tuple-element.32.refs_0_), channel_id=1, source_target_pairs={{2,4},{3,5},{6,8},{7,9},{10,12},{11,13},{14,16},{15,17},{18,20},{1... | collective-permute-start | bytes 491528 | tf_op jit(solution)/shard_map/ppermute | solution.py:336
  3.7 13.3 %collective-permute-start.5 = (f32[1,5,32,256]{3,2,1,0:T(8,128)S(1)}, f32[1,5,32,256]{3,2,1,0:T(8,128)S(1)}, u32[]{:S(2)}, u32[]{:S(2)}) collective-permute-start(f32[1,5,32,256]{3,2,1,0:T(8,128)S(1)} %get-tuple-element.33.refs_2_), channel_id=1, source_target_pairs={{2,4},{3,5},{6,8},{7,9},{10,12},{11,13},{14,16},{15,17},{18,20},{1... | collective-permute-start | bytes 491528 | tf_op jit(solution)/shard_map/ppermute | solution.py:336
  5.1 2.1 %copy-start.3 = (s32[32]{0:T(128)S(1)}, s32[32]{0:T(128)}, u32[]{:S(2)}) copy-start(s32[32]{0:T(128)} %modes_ref.1) | copy-start | bytes 388
  5.1 2.1 %copy-start.4 = (s32[4]{0:T(128)S(1)}, s32[4]{0:T(128)}, u32[]{:S(2)}) copy-start(s32[4]{0:T(128)} %limit_ref.1) | copy-start | bytes 52
  5.1 13.5 %collective-permute-start.7 = (f32[1,5,32,256]{3,2,1,0:T(8,128)S(1)}, f32[1,5,32,256]{3,2,1,0:T(8,128)S(1)}, u32[]{:S(2)}, u32[]{:S(2)}) collective-permute-start(f32[1,5,32,256]{3,2,1,0:T(8,128)S(1)} %get-tuple-element.36.refs_0_), channel_id=1, source_target_pairs={{2,4},{3,5},{6,8},{7,9},{10,12},{11,13},{14,16},{15,17},{18,20},{1... | collective-permute-start | bytes 491528 | tf_op jit(solution)/shard_map/ppermute | solution.py:336
  7.2 13.2 %collective-permute-start.2 = (f32[1,5,32,256]{3,2,1,0:T(8,128)S(1)}, f32[1,5,32,256]{3,2,1,0:T(8,128)S(1)}, u32[]{:S(2)}, u32[]{:S(2)}) collective-permute-start(f32[1,5,32,256]{3,2,1,0:T(8,128)S(1)} %get-tuple-element.26.refs_0_), channel_id=1, source_target_pairs={{2,4},{3,5},{6,8},{7,9},{10,12},{11,13},{14,16},{15,17},{18,20},{1... | collective-permute-start | bytes 491528 | tf_op jit(solution)/shard_map/ppermute | solution.py:336
  17.3 6.6 %collective-permute-start.6 = (f32[320,128]{1,0:T(8,128)S(1)}, f32[320,128]{1,0:T(8,128)S(1)}, u32[]{:S(2)}, u32[]{:S(2)}) collective-permute-start(f32[320,128]{1,0:T(8,128)S(1)} %get-tuple-element.35.mine_ref), channel_id=1, source_target_pairs={{0,1},{1,0},{2,3},{3,2},{4,5},{5,4},{6,7},{7,6},{8,9},{9,8},{10,11... | collective-permute-start | bytes 491528 | tf_op jit(solution)/shard_map/ppermute | solution.py:305
  19.0 4.6 %collective-permute-start.8 = (f32[160,128]{1,0:T(8,128)S(1)}, f32[160,128]{1,0:T(8,128)S(1)}, u32[]{:S(2)}, u32[]{:S(2)}) collective-permute-start(f32[160,128]{1,0:T(8,128)S(1)} %get-tuple-element.38.mine_ref), channel_id=1, source_target_pairs={{0,1},{1,0},{2,3},{3,2},{4,5},{5,4},{6,7},{7,6},{8,9},{9,8},{10,11... | collective-permute-start | bytes 245768 | tf_op jit(solution)/shard_map/ppermute | solution.py:305
  20.7 4.5 %collective-permute-start.3 = (f32[160,128]{1,0:T(8,128)S(1)}, f32[160,128]{1,0:T(8,128)S(1)}, u32[]{:S(2)}, u32[]{:S(2)}) collective-permute-start(f32[160,128]{1,0:T(8,128)S(1)} %get-tuple-element.28.mine_ref), channel_id=1, source_target_pairs={{0,1},{1,0},{2,3},{3,2},{4,5},{5,4},{6,7},{7,6},{8,9},{9,8},{10,11... | collective-permute-start | bytes 245768 | tf_op jit(solution)/shard_map/ppermute | solution.py:305

commit v3 on v2

--- a/solution.py
+++ b/solution.py
@@ -28,10 +28,17 @@
 PARAMS = dict(vmem_limit_bytes=8 << 20)
 
 
-def exact_dot(a, b):
-    return lax.dot_general(
-        a, b, (((1,), (0,)), ((), ())), precision=lax.Precision.HIGHEST, preferred_element_type=jnp.float32
-    )
+def halves(value):
+    high = value.astype(jnp.bfloat16)
+    return high, (value - high.astype(jnp.float32)).astype(jnp.bfloat16)
+
+
+def close_dot(a, high, low):
+    def dot(p, q):
+        return lax.dot_general(p, q, (((1,), (0,)), ((), ())), preferred_element_type=jnp.float32)
+
+    top, rest = halves(a)
+    return dot(top, high) + (dot(top, low) + dot(rest, high))
 
 
 def primitives(s):
@@ -80,9 +87,9 @@
     return base, step, even != end
 
 
-def outer_kernel(last, x_ref, *outs):
+def outer_kernel(last, chunks, x_ref, *outs):
     base, step, forward = toward(lax.axis_index("ax"), last)
-    halo_terms(x_ref, base, step, forward, SENDS, outs)
+    halo_terms(x_ref, base, step, forward, chunks, outs)
 
 
 def inner_kernel(x_ref, t_ref, pack_ref):
@@ -216,8 +223,8 @@
                 base_ref[s, c, at, :] = total
 
     sector = lax.axis_index("az")
-    basis_ref[...] = table_ref[sector]
-    unbasis_ref[...] = back_ref[sector]
+    basis_ref[0], basis_ref[1] = halves(table_ref[sector])
+    unbasis_ref[0], unbasis_ref[1] = halves(back_ref[sector])
     line = lax.broadcasted_iota(jnp.int32, (rows, LANES), 0)
     for s in range(stations):
         inside_ref[s] = (line < limit_ref[s]).astype(jnp.float32)
@@ -241,13 +248,13 @@
     for i, (a, m) in enumerate(inside):
         terms = jnp.where(end, refs[2 * i][...], refs[2 * i + 1][...])
         section_ref[a - first : a - first + m] = base_ref[a : a + m] + terms
-    coeff_ref[...] = exact_dot(section_ref[...].reshape(-1, width), basis_ref[...])
+    coeff_ref[...] = close_dot(section_ref[...].reshape(-1, width), basis_ref[0], basis_ref[1])
 
 
 def smooth(total, section, weight, unbasis, inside):
     _, rows, width = section.shape
     kept = (total.reshape(COMPONENTS, rows, -1) * weight[None]).reshape(COMPONENTS * rows, -1)
-    value = exact_dot(kept, unbasis).reshape(section.shape)
+    value = close_dot(kept, unbasis[0], unbasis[1]).reshape(section.shape)
     pick = (inside > 0.5)[None]
     return [
         jnp.where(pick, value[:, :, t : t + LANES], section[:, :, t : t + LANES]) for t in range(0, width, LANES)
@@ -324,10 +331,12 @@
     pairs += [(j, i) for i, j in pairs]
     route = [(i * sectors + a, j * sectors + a) for i, j in pairs for a in range(sectors)]
     route += [(i * sectors + a, i * sectors + (a + 1) % sectors) for i in (0, line - 1) for a in range(sectors)]
-    terms = call(
-        functools.partial(outer_kernel, line - 1),
-        tuple(struct(m, components, rows, width) for _, m in SENDS), [conserved],
-    )
+    terms = []
+    for chunks in (SENDS[:1], SENDS[1:]):
+        terms += call(
+            functools.partial(outer_kernel, line - 1, chunks),
+            tuple(struct(m, components, rows, width) for _, m in chunks), [conserved],
+        )
     inner, pack = call(inner_kernel, (block, struct(components, stations * REACH + TILE, width)), [conserved])
     across = turned(pack, sectors // 2)
     left, right = (across, across) if sectors == 2 else (turned(pack, 1), turned(pack, -1))
@@ -337,7 +346,11 @@
     inner = lax.ppermute(inner, "ax", [(i, i ^ 1) for i in range(line)])
     base, weight, inside, basis, unbasis = call(
         functools.partial(base_kernel, float(width * sectors)),
-        (block, struct(rows, columns), struct(stations, rows, LANES), struct(width, columns), struct(columns, width)),
+        (
+            block, struct(rows, columns), struct(stations, rows, LANES),
+            jax.ShapeDtypeStruct((2, width, columns), jnp.bfloat16),
+            jax.ShapeDtypeStruct((2, columns, width), jnp.bfloat16),
+        ),
         [conserved, inner, pack, left, right, across, forth, back, cycle_modes, filtered_cycles],
         scalars=2,
         scratch=[

time: 26.4 us -> 26.2 us (level)
  the two profiles are of different devices: /device:TPU:10 before, /device:TPU:18 now
where the time goes in v3:
time: 26.2 us; the launch traced here: 26 us
  waiting for transfers between devices  13.5 us (52%)
  starting transfers between devices  5.74 us (22%)
  Pallas kernels  5.54 us (21%)
  local copies, waits for them, and re-layouts  1.11 us (4%)
    ppermute x4, waiting for transfers between devices, per_device_inner(): arrived.append(lax.ppermute(value, ('ax', 'az'), route))  8.51 us
    pallas_call x10, Pallas kernels, call(): pl.pallas_call(kernel, out_shape=outs, in_specs=[VMEM] * (len(ins) - scal...  5.54 us
    ppermute x4, waiting for transfers between devices, turned(): lax.ppermute(value, 'az', [(i, (i + by) % sectors) for i in range(sectors)])  4.99 us
    ppermute x4, starting transfers between devices, turned(): lax.ppermute(value, 'az', [(i, (i + by) % sectors) for i in range(sectors)])  3.5 us
    ppermute x4, starting transfers between devices, per_device_inner(): arrived.append(lax.ppermute(value, ('ax', 'az'), route))  2.17 us
    unnamed x10, local copies, waits for them, and re-layouts  1.11 us
  transfers between devices with their start and end apart: 9, of which 7 were waited for; matrix products, arithmetic and copies ran while one was open for 0% of the time, Pallas kernels for 17%

profile of v3, /device:TPU:18, one launch (start us, length us, event | category | flops | bytes accessed | tf_op | source)
XLA Modules:
  0.0 26.0 jit_solution(3404376176881218003)
XLA Ops:
  0.0 0.0 copy-start
  0.0 1.1 %copy-done = f32[4,5,32,256]{3,2,1,0:T(8,128)S(1)} copy-done((f32[4,5,32,256]{3,2,1,0:T(8,128)S(1)}, f32[4,5,32,256]{3,2,1,0:T(8,128)}, u32[]{:S(2)}) %copy-start) | copy-done | bytes 655384
  1.1 0.3 %shard_map.55 = (f32[4,5,32,256]{3,2,1,0:T(8,128)S(1)}, f32[5,24,256]{2,1,0:T(8,128)S(1)}) custom-call(f32[4,5,32,256]{3,2,1,0:T(8,128)S(1)} %copy-done), custom_call_target="tpu_custom_call" | custom-call | tf_op jit(solution)/shard_map/pallas_call | solution.py:319
  1.4 0.1 collective-permute-start
  1.5 1.6 %collective-permute-start.1 = (f32[5,24,256]{2,1,0:T(8,128)S(1)}, f32[5,24,256]{2,1,0:T(8,128)S(1)}, u32[]{:S(2)}, u32[]{:S(2)}) collective-permute-start(f32[5,24,256]{2,1,0:T(8,128)S(1)} %get-tuple-element.22.own_ref), channel_id=1, source_target_pairs={{0,1},{1,0},{2,3},{3,2},{4,5},{5,4},{6,7},{7,6},{8,9},{9,8},{10,11... | collective-permute-start | bytes 368648 | tf_op jit(solution)/shard_map/ppermute | solution.py:312
  3.1 0.2 shard_map.57
  3.3 0.0 copy-start.1
  3.3 0.0 copy-start.2
  3.3 0.4 %collective-permute-start.5 = (f32[1,5,32,256]{3,2,1,0:T(8,128)S(1)}, f32[1,5,32,256]{3,2,1,0:T(8,128)S(1)}, u32[]{:S(2)}, u32[]{:S(2)}) collective-permute-start(f32[1,5,32,256]{3,2,1,0:T(8,128)S(1)} %get-tuple-element.31.refs_2_), channel_id=1, source_target_pairs={{2,4},{3,5},{6,8},{7,9},{10,12},{11,13},{14,16},{15,17},{18,20},{1... | collective-permute-start | bytes 491528 | tf_op jit(solution)/shard_map/ppermute | solution.py:345
  3.6 0.1 shard_map.59.refs_0_
  3.8 1.5 %collective-permute-start.4 = (f32[1,5,32,256]{3,2,1,0:T(8,128)S(1)}, f32[1,5,32,256]{3,2,1,0:T(8,128)S(1)}, u32[]{:S(2)}, u32[]{:S(2)}) collective-permute-start(f32[1,5,32,256]{3,2,1,0:T(8,128)S(1)} %shard_map.59.refs_0_), channel_id=1, source_target_pairs={{2,4},{3,5},{6,8},{7,9},{10,12},{11,13},{14,16},{15,17},{18,20},{1... | collective-permute-start | bytes 491528 | tf_op jit(solution)/shard_map/ppermute | solution.py:345
  5.3 0.0 copy-start.3
  5.3 0.0 copy-start.4
  5.3 0.3 %collective-permute-start.7 = (f32[1,5,32,256]{3,2,1,0:T(8,128)S(1)}, f32[1,5,32,256]{3,2,1,0:T(8,128)S(1)}, u32[]{:S(2)}, u32[]{:S(2)}) collective-permute-start(f32[1,5,32,256]{3,2,1,0:T(8,128)S(1)} %get-tuple-element.34.refs_0_), channel_id=1, source_target_pairs={{2,4},{3,5},{6,8},{7,9},{10,12},{11,13},{14,16},{15,17},{18,20},{1... | collective-permute-start | bytes 491528 | tf_op jit(solution)/shard_map/ppermute | solution.py:345
  5.6 1.6 %collective-permute-done.1.left_ref.right_ref.across_ref = f32[5,24,256]{2,1,0:T(8,128)S(1)} collective-permute-done((f32[5,24,256]{2,1,0:T(8,128)S(1)}, f32[5,24,256]{2,1,0:T(8,128)S(1)}, u32[]{:S(2)}, u32[]{:S(2)}) %collective-permute-start.1) | collective-permute-done | bytes 122912 | tf_op jit(solution)/shard_map/ppermute | solution.py:312
  7.2 0.0 collective-permute-start.2
  7.2 0.0 collective-permute-done.inner_ref
  7.2 0.0 copy-done.1
  7.2 0.0 copy-done.2
  7.2 0.0 copy-done.3
  7.2 0.0 copy-done.4
  7.2 2.8 %shard_map.56 = (f32[4,5,32,256]{3,2,1,0:T(8,128)S(1)}, f32[32,128]{1,0:T(8,128)S(1)}, f32[4,32,128]{2,1,0:T(8,128)S(1)}, bf16[2,256,128]{2,1,0:T(8,128)(2,1)S(1)}, bf16[2,128,256]{2,1,0:T(8,128)(2,1)S(1)}) custom-call(f32[4,5,32,256]{3,2,1,0:T(8,128)S(1)} %copy-done, f32[4,5,32,256]{3,2,1,0:T(8,128)S(1)} %collective-permute-done.inner_ref, ...), custom_call_target="tpu_custom_call" | custom-call | tf_op jit(solution)/shard_map/pallas_call | solution.py:319
  10.0 5.1 %collective-permute-done.5.refs_3_ = f32[1,5,32,256]{3,2,1,0:T(8,128)S(1)} collective-permute-done((f32[1,5,32,256]{3,2,1,0:T(8,128)S(1)}, f32[1,5,32,256]{3,2,1,0:T(8,128)S(1)}, u32[]{:S(2)}, u32[]{:S(2)}) %collective-permute-start.5) | collective-permute-done | bytes 163872 | tf_op jit(solution)/shard_map/ppermute | solution.py:345
  15.1 1.8 %collective-permute-done.4.refs_1_ = f32[1,5,32,256]{3,2,1,0:T(8,128)S(1)} collective-permute-done((f32[1,5,32,256]{3,2,1,0:T(8,128)S(1)}, f32[1,5,32,256]{3,2,1,0:T(8,128)S(1)}, u32[]{:S(2)}, u32[]{:S(2)}) %collective-permute-start.4) | collective-permute-done | bytes 163872 | tf_op jit(solution)/shard_map/ppermute | solution.py:345
  16.9 0.3 %shard_map.60 = (f32[2,5,32,256]{3,2,1,0:T(8,128)S(1)}, f32[320,128]{1,0:T(8,128)S(1)}) custom-call(f32[4,5,32,256]{3,2,1,0:T(8,128)S(1)} %get-tuple-element.23.base_ref, bf16[2,256,128]{2,1,0:T(8,128)(2,1)S(1)} %get-tuple-element.24.basis_ref, f32[1,5,32,256]{3,2,1,0:T(8,128)S(1)} %shard_map.59.refs_0_, ...), custom_call_target="tpu_custom_call" | custom-call | tf_op jit(solution)/shard_map/pallas_call | solution.py:319
  17.2 0.6 %collective-permute-start.6 = (f32[320,128]{1,0:T(8,128)S(1)}, f32[320,128]{1,0:T(8,128)S(1)}, u32[]{:S(2)}, u32[]{:S(2)}) collective-permute-start(f32[320,128]{1,0:T(8,128)S(1)} %get-tuple-element.33.mine_ref), channel_id=1, source_target_pairs={{0,1},{1,0},{2,3},{3,2},{4,5},{5,4},{6,7},{7,6},{8,9},{9,8},{10,11... | collective-permute-start | bytes 491528 | tf_op jit(solution)/shard_map/ppermute | solution.py:312
  17.8 0.9 %collective-permute-done.7.refs_1_ = f32[1,5,32,256]{3,2,1,0:T(8,128)S(1)} collective-permute-done((f32[1,5,32,256]{3,2,1,0:T(8,128)S(1)}, f32[1,5,32,256]{3,2,1,0:T(8,128)S(1)}, u32[]{:S(2)}, u32[]{:S(2)}) %collective-permute-start.7) | collective-permute-done | bytes 163872 | tf_op jit(solution)/shard_map/ppermute | solution.py:345
  18.6 0.2 shard_map.62
  18.9 0.7 %collective-permute-start.8 = (f32[160,128]{1,0:T(8,128)S(1)}, f32[160,128]{1,0:T(8,128)S(1)}, u32[]{:S(2)}, u32[]{:S(2)}) collective-permute-start(f32[160,128]{1,0:T(8,128)S(1)} %get-tuple-element.36.mine_ref), channel_id=1, source_target_pairs={{0,1},{1,0},{2,3},{3,2},{4,5},{5,4},{6,7},{7,6},{8,9},{9,8},{10,11... | collective-permute-start | bytes 245768 | tf_op jit(solution)/shard_map/ppermute | solution.py:312
  19.6 0.8 %collective-permute-done.2.refs_1_ = f32[1,5,32,256]{3,2,1,0:T(8,128)S(1)} collective-permute-done((f32[1,5,32,256]{3,2,1,0:T(8,128)S(1)}, f32[1,5,32,256]{3,2,1,0:T(8,128)S(1)}, u32[]{:S(2)}, u32[]{:S(2)}) %collective-permute-start.2) | collective-permute-done | bytes 163872 | tf_op jit(solution)/shard_map/ppermute | solution.py:345
  20.4 0.2 shard_map.58
  20.6 0.6 %collective-permute-start.3 = (f32[160,128]{1,0:T(8,128)S(1)}, f32[160,128]{1,0:T(8,128)S(1)}, u32[]{:S(2)}, u32[]{:S(2)}) collective-permute-start(f32[160,128]{1,0:T(8,128)S(1)} %get-tuple-element.27.mine_ref), channel_id=1, source_target_pairs={{0,1},{1,0},{2,3},{3,2},{4,5},{5,4},{6,7},{7,6},{8,9},{9,8},{10,11... | collective-permute-start | bytes 245768 | tf_op jit(solution)/shard_map/ppermute | solution.py:312
  21.2 2.2 %collective-permute-done.8.other_ref = f32[160,128]{1,0:T(8,128)S(1)} collective-permute-done((f32[160,128]{1,0:T(8,128)S(1)}, f32[160,128]{1,0:T(8,128)S(1)}, u32[]{:S(2)}, u32[]{:S(2)}) %collective-permute-start.8) | collective-permute-done | bytes 81952 | tf_op jit(solution)/shard_map/ppermute | solution.py:312
  23.4 0.2 shard_map.63.refs_1_
  23.7 0.0 collective-permute-done.6.other_ref
  23.7 0.3 %shard_map.61.refs_0_ = f32[2,5,32,256]{3,2,1,0:T(8,128)S(1)} custom-call(f32[2,5,32,256]{3,2,1,0:T(8,128)S(1)} %get-tuple-element.32.section_ref, f32[320,128]{1,0:T(8,128)S(1)} %get-tuple-element.33.mine_ref, f32[320,128]{1,0:T(8,128)S(1)} %collective-permute-done.6.other_ref, f32[32,128]{1,0:T(8,128)S(1)} %get-tuple-element.28.weight_ref, ...), custom_call_target="tpu_custom_call" | custom-call | tf_op jit(solution)/shard_map/pallas_call | solution.py:319
  24.0 1.2 %collective-permute-done.3.other_ref = f32[160,128]{1,0:T(8,128)S(1)} collective-permute-done((f32[160,128]{1,0:T(8,128)S(1)}, f32[160,128]{1,0:T(8,128)S(1)}, u32[]{:S(2)}, u32[]{:S(2)}) %collective-permute-start.3) | collective-permute-done | bytes 81952 | tf_op jit(solution)/shard_map/ppermute | solution.py:312
  25.1 0.9 %shard_map.64 = f32[4,5,32,256]{3,2,1,0:T(8,128)} custom-call(f32[1,5,32,256]{3,2,1,0:T(8,128)S(1)} %get-tuple-element.26.section_ref, f32[160,128]{1,0:T(8,128)S(1)} %get-tuple-element.27.mine_ref, f32[160,128]{1,0:T(8,128)S(1)} %collective-permute-done.3.other_ref, f32[32,128]{1,0:T(8,128)S(1)} %get-tuple-element.28.weight_ref, ...), custom_call_target="tpu_custom_call" | custom-call | tf_op jit(solution)/shard_map/pallas_call | solution.py:319
Async XLA Ops:
  0.0 1.1 %copy-start = (f32[4,5,32,256]{3,2,1,0:T(8,128)S(1)}, f32[4,5,32,256]{3,2,1,0:T(8,128)}, u32[]{:S(2)}) copy-start(f32[4,5,32,256]{3,2,1,0:T(8,128)} %x_ref.7) | copy-start | bytes 1966084
  1.4 5.8 %collective-permute-start = (f32[4,5,32,256]{3,2,1,0:T(8,128)S(1)}, f32[4,5,32,256]{3,2,1,0:T(8,128)S(1)}, u32[]{:S(2)}, u32[]{:S(2)}) collective-permute-start(f32[4,5,32,256]{3,2,1,0:T(8,128)S(1)} %get-tuple-element.21), channel_id=1, source_target_pairs={{0,2},{2,0},{4,6},{6,4},{8,10},{10,8},{12,14},{14,12},{16,18},{18,... | collective-permute-start | bytes 1966088 | tf_op jit(solution)/shard_map/ppermute | solution.py:346
  1.5 5.7 %collective-permute-start.1 = (f32[5,24,256]{2,1,0:T(8,128)S(1)}, f32[5,24,256]{2,1,0:T(8,128)S(1)}, u32[]{:S(2)}, u32[]{:S(2)}) collective-permute-start(f32[5,24,256]{2,1,0:T(8,128)S(1)} %get-tuple-element.22.own_ref), channel_id=1, source_target_pairs={{0,1},{1,0},{2,3},{3,2},{4,5},{5,4},{6,7},{7,6},{8,9},{9,8},{10,11... | collective-permute-start | bytes 368648 | tf_op jit(solution)/shard_map/ppermute | solution.py:312
  3.3 4.0 %copy-start.1 = (f32[2,256,128]{2,1,0:T(8,128)S(1)}, f32[2,256,128]{2,1,0:T(8,128)}, u32[]{:S(2)}) copy-start(f32[2,256,128]{2,1,0:T(8,128)} %constant.4.clone.table_ref) | copy-start | bytes 786436
  3.3 3.9 %copy-start.2 = (f32[2,128,256]{2,1,0:T(8,128)S(1)}, f32[2,128,256]{2,1,0:T(8,128)}, u32[]{:S(2)}) copy-start(f32[2,128,256]{2,1,0:T(8,128)} %constant.5.clone.back_ref) | copy-start | bytes 786436
  3.3 11.8 %collective-permute-start.5 = (f32[1,5,32,256]{3,2,1,0:T(8,128)S(1)}, f32[1,5,32,256]{3,2,1,0:T(8,128)S(1)}, u32[]{:S(2)}, u32[]{:S(2)}) collective-permute-start(f32[1,5,32,256]{3,2,1,0:T(8,128)S(1)} %get-tuple-element.31.refs_2_), channel_id=1, source_target_pairs={{2,4},{3,5},{6,8},{7,9},{10,12},{11,13},{14,16},{15,17},{18,20},{1... | collective-permute-start | bytes 491528 | tf_op jit(solution)/shard_map/ppermute | solution.py:345
  3.8 13.1 %collective-permute-start.4 = (f32[1,5,32,256]{3,2,1,0:T(8,128)S(1)}, f32[1,5,32,256]{3,2,1,0:T(8,128)S(1)}, u32[]{:S(2)}, u32[]{:S(2)}) collective-permute-start(f32[1,5,32,256]{3,2,1,0:T(8,128)S(1)} %shard_map.59.refs_0_), channel_id=1, source_target_pairs={{2,4},{3,5},{6,8},{7,9},{10,12},{11,13},{14,16},{15,17},{18,20},{1... | collective-permute-start | bytes 491528 | tf_op jit(solution)/shard_map/ppermute | solution.py:345
  5.3 1.9 %copy-start.3 = (s32[32]{0:T(128)S(1)}, s32[32]{0:T(128)}, u32[]{:S(2)}) copy-start(s32[32]{0:T(128)} %modes_ref.1) | copy-start | bytes 388
  5.3 2.0 %copy-start.4 = (s32[4]{0:T(128)S(1)}, s32[4]{0:T(128)}, u32[]{:S(2)}) copy-start(s32[4]{0:T(128)} %limit_ref.1) | copy-start | bytes 52
  5.3 13.3 %collective-permute-start.7 = (f32[1,5,32,256]{3,2,1,0:T(8,128)S(1)}, f32[1,5,32,256]{3,2,1,0:T(8,128)S(1)}, u32[]{:S(2)}, u32[]{:S(2)}) collective-permute-start(f32[1,5,32,256]{3,2,1,0:T(8,128)S(1)} %get-tuple-element.34.refs_0_), channel_id=1, source_target_pairs={{2,4},{3,5},{6,8},{7,9},{10,12},{11,13},{14,16},{15,17},{18,20},{1... | collective-permute-start | bytes 491528 | tf_op jit(solution)/shard_map/ppermute | solution.py:345
  7.2 13.2 %collective-permute-start.2 = (f32[1,5,32,256]{3,2,1,0:T(8,128)S(1)}, f32[1,5,32,256]{3,2,1,0:T(8,128)S(1)}, u32[]{:S(2)}, u32[]{:S(2)}) collective-permute-start(f32[1,5,32,256]{3,2,1,0:T(8,128)S(1)} %get-tuple-element.25.refs_0_), channel_id=1, source_target_pairs={{2,4},{3,5},{6,8},{7,9},{10,12},{11,13},{14,16},{15,17},{18,20},{1... | collective-permute-start | bytes 491528 | tf_op jit(solution)/shard_map/ppermute | solution.py:345
  17.2 6.5 %collective-permute-start.6 = (f32[320,128]{1,0:T(8,128)S(1)}, f32[320,128]{1,0:T(8,128)S(1)}, u32[]{:S(2)}, u32[]{:S(2)}) collective-permute-start(f32[320,128]{1,0:T(8,128)S(1)} %get-tuple-element.33.mine_ref), channel_id=1, source_target_pairs={{0,1},{1,0},{2,3},{3,2},{4,5},{5,4},{6,7},{7,6},{8,9},{9,8},{10,11... | collective-permute-start | bytes 491528 | tf_op jit(solution)/shard_map/ppermute | solution.py:312
  18.9 4.6 %collective-permute-start.8 = (f32[160,128]{1,0:T(8,128)S(1)}, f32[160,128]{1,0:T(8,128)S(1)}, u32[]{:S(2)}, u32[]{:S(2)}) collective-permute-start(f32[160,128]{1,0:T(8,128)S(1)} %get-tuple-element.36.mine_ref), channel_id=1, source_target_pairs={{0,1},{1,0},{2,3},{3,2},{4,5},{5,4},{6,7},{7,6},{8,9},{9,8},{10,11... | collective-permute-start | bytes 245768 | tf_op jit(solution)/shard_map/ppermute | solution.py:312
  20.6 4.5 %collective-permute-start.3 = (f32[160,128]{1,0:T(8,128)S(1)}, f32[160,128]{1,0:T(8,128)S(1)}, u32[]{:S(2)}, u32[]{:S(2)}) collective-permute-start(f32[160,128]{1,0:T(8,128)S(1)} %get-tuple-element.27.mine_ref), channel_id=1, source_target_pairs={{0,1},{1,0},{2,3},{3,2},{4,5},{5,4},{6,7},{7,6},{8,9},{9,8},{10,11... | collective-permute-start | bytes 245768 | tf_op jit(solution)/shard_map/ppermute | solution.py:312

commit v4 on v3

--- a/solution.py
+++ b/solution.py
@@ -87,9 +87,38 @@
     return base, step, even != end
 
 
-def outer_kernel(last, chunks, x_ref, *outs):
+def border_terms(near, forward, n, c):
+    scale = jnp.where(forward, -TIME_STEP, TIME_STEP)
+    return scale * sum(STENCIL[REACH + h - n - 1] * near[h][c] for h in range(n + 1))
+
+
+def place_of(n):
+    return jnp.where(lax.rem(lax.axis_index("ax"), 2) == 0, REACH - 1 - n, n)
+
+
+def first_kernel(last, x_ref, out_ref, buffer, sem):
+    base, _, forward = toward(lax.axis_index("ax"), last)
+    copy = pltpu.make_async_copy(x_ref.at[base], buffer, sem)
+    copy.start()
+    copy.wait()
+    for r in range(0, buffer.shape[1], TILE):
+        at = slice(r, r + TILE)
+        near = [axial_flux([buffer[c, at, :] for c in range(COMPONENTS)])]
+        for c in range(COMPONENTS):
+            out_ref[0, c, at, :] = border_terms(near, forward, 0, c)
+
+
+def outer_kernel(last, x_ref, *outs):
     base, step, forward = toward(lax.axis_index("ax"), last)
-    halo_terms(x_ref, base, step, forward, chunks, outs)
+    for r in range(0, x_ref.shape[2], TILE):
+        at = slice(r, r + TILE)
+        near = [
+            axial_flux([x_ref[base + step * h, c, at, :] for c in range(COMPONENTS)]) for h in range(REACH)
+        ]
+        for (first, count), out in zip(SENDS[1:], outs):
+            for n in range(count):
+                for c in range(COMPONENTS):
+                    out[n, c, at, :] = border_terms(near, forward, first + n, c)
 
 
 def inner_kernel(x_ref, t_ref, pack_ref):
@@ -100,21 +129,21 @@
     halo_terms(x_ref, base, step, forward, [(0, stations)], [t_ref])
     groups = rows // TILE
     lane = lax.broadcasted_iota(jnp.int32, (TILE, LANES), 1)
+    span = pack_ref.shape[0] // COMPONENTS
     for c in range(COMPONENTS):
         edge = jnp.zeros((TILE, LANES), jnp.float32)
         for s in range(stations):
-            pack_ref[c, s * REACH : (s + 1) * REACH, :] = x_ref[s, c, 0:REACH, :]
+            pack_ref[c * span + s * REACH : c * span + (s + 1) * REACH, :] = x_ref[s, c, 0:REACH, :]
             for g in range(groups):
                 place = (s * groups + g) * 2 * REACH
                 first = x_ref[s, c, g * TILE : (g + 1) * TILE, 0:LANES]
                 final = x_ref[s, c, g * TILE : (g + 1) * TILE, width - LANES : width]
                 both = pltpu.roll(jnp.where(lane < REACH, first, final), (place + REACH) % LANES, 1)
                 edge = jnp.where((lane >= place) & (lane < place + 2 * REACH), both, edge)
-        pack_ref[c, stations * REACH : stations * REACH + TILE, 0:LANES] = edge
-        if width > LANES:
-            pack_ref[c, stations * REACH : stations * REACH + TILE, LANES:width] = jnp.zeros(
-                (TILE, width - LANES), jnp.float32
-            )
+        height = TILE * LANES // width
+        start = (c + 1) * span - height
+        for i in range(width // LANES):
+            pack_ref[start : start + height, i * LANES : (i + 1) * LANES] = edge[i * height : (i + 1) * height]
 
 
 def base_kernel(
@@ -125,7 +154,16 @@
     points = int(round(turn))
     groups = rows // TILE
     lane = lax.broadcasted_iota(jnp.int32, (TILE, LANES), 1)
-    edge_rows = pl.ds(stations * REACH, TILE)
+    span = own_ref.shape[0] // COMPONENTS
+    height = TILE * LANES // width
+
+    def edge_of(ref, c):
+        start = (c + 1) * span - height
+        parts = [
+            ref[start : start + height, i * LANES : (i + 1) * LANES] for i in range(width // LANES)
+        ]
+        return parts[0] if len(parts) == 1 else jnp.concatenate(parts, axis=0)
+
     per_angle = turn / (2.0 * math.pi)
 
     slot = lane % (2 * REACH)
@@ -135,10 +173,10 @@
         _, _, vel, p = primitives(s)
         return flux(s, vel, p, 3)
 
-    own = edge_flux([own_ref[c, edge_rows, 0:LANES] for c in range(COMPONENTS)])
+    own = edge_flux([edge_of(own_ref, c) for c in range(COMPONENTS)])
     other = edge_flux(
         [
-            jnp.where(from_left, left_ref[c, edge_rows, 0:LANES], right_ref[c, edge_rows, 0:LANES])
+            jnp.where(from_left, edge_of(left_ref, c), edge_of(right_ref, c))
             for c in range(COMPONENTS)
         ]
     )
@@ -157,7 +195,7 @@
         fixes.append(fix)
 
     for s in range(stations):
-        cross = [across_ref[c, s * REACH : (s + 1) * REACH, :] for c in range(COMPONENTS)]
+        cross = [across_ref[c * span + s * REACH : c * span + (s + 1) * REACH, :] for c in range(COMPONENTS)]
         _, vel, _, p = primitives(cross)
         far = flux(cross, vel, p, 2)
         for c in range(COMPONENTS):
@@ -246,8 +284,9 @@
     end = (me == 0) | (me == last)
     inside = [(a, m) for a, m in SENDS if first <= a < first + count]
     for i, (a, m) in enumerate(inside):
-        terms = jnp.where(end, refs[2 * i][...], refs[2 * i + 1][...])
-        section_ref[a - first : a - first + m] = base_ref[a : a + m] + terms
+        for k in range(m):
+            terms = jnp.where(end, refs[2 * i][k], refs[2 * i + 1][k])
+            section_ref[a - first + k] = base_ref[place_of(a + k)] + terms
     coeff_ref[...] = close_dot(section_ref[...].reshape(-1, width), basis_ref[0], basis_ref[1])
 
 
@@ -268,7 +307,8 @@
         done, (out_ref, target, sem) = refs[:LAST], refs[LAST:]
         for i, ref in enumerate(done):
             a, m = GROUPS[i]
-            copies.append(pltpu.make_async_copy(ref, out_ref.at[a : a + m], sem.at[i]))
+            for k in range(m):
+                copies.append(pltpu.make_async_copy(ref.at[k], out_ref.at[place_of(a + k)], sem.at[a + k]))
         for copy in copies:
             copy.start()
     else:
@@ -277,12 +317,15 @@
     for s in range(count):
         part = slice(s * lines, (s + 1) * lines)
         total = mine_ref[part, :] + other_ref[part, :]
-        parts = smooth(total, section_ref[s], weight_ref[...], unbasis_ref[...], inside_ref[first + s])
+        parts = smooth(total, section_ref[s], weight_ref[...], unbasis_ref[...], inside_ref[place_of(first + s)])
         for i, value in enumerate(parts):
             target[s, :, :, i * LANES : (i + 1) * LANES] = value
     if n == LAST:
-        copies.append(pltpu.make_async_copy(target, out_ref.at[first : first + count], sem.at[LAST]))
-        copies[-1].start()
+        for s in range(count):
+            copies.append(
+                pltpu.make_async_copy(target.at[s], out_ref.at[place_of(first + s)], sem.at[first + s])
+            )
+            copies[-1].start()
         for copy in copies:
             copy.wait()
 
@@ -331,13 +374,19 @@
     pairs += [(j, i) for i, j in pairs]
     route = [(i * sectors + a, j * sectors + a) for i, j in pairs for a in range(sectors)]
     route += [(i * sectors + a, i * sectors + (a + 1) % sectors) for i in (0, line - 1) for a in range(sectors)]
-    terms = []
-    for chunks in (SENDS[:1], SENDS[1:]):
-        terms += call(
-            functools.partial(outer_kernel, line - 1, chunks),
-            tuple(struct(m, components, rows, width) for _, m in chunks), [conserved],
-        )
-    inner, pack = call(inner_kernel, (block, struct(components, stations * REACH + TILE, width)), [conserved])
+    sent = [struct(m, components, rows, width) for _, m in SENDS]
+    terms = [
+        pl.pallas_call(
+            functools.partial(first_kernel, line - 1), out_shape=sent[0],
+            in_specs=[pl.BlockSpec(memory_space=pltpu.HBM)], out_specs=VMEM,
+            scratch_shapes=[pltpu.VMEM(conserved.shape[1:], jnp.float32), pltpu.SemaphoreType.DMA],
+            compiler_params=params, name="first",
+        )(pltpu.with_memory_space_constraint(conserved, pltpu.HBM))
+    ]
+    terms += call(functools.partial(outer_kernel, line - 1), tuple(sent[1:]), [conserved])
+    inner, pack = call(
+        inner_kernel, (block, struct(components * (stations * REACH + TILE * LANES // width), width)), [conserved]
+    )
     across = turned(pack, sectors // 2)
     left, right = (across, across) if sectors == 2 else (turned(pack, 1), turned(pack, -1))
     arrived = []
@@ -374,7 +423,7 @@
             done.append(call(functools.partial(inverse_kernel, n), shapes[n], operands))
     return call(
         functools.partial(inverse_kernel, LAST), block, operands + done, out_specs=ANY,
-        scratch=[pltpu.VMEM(shapes[LAST].shape, jnp.float32), pltpu.SemaphoreType.DMA((len(GROUPS),))],
+        scratch=[pltpu.VMEM(shapes[LAST].shape, jnp.float32), pltpu.SemaphoreType.DMA((stations,))],
     )
 
 

time: 26.2 us -> 26.2 us (level)
  the two profiles are of different devices: /device:TPU:18 before, /device:TPU:2 now
where the time goes in v4:
time: 26.2 us; the launch traced here: 26 us
  waiting for transfers between devices  11.6 us (44%)
  starting transfers between devices  6.76 us (26%)
  Pallas kernels  6.45 us (25%)
  local copies, waits for them, and re-layouts  1.11 us (4%)
    ppermute x4, waiting for transfers between devices, per_device_inner(): arrived.append(lax.ppermute(value, ('ax', 'az'), route))  7.77 us
    pallas_call x9, Pallas kernels, call(): pl.pallas_call(kernel, out_shape=outs, in_specs=[VMEM] * (len(ins) - scal...  5.49 us
    ppermute x4, waiting for transfers between devices, turned(): lax.ppermute(value, 'az', [(i, (i + by) % sectors) for i in range(sectors)])  3.8 us
    ppermute x4, starting transfers between devices, turned(): lax.ppermute(value, 'az', [(i, (i + by) % sectors) for i in range(sectors)])  3.51 us
    ppermute x4, starting transfers between devices, per_device_inner(): arrived.append(lax.ppermute(value, ('ax', 'az'), route))  3.17 us
    unnamed x12, local copies, waits for them, and re-layouts  1.11 us
    pallas_call x1, Pallas kernels, per_device_inner(): pl.pallas_call(functools.partial(first_kernel, line - 1), out_shape=sent[...  0.96 us
  transfers between devices with their start and end apart: 9, of which 6 were waited for; matrix products, arithmetic and copies ran while one was open for 0% of the time, Pallas kernels for 20%

profile of v4, /device:TPU:2, one launch (start us, length us, event | category | flops | bytes accessed | tf_op | source)
XLA Modules:
  0.0 26.0 jit_solution(1930688666205226187)
XLA Ops:
  0.0 0.0 copy-start
  0.0 1.1 %copy-done = f32[4,5,32,256]{3,2,1,0:T(8,128)S(1)} copy-done((f32[4,5,32,256]{3,2,1,0:T(8,128)S(1)}, f32[4,5,32,256]{3,2,1,0:T(8,128)}, u32[]{:S(2)}) %copy-start) | copy-done | bytes 655384
  1.1 0.3 %shard_map.55 = (f32[4,5,32,256]{3,2,1,0:T(8,128)S(1)}, f32[100,256]{1,0:T(8,128)S(1)}) custom-call(f32[4,5,32,256]{3,2,1,0:T(8,128)S(1)} %copy-done), custom_call_target="tpu_custom_call" | custom-call | tf_op jit(solution)/shard_map/pallas_call | solution.py:362
  1.4 0.1 collective-permute-start
  1.5 0.0 copy-start.1
  1.5 1.6 %collective-permute-start.1 = (f32[100,256]{1,0:T(8,128)S(1)}, f32[100,256]{1,0:T(8,128)S(1)}, u32[]{:S(2)}, u32[]{:S(2)}) collective-permute-start(f32[100,256]{1,0:T(8,128)S(1)} %get-tuple-element.22.own_ref), channel_id=1, source_target_pairs={{0,1},{1,0},{2,3},{3,2},{4,5},{5,4},{6,7},{7,6},{8,9},{9,8},{10,11... | collective-permute-start | bytes 307208 | tf_op jit(solution)/shard_map/ppermute | solution.py:355
  3.1 0.2 shard_map.57
  3.3 0.0 copy-start.2
  3.3 0.0 copy-start.3
  3.3 0.3 %collective-permute-start.5 = (f32[1,5,32,256]{3,2,1,0:T(8,128)S(1)}, f32[1,5,32,256]{3,2,1,0:T(8,128)S(1)}, u32[]{:S(2)}, u32[]{:S(2)}) collective-permute-start(f32[1,5,32,256]{3,2,1,0:T(8,128)S(1)} %get-tuple-element.31.refs_2_), channel_id=1, source_target_pairs={{2,4},{3,5},{6,8},{7,9},{10,12},{11,13},{14,16},{15,17},{18,20},{1... | collective-permute-start | bytes 491528 | tf_op jit(solution)/shard_map/ppermute | solution.py:394
  3.6 1.0 %first.1.refs_0_ = f32[1,5,32,256]{3,2,1,0:T(8,128)S(1)} custom-call(f32[4,5,32,256]{3,2,1,0:T(8,128)} %x_ref.7), custom_call_target="tpu_custom_call" | custom-call | tf_op jit(solution)/shard_map/first/pallas_call | solution.py:379
  4.6 1.5 %collective-permute-start.4 = (f32[1,5,32,256]{3,2,1,0:T(8,128)S(1)}, f32[1,5,32,256]{3,2,1,0:T(8,128)S(1)}, u32[]{:S(2)}, u32[]{:S(2)}) collective-permute-start(f32[1,5,32,256]{3,2,1,0:T(8,128)S(1)} %first.1.refs_0_), channel_id=1, source_target_pairs={{2,4},{3,5},{6,8},{7,9},{10,12},{11,13},{14,16},{15,17},{18,20},{1... | collective-permute-start | bytes 491528 | tf_op jit(solution)/shard_map/ppermute | solution.py:394
  6.1 0.0 copy-start.4
  6.1 0.0 copy-start.5
  6.1 0.3 %collective-permute-start.7 = (f32[1,5,32,256]{3,2,1,0:T(8,128)S(1)}, f32[1,5,32,256]{3,2,1,0:T(8,128)S(1)}, u32[]{:S(2)}, u32[]{:S(2)}) collective-permute-start(f32[1,5,32,256]{3,2,1,0:T(8,128)S(1)} %get-tuple-element.34.refs_0_), channel_id=1, source_target_pairs={{2,4},{3,5},{6,8},{7,9},{10,12},{11,13},{14,16},{15,17},{18,20},{1... | collective-permute-start | bytes 491528 | tf_op jit(solution)/shard_map/ppermute | solution.py:394
  6.4 0.4 %collective-permute-done.1.left_ref.right_ref.across_ref = f32[100,256]{1,0:T(8,128)S(1)} collective-permute-done((f32[100,256]{1,0:T(8,128)S(1)}, f32[100,256]{1,0:T(8,128)S(1)}, u32[]{:S(2)}, u32[]{:S(2)}) %collective-permute-start.1) | collective-permute-done | bytes 102432 | tf_op jit(solution)/shard_map/ppermute | solution.py:355
  6.9 1.0 %collective-permute-start.2 = (f32[1,5,32,256]{3,2,1,0:T(8,128)S(1)}, f32[1,5,32,256]{3,2,1,0:T(8,128)S(1)}, u32[]{:S(2)}, u32[]{:S(2)}) collective-permute-start(f32[1,5,32,256]{3,2,1,0:T(8,128)S(1)} %get-tuple-element.25.refs_0_), channel_id=1, source_target_pairs={{2,4},{3,5},{6,8},{7,9},{10,12},{11,13},{14,16},{15,17},{18,20},{1... | collective-permute-start | bytes 491528 | tf_op jit(solution)/shard_map/ppermute | solution.py:394
  7.9 0.0 collective-permute-done.inner_ref
  7.9 0.0 copy-done.1
  7.9 0.0 copy-done.2
  7.9 0.0 copy-done.3
  7.9 0.0 copy-done.4
  7.9 0.0 copy-done.5
  7.9 2.8 %shard_map.56 = (f32[4,5,32,256]{3,2,1,0:T(8,128)S(1)}, f32[32,128]{1,0:T(8,128)S(1)}, f32[4,32,128]{2,1,0:T(8,128)S(1)}, bf16[2,256,128]{2,1,0:T(8,128)(2,1)S(1)}, bf16[2,128,256]{2,1,0:T(8,128)(2,1)S(1)}) custom-call(f32[4,5,32,256]{3,2,1,0:T(8,128)S(1)} %copy-done.1, f32[4,5,32,256]{3,2,1,0:T(8,128)S(1)} %collective-permute-done.inner_ref, ...), custom_call_target="tpu_custom_call" | custom-call | tf_op jit(solution)/shard_map/pallas_call | solution.py:362
  10.8 0.0 collective-permute-done.5.refs_3_
  10.8 6.1 %collective-permute-done.4.refs_1_ = f32[1,5,32,256]{3,2,1,0:T(8,128)S(1)} collective-permute-done((f32[1,5,32,256]{3,2,1,0:T(8,128)S(1)}, f32[1,5,32,256]{3,2,1,0:T(8,128)S(1)}, u32[]{:S(2)}, u32[]{:S(2)}) %collective-permute-start.4) | collective-permute-done | bytes 163872 | tf_op jit(solution)/shard_map/ppermute | solution.py:394
  16.9 0.3 %shard_map.59 = (f32[2,5,32,256]{3,2,1,0:T(8,128)S(1)}, f32[320,128]{1,0:T(8,128)S(1)}) custom-call(f32[4,5,32,256]{3,2,1,0:T(8,128)S(1)} %get-tuple-element.23.base_ref, bf16[2,256,128]{2,1,0:T(8,128)(2,1)S(1)} %get-tuple-element.24.basis_ref, f32[1,5,32,256]{3,2,1,0:T(8,128)S(1)} %first.1.refs_0_, f32[1,5,32,256]{3,2,1,0:T(8,128)S(1)} %collective-permute-done.4.refs_1_, ...), custom_call_target="tpu_custom_call" | custom-call | tf_op jit(solution)/shard_map/pallas_call | solution.py:362
  17.2 0.6 %collective-permute-start.6 = (f32[320,128]{1,0:T(8,128)S(1)}, f32[320,128]{1,0:T(8,128)S(1)}, u32[]{:S(2)}, u32[]{:S(2)}) collective-permute-start(f32[320,128]{1,0:T(8,128)S(1)} %get-tuple-element.33.mine_ref), channel_id=1, source_target_pairs={{0,1},{1,0},{2,3},{3,2},{4,5},{5,4},{6,7},{7,6},{8,9},{9,8},{10,11... | collective-permute-start | bytes 491528 | tf_op jit(solution)/shard_map/ppermute | solution.py:355
  17.7 0.9 %collective-permute-done.7.refs_1_ = f32[1,5,32,256]{3,2,1,0:T(8,128)S(1)} collective-permute-done((f32[1,5,32,256]{3,2,1,0:T(8,128)S(1)}, f32[1,5,32,256]{3,2,1,0:T(8,128)S(1)}, u32[]{:S(2)}, u32[]{:S(2)}) %collective-permute-start.7) | collective-permute-done | bytes 163872 | tf_op jit(solution)/shard_map/ppermute | solution.py:394
  18.6 0.2 shard_map.61
  18.9 0.7 %collective-permute-start.8 = (f32[160,128]{1,0:T(8,128)S(1)}, f32[160,128]{1,0:T(8,128)S(1)}, u32[]{:S(2)}, u32[]{:S(2)}) collective-permute-start(f32[160,128]{1,0:T(8,128)S(1)} %get-tuple-element.36.mine_ref), channel_id=1, source_target_pairs={{0,1},{1,0},{2,3},{3,2},{4,5},{5,4},{6,7},{7,6},{8,9},{9,8},{10,11... | collective-permute-start | bytes 245768 | tf_op jit(solution)/shard_map/ppermute | solution.py:355
  19.6 0.8 %collective-permute-done.2.refs_1_ = f32[1,5,32,256]{3,2,1,0:T(8,128)S(1)} collective-permute-done((f32[1,5,32,256]{3,2,1,0:T(8,128)S(1)}, f32[1,5,32,256]{3,2,1,0:T(8,128)S(1)}, u32[]{:S(2)}, u32[]{:S(2)}) %collective-permute-start.2) | collective-permute-done | bytes 163872 | tf_op jit(solution)/shard_map/ppermute | solution.py:394
  20.4 0.2 shard_map.58
  20.6 0.6 %collective-permute-start.3 = (f32[160,128]{1,0:T(8,128)S(1)}, f32[160,128]{1,0:T(8,128)S(1)}, u32[]{:S(2)}, u32[]{:S(2)}) collective-permute-start(f32[160,128]{1,0:T(8,128)S(1)} %get-tuple-element.27.mine_ref), channel_id=1, source_target_pairs={{0,1},{1,0},{2,3},{3,2},{4,5},{5,4},{6,7},{7,6},{8,9},{9,8},{10,11... | collective-permute-start | bytes 245768 | tf_op jit(solution)/shard_map/ppermute | solution.py:355
  21.2 2.2 %collective-permute-done.8.other_ref = f32[160,128]{1,0:T(8,128)S(1)} collective-permute-done((f32[160,128]{1,0:T(8,128)S(1)}, f32[160,128]{1,0:T(8,128)S(1)}, u32[]{:S(2)}, u32[]{:S(2)}) %collective-permute-start.8) | collective-permute-done | bytes 81952 | tf_op jit(solution)/shard_map/ppermute | solution.py:355
  23.4 0.2 shard_map.62.refs_1_
  23.7 0.0 collective-permute-done.6.other_ref
  23.7 0.3 %shard_map.60.refs_0_ = f32[2,5,32,256]{3,2,1,0:T(8,128)S(1)} custom-call(f32[2,5,32,256]{3,2,1,0:T(8,128)S(1)} %get-tuple-element.32.section_ref, f32[320,128]{1,0:T(8,128)S(1)} %get-tuple-element.33.mine_ref, f32[320,128]{1,0:T(8,128)S(1)} %collective-permute-done.6.other_ref, f32[32,128]{1,0:T(8,128)S(1)} %get-tuple-element.28.weight_ref, ...), custom_call_target="tpu_custom_call" | custom-call | tf_op jit(solution)/shard_map/pallas_call | solution.py:362
  24.0 1.2 %collective-permute-done.3.other_ref = f32[160,128]{1,0:T(8,128)S(1)} collective-permute-done((f32[160,128]{1,0:T(8,128)S(1)}, f32[160,128]{1,0:T(8,128)S(1)}, u32[]{:S(2)}, u32[]{:S(2)}) %collective-permute-start.3) | collective-permute-done | bytes 81952 | tf_op jit(solution)/shard_map/ppermute | solution.py:355
  25.1 0.9 %shard_map.63 = f32[4,5,32,256]{3,2,1,0:T(8,128)} custom-call(f32[1,5,32,256]{3,2,1,0:T(8,128)S(1)} %get-tuple-element.26.section_ref, f32[160,128]{1,0:T(8,128)S(1)} %get-tuple-element.27.mine_ref, f32[160,128]{1,0:T(8,128)S(1)} %collective-permute-done.3.other_ref, f32[32,128]{1,0:T(8,128)S(1)} %get-tuple-element.28.weight_ref, ...), custom_call_target="tpu_custom_call" | custom-call | tf_op jit(solution)/shard_map/pallas_call | solution.py:362
Async XLA Ops:
  0.0 1.1 %copy-start = (f32[4,5,32,256]{3,2,1,0:T(8,128)S(1)}, f32[4,5,32,256]{3,2,1,0:T(8,128)}, u32[]{:S(2)}) copy-start(f32[4,5,32,256]{3,2,1,0:T(8,128)} %x_ref.7) | copy-start | bytes 1966084
  1.4 6.5 %collective-permute-start = (f32[4,5,32,256]{3,2,1,0:T(8,128)S(1)}, f32[4,5,32,256]{3,2,1,0:T(8,128)S(1)}, u32[]{:S(2)}, u32[]{:S(2)}) collective-permute-start(f32[4,5,32,256]{3,2,1,0:T(8,128)S(1)} %get-tuple-element.21), channel_id=1, source_target_pairs={{0,2},{2,0},{4,6},{6,4},{8,10},{10,8},{12,14},{14,12},{16,18},{18,... | collective-permute-start | bytes 1966088 | tf_op jit(solution)/shard_map/ppermute | solution.py:395
  1.5 6.4 %copy-start.1 = (f32[4,5,32,256]{3,2,1,0:T(8,128)S(1)}, f32[4,5,32,256]{3,2,1,0:T(8,128)}, u32[]{:S(2)}) copy-start(f32[4,5,32,256]{3,2,1,0:T(8,128)} %x_ref.7) | copy-start | bytes 1966084
  1.5 5.4 %collective-permute-start.1 = (f32[100,256]{1,0:T(8,128)S(1)}, f32[100,256]{1,0:T(8,128)S(1)}, u32[]{:S(2)}, u32[]{:S(2)}) collective-permute-start(f32[100,256]{1,0:T(8,128)S(1)} %get-tuple-element.22.own_ref), channel_id=1, source_target_pairs={{0,1},{1,0},{2,3},{3,2},{4,5},{5,4},{6,7},{7,6},{8,9},{9,8},{10,11... | collective-permute-start | bytes 307208 | tf_op jit(solution)/shard_map/ppermute | solution.py:355
  3.3 4.6 %copy-start.2 = (f32[2,256,128]{2,1,0:T(8,128)S(1)}, f32[2,256,128]{2,1,0:T(8,128)}, u32[]{:S(2)}) copy-start(f32[2,256,128]{2,1,0:T(8,128)} %constant.4.clone.table_ref) | copy-start | bytes 786436
  3.3 4.6 %copy-start.3 = (f32[2,128,256]{2,1,0:T(8,128)S(1)}, f32[2,128,256]{2,1,0:T(8,128)}, u32[]{:S(2)}) copy-start(f32[2,128,256]{2,1,0:T(8,128)} %constant.5.clone.back_ref) | copy-start | bytes 786436
  3.3 7.5 %collective-permute-start.5 = (f32[1,5,32,256]{3,2,1,0:T(8,128)S(1)}, f32[1,5,32,256]{3,2,1,0:T(8,128)S(1)}, u32[]{:S(2)}, u32[]{:S(2)}) collective-permute-start(f32[1,5,32,256]{3,2,1,0:T(8,128)S(1)} %get-tuple-element.31.refs_2_), channel_id=1, source_target_pairs={{2,4},{3,5},{6,8},{7,9},{10,12},{11,13},{14,16},{15,17},{18,20},{1... | collective-permute-start | bytes 491528 | tf_op jit(solution)/shard_map/ppermute | solution.py:394
  4.6 12.3 %collective-permute-start.4 = (f32[1,5,32,256]{3,2,1,0:T(8,128)S(1)}, f32[1,5,32,256]{3,2,1,0:T(8,128)S(1)}, u32[]{:S(2)}, u32[]{:S(2)}) collective-permute-start(f32[1,5,32,256]{3,2,1,0:T(8,128)S(1)} %first.1.refs_0_), channel_id=1, source_target_pairs={{2,4},{3,5},{6,8},{7,9},{10,12},{11,13},{14,16},{15,17},{18,20},{1... | collective-permute-start | bytes 491528 | tf_op jit(solution)/shard_map/ppermute | solution.py:394
  6.1 1.8 %copy-start.4 = (s32[32]{0:T(128)S(1)}, s32[32]{0:T(128)}, u32[]{:S(2)}) copy-start(s32[32]{0:T(128)} %modes_ref.1) | copy-start | bytes 388
  6.1 1.8 %copy-start.5 = (s32[4]{0:T(128)S(1)}, s32[4]{0:T(128)}, u32[]{:S(2)}) copy-start(s32[4]{0:T(128)} %limit_ref.1) | copy-start | bytes 52
  6.1 12.5 %collective-permute-start.7 = (f32[1,5,32,256]{3,2,1,0:T(8,128)S(1)}, f32[1,5,32,256]{3,2,1,0:T(8,128)S(1)}, u32[]{:S(2)}, u32[]{:S(2)}) collective-permute-start(f32[1,5,32,256]{3,2,1,0:T(8,128)S(1)} %get-tuple-element.34.refs_0_), channel_id=1, source_target_pairs={{2,4},{3,5},{6,8},{7,9},{10,12},{11,13},{14,16},{15,17},{18,20},{1... | collective-permute-start | bytes 491528 | tf_op jit(solution)/shard_map/ppermute | solution.py:394
  6.9 13.5 %collective-permute-start.2 = (f32[1,5,32,256]{3,2,1,0:T(8,128)S(1)}, f32[1,5,32,256]{3,2,1,0:T(8,128)S(1)}, u32[]{:S(2)}, u32[]{:S(2)}) collective-permute-start(f32[1,5,32,256]{3,2,1,0:T(8,128)S(1)} %get-tuple-element.25.refs_0_), channel_id=1, source_target_pairs={{2,4},{3,5},{6,8},{7,9},{10,12},{11,13},{14,16},{15,17},{18,20},{1... | collective-permute-start | bytes 491528 | tf_op jit(solution)/shard_map/ppermute | solution.py:394
  17.2 6.5 %collective-permute-start.6 = (f32[320,128]{1,0:T(8,128)S(1)}, f32[320,128]{1,0:T(8,128)S(1)}, u32[]{:S(2)}, u32[]{:S(2)}) collective-permute-start(f32[320,128]{1,0:T(8,128)S(1)} %get-tuple-element.33.mine_ref), channel_id=1, source_target_pairs={{0,1},{1,0},{2,3},{3,2},{4,5},{5,4},{6,7},{7,6},{8,9},{9,8},{10,11... | collective-permute-start | bytes 491528 | tf_op jit(solution)/shard_map/ppermute | solution.py:355
  18.9 4.6 %collective-permute-start.8 = (f32[160,128]{1,0:T(8,128)S(1)}, f32[160,128]{1,0:T(8,128)S(1)}, u32[]{:S(2)}, u32[]{:S(2)}) collective-permute-start(f32[160,128]{1,0:T(8,128)S(1)} %get-tuple-element.36.mine_ref), channel_id=1, source_target_pairs={{0,1},{1,0},{2,3},{3,2},{4,5},{5,4},{6,7},{7,6},{8,9},{9,8},{10,11... | collective-permute-start | bytes 245768 | tf_op jit(solution)/shard_map/ppermute | solution.py:355
  20.6 4.5 %collective-permute-start.3 = (f32[160,128]{1,0:T(8,128)S(1)}, f32[160,128]{1,0:T(8,128)S(1)}, u32[]{:S(2)}, u32[]{:S(2)}) collective-permute-start(f32[160,128]{1,0:T(8,128)S(1)} %get-tuple-element.27.mine_ref), channel_id=1, source_target_pairs={{0,1},{1,0},{2,3},{3,2},{4,5},{5,4},{6,7},{7,6},{8,9},{9,8},{10,11... | collective-permute-start | bytes 245768 | tf_op jit(solution)/shard_map/ppermute | solution.py:355

commit v5 on v4

--- a/solution.py
+++ b/solution.py
@@ -20,7 +20,7 @@
 LANES = 128
 SENDS = ((0, 1), (1, 1), (2, 1), (3, 1))
 GROUPS = ((0, 2), (2, 1), (3, 1))
-LAST = len(GROUPS) - 1
+PIECES = ((0, 2), (2, 4), (4, 5))
 
 VMEM = pl.BlockSpec(memory_space=pltpu.VMEM)
 SMEM = pl.BlockSpec(memory_space=pltpu.SMEM)
@@ -34,11 +34,10 @@
 
 
 def close_dot(a, high, low):
-    def dot(p, q):
-        return lax.dot_general(p, q, (((1,), (0,)), ((), ())), preferred_element_type=jnp.float32)
-
     top, rest = halves(a)
-    return dot(top, high) + (dot(top, low) + dot(rest, high))
+    left = jnp.concatenate([top, top, rest], axis=1)
+    right = jnp.concatenate([high, low, high], axis=0)
+    return lax.dot_general(left, right, (((1,), (0,)), ((), ())), preferred_element_type=jnp.float32)
 
 
 def primitives(s):
@@ -290,44 +289,31 @@
     coeff_ref[...] = close_dot(section_ref[...].reshape(-1, width), basis_ref[0], basis_ref[1])
 
 
-def smooth(total, section, weight, unbasis, inside):
-    _, rows, width = section.shape
-    kept = (total.reshape(COMPONENTS, rows, -1) * weight[None]).reshape(COMPONENTS * rows, -1)
-    value = close_dot(kept, unbasis[0], unbasis[1]).reshape(section.shape)
-    pick = (inside > 0.5)[None]
-    return [
-        jnp.where(pick, value[:, :, t : t + LANES], section[:, :, t : t + LANES]) for t in range(0, width, LANES)
-    ]
-
-
 def inverse_kernel(n, section_ref, mine_ref, other_ref, weight_ref, unbasis_ref, inside_ref, *refs):
     first, count = GROUPS[n]
+    out_ref, target, sem = refs[-3:]
+    rows, width = section_ref.shape[2:]
+    lines = COMPONENTS * rows
     copies = []
-    if n == LAST:
-        done, (out_ref, target, sem) = refs[:LAST], refs[LAST:]
-        for i, ref in enumerate(done):
-            a, m = GROUPS[i]
-            for k in range(m):
-                copies.append(pltpu.make_async_copy(ref.at[k], out_ref.at[place_of(a + k)], sem.at[a + k]))
-        for copy in copies:
-            copy.start()
-    else:
-        (target,) = refs
-    lines = COMPONENTS * section_ref.shape[2]
     for s in range(count):
-        part = slice(s * lines, (s + 1) * lines)
-        total = mine_ref[part, :] + other_ref[part, :]
-        parts = smooth(total, section_ref[s], weight_ref[...], unbasis_ref[...], inside_ref[place_of(first + s)])
-        for i, value in enumerate(parts):
-            target[s, :, :, i * LANES : (i + 1) * LANES] = value
-    if n == LAST:
-        for s in range(count):
+        here = place_of(first + s)
+        inside = (inside_ref[here] > 0.5)[None]
+        for low, high in PIECES:
+            part = slice(s * lines + low * rows, s * lines + high * rows)
+            total = (mine_ref[part, :] + other_ref[part, :]).reshape(high - low, rows, -1)
+            kept = (total * weight_ref[...][None]).reshape((high - low) * rows, -1)
+            value = close_dot(kept, unbasis_ref[0], unbasis_ref[1]).reshape(high - low, rows, width)
+            for t in range(0, width, LANES):
+                at = slice(t, t + LANES)
+                target[s, low:high, :, at] = jnp.where(inside, value[:, :, at], section_ref[s, low:high, :, at])
             copies.append(
-                pltpu.make_async_copy(target.at[s], out_ref.at[place_of(first + s)], sem.at[first + s])
+                pltpu.make_async_copy(
+                    target.at[s, low:high], out_ref.at[here, low:high], sem.at[len(copies)]
+                )
             )
             copies[-1].start()
-        for copy in copies:
-            copy.wait()
+    for copy in copies:
+        copy.wait()
 
 
 def fourier_tables(sectors, width):
@@ -419,12 +405,15 @@
         )
         other = others(mine)
         operands = [section, mine, other, weight, unbasis, inside]
-        if n < LAST:
-            done.append(call(functools.partial(inverse_kernel, n), shapes[n], operands))
-    return call(
-        functools.partial(inverse_kernel, LAST), block, operands + done, out_specs=ANY,
-        scratch=[pltpu.VMEM(shapes[LAST].shape, jnp.float32), pltpu.SemaphoreType.DMA((stations,))],
-    )
+        out = pl.pallas_call(
+            functools.partial(inverse_kernel, n), out_shape=block,
+            in_specs=[VMEM] * len(operands) + [ANY] * len(done), out_specs=ANY,
+            scratch_shapes=[pltpu.VMEM(shapes[n].shape, jnp.float32), pltpu.SemaphoreType.DMA((count * len(PIECES),))],
+            input_output_aliases={len(operands): 0} if done else {},
+            compiler_params=params,
+        )(*operands, *done)
+        done = [out]
+    return done[0]
 
 
 def solution(mesh):

time: 26.2 us -> 26.1 us (level)
  waiting for transfers between devices: 11.6 us -> 10.2 us
  Pallas kernels: 6.45 us -> 7.76 us
    pallas_call x0 -> x3, Pallas kernels: none -> 2.75 us  [per_device_inner(): pl.pallas_call(functools.partial(inverse_kernel, n), out_shape=block, in_...]
    pallas_call x9 -> x6, Pallas kernels: 5.49 us -> 4.05 us  [call(): pl.pallas_call(kernel, out_shape=outs, in_specs=[VMEM] * (len(ins) - scal...]
    ppermute x4, waiting for transfers between devices: 3.8 us -> 2.42 us  [turned(): lax.ppermute(value, 'az', [(i, (i + by) % sectors) for i in range(sectors)])]
  transfers between devices with their start and end apart: 9 -> 9, of which waited for: 6 -> 6; matrix products, arithmetic and copies ran while one was open for 0% -> 0% of each run, Pallas kernels for 20% -> 25%
where the time goes in v5:
time: 26.1 us; the launch traced here: 26 us
  waiting for transfers between devices  10.2 us (39%)
  Pallas kernels  7.76 us (30%)
  starting transfers between devices  6.75 us (26%)
  local copies, waits for them, and re-layouts  1.11 us (4%)
    ppermute x4, waiting for transfers between devices, per_device_inner(): arrived.append(lax.ppermute(value, ('ax', 'az'), route))  7.79 us
    pallas_call x6, Pallas kernels, call(): pl.pallas_call(kernel, out_shape=outs, in_specs=[VMEM] * (len(ins) - scal...  4.05 us
    ppermute x4, starting transfers between devices, turned(): lax.ppermute(value, 'az', [(i, (i + by) % sectors) for i in range(sectors)])  3.5 us
    ppermute x4, starting transfers between devices, per_device_inner(): arrived.append(lax.ppermute(value, ('ax', 'az'), route))  3.17 us
    pallas_call x3, Pallas kernels, per_device_inner(): pl.pallas_call(functools.partial(inverse_kernel, n), out_shape=block, in_...  2.75 us
    ppermute x4, waiting for transfers between devices, turned(): lax.ppermute(value, 'az', [(i, (i + by) % sectors) for i in range(sectors)])  2.42 us
    unnamed x12, local copies, waits for them, and re-layouts  1.11 us
    pallas_call x1, Pallas kernels, per_device_inner(): pl.pallas_call(functools.partial(first_kernel, line - 1), out_shape=sent[...  0.96 us
  transfers between devices with their start and end apart: 9, of which 6 were waited for; matrix products, arithmetic and copies ran while one was open for 0% of the time, Pallas kernels for 25%

profile of v5, /device:TPU:2, one launch (start us, length us, event | category | flops | bytes accessed | tf_op | source)
XLA Modules:
  0.0 26.0 jit_solution(14608380628679162277)
XLA Ops:
  0.0 0.0 copy-start
  0.0 1.1 %copy-done = f32[4,5,32,256]{3,2,1,0:T(8,128)S(1)} copy-done((f32[4,5,32,256]{3,2,1,0:T(8,128)S(1)}, f32[4,5,32,256]{3,2,1,0:T(8,128)}, u32[]{:S(2)}) %copy-start) | copy-done | bytes 655384
  1.1 0.3 %shard_map.55 = (f32[4,5,32,256]{3,2,1,0:T(8,128)S(1)}, f32[100,256]{1,0:T(8,128)S(1)}) custom-call(f32[4,5,32,256]{3,2,1,0:T(8,128)S(1)} %copy-done), custom_call_target="tpu_custom_call" | custom-call | tf_op jit(solution)/shard_map/pallas_call | solution.py:348
  1.4 0.1 collective-permute-start
  1.5 0.0 copy-start.1
  1.5 1.6 %collective-permute-start.1 = (f32[100,256]{1,0:T(8,128)S(1)}, f32[100,256]{1,0:T(8,128)S(1)}, u32[]{:S(2)}, u32[]{:S(2)}) collective-permute-start(f32[100,256]{1,0:T(8,128)S(1)} %get-tuple-element.22.own_ref), channel_id=1, source_target_pairs={{0,1},{1,0},{2,3},{3,2},{4,5},{5,4},{6,7},{7,6},{8,9},{9,8},{10,11... | collective-permute-start | bytes 307208 | tf_op jit(solution)/shard_map/ppermute | solution.py:341
  3.1 0.2 shard_map.57
  3.3 0.0 copy-start.2
  3.3 0.0 copy-start.3
  3.3 0.3 %collective-permute-start.7 = (f32[1,5,32,256]{3,2,1,0:T(8,128)S(1)}, f32[1,5,32,256]{3,2,1,0:T(8,128)S(1)}, u32[]{:S(2)}, u32[]{:S(2)}) collective-permute-start(f32[1,5,32,256]{3,2,1,0:T(8,128)S(1)} %get-tuple-element.34.refs_2_), channel_id=1, source_target_pairs={{2,4},{3,5},{6,8},{7,9},{10,12},{11,13},{14,16},{15,17},{18,20},{1... | collective-permute-start | bytes 491528 | tf_op jit(solution)/shard_map/ppermute | solution.py:380
  3.6 1.0 %first.1.refs_0_ = f32[1,5,32,256]{3,2,1,0:T(8,128)S(1)} custom-call(f32[4,5,32,256]{3,2,1,0:T(8,128)} %x_ref.7), custom_call_target="tpu_custom_call" | custom-call | tf_op jit(solution)/shard_map/first/pallas_call | solution.py:365
  4.6 1.5 %collective-permute-start.6 = (f32[1,5,32,256]{3,2,1,0:T(8,128)S(1)}, f32[1,5,32,256]{3,2,1,0:T(8,128)S(1)}, u32[]{:S(2)}, u32[]{:S(2)}) collective-permute-start(f32[1,5,32,256]{3,2,1,0:T(8,128)S(1)} %first.1.refs_0_), channel_id=1, source_target_pairs={{2,4},{3,5},{6,8},{7,9},{10,12},{11,13},{14,16},{15,17},{18,20},{1... | collective-permute-start | bytes 491528 | tf_op jit(solution)/shard_map/ppermute | solution.py:380
  6.1 0.0 copy-start.4
  6.1 0.0 copy-start.5
  6.1 0.3 %collective-permute-start.4 = (f32[1,5,32,256]{3,2,1,0:T(8,128)S(1)}, f32[1,5,32,256]{3,2,1,0:T(8,128)S(1)}, u32[]{:S(2)}, u32[]{:S(2)}) collective-permute-start(f32[1,5,32,256]{3,2,1,0:T(8,128)S(1)} %get-tuple-element.31.refs_0_), channel_id=1, source_target_pairs={{2,4},{3,5},{6,8},{7,9},{10,12},{11,13},{14,16},{15,17},{18,20},{1... | collective-permute-start | bytes 491528 | tf_op jit(solution)/shard_map/ppermute | solution.py:380
  6.4 0.4 %collective-permute-done.1.left_ref.right_ref.across_ref = f32[100,256]{1,0:T(8,128)S(1)} collective-permute-done((f32[100,256]{1,0:T(8,128)S(1)}, f32[100,256]{1,0:T(8,128)S(1)}, u32[]{:S(2)}, u32[]{:S(2)}) %collective-permute-start.1) | collective-permute-done | bytes 102432 | tf_op jit(solution)/shard_map/ppermute | solution.py:341
  6.9 1.0 %collective-permute-start.2 = (f32[1,5,32,256]{3,2,1,0:T(8,128)S(1)}, f32[1,5,32,256]{3,2,1,0:T(8,128)S(1)}, u32[]{:S(2)}, u32[]{:S(2)}) collective-permute-start(f32[1,5,32,256]{3,2,1,0:T(8,128)S(1)} %get-tuple-element.25.refs_0_), channel_id=1, source_target_pairs={{2,4},{3,5},{6,8},{7,9},{10,12},{11,13},{14,16},{15,17},{18,20},{1... | collective-permute-start | bytes 491528 | tf_op jit(solution)/shard_map/ppermute | solution.py:380
  7.9 0.0 collective-permute-done.inner_ref
  7.9 0.0 copy-done.1
  7.9 0.0 copy-done.2
  7.9 0.0 copy-done.3
  7.9 0.0 copy-done.4
  7.9 0.0 copy-done.5
  7.9 2.8 %shard_map.56 = (f32[4,5,32,256]{3,2,1,0:T(8,128)S(1)}, f32[32,128]{1,0:T(8,128)S(1)}, f32[4,32,128]{2,1,0:T(8,128)S(1)}, bf16[2,256,128]{2,1,0:T(8,128)(2,1)S(1)}, bf16[2,128,256]{2,1,0:T(8,128)(2,1)S(1)}) custom-call(f32[4,5,32,256]{3,2,1,0:T(8,128)S(1)} %copy-done.1, f32[4,5,32,256]{3,2,1,0:T(8,128)S(1)} %collective-permute-done.inner_ref, ...), custom_call_target="tpu_custom_call" | custom-call | tf_op jit(solution)/shard_map/pallas_call | solution.py:348
  10.8 0.0 collective-permute-done.7.refs_3_
  10.8 6.1 %collective-permute-done.6.refs_1_ = f32[1,5,32,256]{3,2,1,0:T(8,128)S(1)} collective-permute-done((f32[1,5,32,256]{3,2,1,0:T(8,128)S(1)}, f32[1,5,32,256]{3,2,1,0:T(8,128)S(1)}, u32[]{:S(2)}, u32[]{:S(2)}) %collective-permute-start.6) | collective-permute-done | bytes 163872 | tf_op jit(solution)/shard_map/ppermute | solution.py:380
  16.9 0.3 %shard_map.60 = (f32[2,5,32,256]{3,2,1,0:T(8,128)S(1)}, f32[320,128]{1,0:T(8,128)S(1)}) custom-call(f32[4,5,32,256]{3,2,1,0:T(8,128)S(1)} %get-tuple-element.23.base_ref, bf16[2,256,128]{2,1,0:T(8,128)(2,1)S(1)} %get-tuple-element.24.basis_ref, f32[1,5,32,256]{3,2,1,0:T(8,128)S(1)} %first.1.refs_0_, f32[1,5,32,256]{3,2,1,0:T(8,128)S(1)} %collective-permute-done.6.refs_1_, ...), custom_call_target="tpu_custom_call" | custom-call | tf_op jit(solution)/shard_map/pallas_call | solution.py:348
  17.2 0.6 %collective-permute-start.8 = (f32[320,128]{1,0:T(8,128)S(1)}, f32[320,128]{1,0:T(8,128)S(1)}, u32[]{:S(2)}, u32[]{:S(2)}) collective-permute-start(f32[320,128]{1,0:T(8,128)S(1)} %get-tuple-element.36.mine_ref), channel_id=1, source_target_pairs={{0,1},{1,0},{2,3},{3,2},{4,5},{5,4},{6,7},{7,6},{8,9},{9,8},{10,11... | collective-permute-start | bytes 491528 | tf_op jit(solution)/shard_map/ppermute | solution.py:341
  17.7 0.9 %collective-permute-done.4.refs_1_ = f32[1,5,32,256]{3,2,1,0:T(8,128)S(1)} collective-permute-done((f32[1,5,32,256]{3,2,1,0:T(8,128)S(1)}, f32[1,5,32,256]{3,2,1,0:T(8,128)S(1)}, u32[]{:S(2)}, u32[]{:S(2)}) %collective-permute-start.4) | collective-permute-done | bytes 163872 | tf_op jit(solution)/shard_map/ppermute | solution.py:380
  18.6 0.2 shard_map.59
  18.8 0.7 %collective-permute-start.5 = (f32[160,128]{1,0:T(8,128)S(1)}, f32[160,128]{1,0:T(8,128)S(1)}, u32[]{:S(2)}, u32[]{:S(2)}) collective-permute-start(f32[160,128]{1,0:T(8,128)S(1)} %get-tuple-element.33.mine_ref), channel_id=1, source_target_pairs={{0,1},{1,0},{2,3},{3,2},{4,5},{5,4},{6,7},{7,6},{8,9},{9,8},{10,11... | collective-permute-start | bytes 245768 | tf_op jit(solution)/shard_map/ppermute | solution.py:341
  19.6 0.8 %collective-permute-done.2.refs_1_ = f32[1,5,32,256]{3,2,1,0:T(8,128)S(1)} collective-permute-done((f32[1,5,32,256]{3,2,1,0:T(8,128)S(1)}, f32[1,5,32,256]{3,2,1,0:T(8,128)S(1)}, u32[]{:S(2)}, u32[]{:S(2)}) %collective-permute-start.2) | collective-permute-done | bytes 163872 | tf_op jit(solution)/shard_map/ppermute | solution.py:380
  20.4 0.2 shard_map.58
  20.6 0.6 %collective-permute-start.3 = (f32[160,128]{1,0:T(8,128)S(1)}, f32[160,128]{1,0:T(8,128)S(1)}, u32[]{:S(2)}, u32[]{:S(2)}) collective-permute-start(f32[160,128]{1,0:T(8,128)S(1)} %get-tuple-element.27.mine_ref), channel_id=1, source_target_pairs={{0,1},{1,0},{2,3},{3,2},{4,5},{5,4},{6,7},{7,6},{8,9},{9,8},{10,11... | collective-permute-start | bytes 245768 | tf_op jit(solution)/shard_map/ppermute | solution.py:341
  21.2 1.3 %collective-permute-done.8.other_ref = f32[320,128]{1,0:T(8,128)S(1)} collective-permute-done((f32[320,128]{1,0:T(8,128)S(1)}, f32[320,128]{1,0:T(8,128)S(1)}, u32[]{:S(2)}, u32[]{:S(2)}) %collective-permute-start.8) | collective-permute-done | bytes 163872 | tf_op jit(solution)/shard_map/ppermute | solution.py:341
  22.6 1.0 %shard_map.61.refs_0_ = f32[4,5,32,256]{3,2,1,0:T(8,128)} custom-call(f32[2,5,32,256]{3,2,1,0:T(8,128)S(1)} %get-tuple-element.35.section_ref, f32[320,128]{1,0:T(8,128)S(1)} %get-tuple-element.36.mine_ref, f32[320,128]{1,0:T(8,128)S(1)} %collective-permute-done.8.other_ref, f32[32,128]{1,0:T(8,128)S(1)} %get-tuple-element.28.weight_ref, ...), custom_call_target="tpu_custom_call" | custom-call | tf_op jit(solution)/shard_map/pallas_call | solution.py:408
  23.6 0.0 collective-permute-done.5.other_ref
  23.6 0.9 %shard_map.62.refs_0_ = f32[4,5,32,256]{3,2,1,0:T(8,128)} custom-call(f32[1,5,32,256]{3,2,1,0:T(8,128)S(1)} %get-tuple-element.32.section_ref, f32[160,128]{1,0:T(8,128)S(1)} %get-tuple-element.33.mine_ref, f32[160,128]{1,0:T(8,128)S(1)} %collective-permute-done.5.other_ref, ...), custom_call_target="tpu_custom_call", output_to_operand_aliasing={{}: (6, {})} | custom-call | tf_op jit(solution)/shard_map/pallas_call | solution.py:408
  24.5 0.6 %collective-permute-done.3.other_ref = f32[160,128]{1,0:T(8,128)S(1)} collective-permute-done((f32[160,128]{1,0:T(8,128)S(1)}, f32[160,128]{1,0:T(8,128)S(1)}, u32[]{:S(2)}, u32[]{:S(2)}) %collective-permute-start.3) | collective-permute-done | bytes 81952 | tf_op jit(solution)/shard_map/ppermute | solution.py:341
  25.1 0.9 %shard_map.63 = f32[4,5,32,256]{3,2,1,0:T(8,128)} custom-call(f32[1,5,32,256]{3,2,1,0:T(8,128)S(1)} %get-tuple-element.26.section_ref, f32[160,128]{1,0:T(8,128)S(1)} %get-tuple-element.27.mine_ref, f32[160,128]{1,0:T(8,128)S(1)} %collective-permute-done.3.other_ref, f32[32,128]{1,0:T(8,128)S(1)} %get-tuple-element.28.weight_ref, ...), custom_call_target="tpu_custom_call", output_to_operand_aliasing={{}: (6, {})} | custom-call | tf_op jit(solution)/shard_map/pallas_call | solution.py:408
Async XLA Ops:
  0.0 1.1 %copy-start = (f32[4,5,32,256]{3,2,1,0:T(8,128)S(1)}, f32[4,5,32,256]{3,2,1,0:T(8,128)}, u32[]{:S(2)}) copy-start(f32[4,5,32,256]{3,2,1,0:T(8,128)} %x_ref.7) | copy-start | bytes 1966084
  1.4 6.5 %collective-permute-start = (f32[4,5,32,256]{3,2,1,0:T(8,128)S(1)}, f32[4,5,32,256]{3,2,1,0:T(8,128)S(1)}, u32[]{:S(2)}, u32[]{:S(2)}) collective-permute-start(f32[4,5,32,256]{3,2,1,0:T(8,128)S(1)} %get-tuple-element.21), channel_id=1, source_target_pairs={{0,2},{2,0},{4,6},{6,4},{8,10},{10,8},{12,14},{14,12},{16,18},{18,... | collective-permute-start | bytes 1966088 | tf_op jit(solution)/shard_map/ppermute | solution.py:381
  1.5 6.4 %copy-start.1 = (f32[4,5,32,256]{3,2,1,0:T(8,128)S(1)}, f32[4,5,32,256]{3,2,1,0:T(8,128)}, u32[]{:S(2)}) copy-start(f32[4,5,32,256]{3,2,1,0:T(8,128)} %x_ref.7) | copy-start | bytes 1966084
  1.5 5.4 %collective-permute-start.1 = (f32[100,256]{1,0:T(8,128)S(1)}, f32[100,256]{1,0:T(8,128)S(1)}, u32[]{:S(2)}, u32[]{:S(2)}) collective-permute-start(f32[100,256]{1,0:T(8,128)S(1)} %get-tuple-element.22.own_ref), channel_id=1, source_target_pairs={{0,1},{1,0},{2,3},{3,2},{4,5},{5,4},{6,7},{7,6},{8,9},{9,8},{10,11... | collective-permute-start | bytes 307208 | tf_op jit(solution)/shard_map/ppermute | solution.py:341
  3.3 4.6 %copy-start.2 = (f32[2,256,128]{2,1,0:T(8,128)S(1)}, f32[2,256,128]{2,1,0:T(8,128)}, u32[]{:S(2)}) copy-start(f32[2,256,128]{2,1,0:T(8,128)} %constant.4.clone.table_ref) | copy-start | bytes 786436
  3.3 4.6 %copy-start.3 = (f32[2,128,256]{2,1,0:T(8,128)S(1)}, f32[2,128,256]{2,1,0:T(8,128)}, u32[]{:S(2)}) copy-start(f32[2,128,256]{2,1,0:T(8,128)} %constant.5.clone.back_ref) | copy-start | bytes 786436
  3.3 7.5 %collective-permute-start.7 = (f32[1,5,32,256]{3,2,1,0:T(8,128)S(1)}, f32[1,5,32,256]{3,2,1,0:T(8,128)S(1)}, u32[]{:S(2)}, u32[]{:S(2)}) collective-permute-start(f32[1,5,32,256]{3,2,1,0:T(8,128)S(1)} %get-tuple-element.34.refs_2_), channel_id=1, source_target_pairs={{2,4},{3,5},{6,8},{7,9},{10,12},{11,13},{14,16},{15,17},{18,20},{1... | collective-permute-start | bytes 491528 | tf_op jit(solution)/shard_map/ppermute | solution.py:380
  4.6 12.3 %collective-permute-start.6 = (f32[1,5,32,256]{3,2,1,0:T(8,128)S(1)}, f32[1,5,32,256]{3,2,1,0:T(8,128)S(1)}, u32[]{:S(2)}, u32[]{:S(2)}) collective-permute-start(f32[1,5,32,256]{3,2,1,0:T(8,128)S(1)} %first.1.refs_0_), channel_id=1, source_target_pairs={{2,4},{3,5},{6,8},{7,9},{10,12},{11,13},{14,16},{15,17},{18,20},{1... | collective-permute-start | bytes 491528 | tf_op jit(solution)/shard_map/ppermute | solution.py:380
  6.1 1.8 %copy-start.4 = (s32[32]{0:T(128)S(1)}, s32[32]{0:T(128)}, u32[]{:S(2)}) copy-start(s32[32]{0:T(128)} %modes_ref.1) | copy-start | bytes 388
  6.1 1.8 %copy-start.5 = (s32[4]{0:T(128)S(1)}, s32[4]{0:T(128)}, u32[]{:S(2)}) copy-start(s32[4]{0:T(128)} %limit_ref.1) | copy-start | bytes 52
  6.1 12.5 %collective-permute-start.4 = (f32[1,5,32,256]{3,2,1,0:T(8,128)S(1)}, f32[1,5,32,256]{3,2,1,0:T(8,128)S(1)}, u32[]{:S(2)}, u32[]{:S(2)}) collective-permute-start(f32[1,5,32,256]{3,2,1,0:T(8,128)S(1)} %get-tuple-element.31.refs_0_), channel_id=1, source_target_pairs={{2,4},{3,5},{6,8},{7,9},{10,12},{11,13},{14,16},{15,17},{18,20},{1... | collective-permute-start | bytes 491528 | tf_op jit(solution)/shard_map/ppermute | solution.py:380
  6.9 13.5 %collective-permute-start.2 = (f32[1,5,32,256]{3,2,1,0:T(8,128)S(1)}, f32[1,5,32,256]{3,2,1,0:T(8,128)S(1)}, u32[]{:S(2)}, u32[]{:S(2)}) collective-permute-start(f32[1,5,32,256]{3,2,1,0:T(8,128)S(1)} %get-tuple-element.25.refs_0_), channel_id=1, source_target_pairs={{2,4},{3,5},{6,8},{7,9},{10,12},{11,13},{14,16},{15,17},{18,20},{1... | collective-permute-start | bytes 491528 | tf_op jit(solution)/shard_map/ppermute | solution.py:380
  17.2 5.4 %collective-permute-start.8 = (f32[320,128]{1,0:T(8,128)S(1)}, f32[320,128]{1,0:T(8,128)S(1)}, u32[]{:S(2)}, u32[]{:S(2)}) collective-permute-start(f32[320,128]{1,0:T(8,128)S(1)} %get-tuple-element.36.mine_ref), channel_id=1, source_target_pairs={{0,1},{1,0},{2,3},{3,2},{4,5},{5,4},{6,7},{7,6},{8,9},{9,8},{10,11... | collective-permute-start | bytes 491528 | tf_op jit(solution)/shard_map/ppermute | solution.py:341
  18.8 4.7 %collective-permute-start.5 = (f32[160,128]{1,0:T(8,128)S(1)}, f32[160,128]{1,0:T(8,128)S(1)}, u32[]{:S(2)}, u32[]{:S(2)}) collective-permute-start(f32[160,128]{1,0:T(8,128)S(1)} %get-tuple-element.33.mine_ref), channel_id=1, source_target_pairs={{0,1},{1,0},{2,3},{3,2},{4,5},{5,4},{6,7},{7,6},{8,9},{9,8},{10,11... | collective-permute-start | bytes 245768 | tf_op jit(solution)/shard_map/ppermute | solution.py:341
  20.6 4.5 %collective-permute-start.3 = (f32[160,128]{1,0:T(8,128)S(1)}, f32[160,128]{1,0:T(8,128)S(1)}, u32[]{:S(2)}, u32[]{:S(2)}) collective-permute-start(f32[160,128]{1,0:T(8,128)S(1)} %get-tuple-element.27.mine_ref), channel_id=1, source_target_pairs={{0,1},{1,0},{2,3},{3,2},{4,5},{5,4},{6,7},{7,6},{8,9},{9,8},{10,11... | collective-permute-start | bytes 245768 | tf_op jit(solution)/shard_map/ppermute | solution.py:341

commit v6 on v5

--- a/solution.py
+++ b/solution.py
@@ -97,10 +97,16 @@
 
 def first_kernel(last, x_ref, out_ref, buffer, sem):
     base, _, forward = toward(lax.axis_index("ax"), last)
-    copy = pltpu.make_async_copy(x_ref.at[base], buffer, sem)
-    copy.start()
-    copy.wait()
+    half = buffer.shape[1] // 2
+    copies = [
+        pltpu.make_async_copy(x_ref.at[base, :, pl.ds(i * half, half)], buffer.at[:, pl.ds(i * half, half)], sem.at[i])
+        for i in (0, 1)
+    ]
+    for copy in copies:
+        copy.start()
     for r in range(0, buffer.shape[1], TILE):
+        if r % half == 0:
+            copies[r // half].wait()
         at = slice(r, r + TILE)
         near = [axial_flux([buffer[c, at, :] for c in range(COMPONENTS)])]
         for c in range(COMPONENTS):
@@ -365,7 +371,7 @@
         pl.pallas_call(
             functools.partial(first_kernel, line - 1), out_shape=sent[0],
             in_specs=[pl.BlockSpec(memory_space=pltpu.HBM)], out_specs=VMEM,
-            scratch_shapes=[pltpu.VMEM(conserved.shape[1:], jnp.float32), pltpu.SemaphoreType.DMA],
+            scratch_shapes=[pltpu.VMEM(conserved.shape[1:], jnp.float32), pltpu.SemaphoreType.DMA((2,))],
             compiler_params=params, name="first",
         )(pltpu.with_memory_space_constraint(conserved, pltpu.HBM))
     ]

time: 26.1 us -> 26.1 us (level)
  no operation moved by 1% of the time
where the time goes in v6:
time: 26.1 us; the launch traced here: 26 us
  waiting for transfers between devices  10.2 us (39%)
  Pallas kernels  7.77 us (30%)
  starting transfers between devices  6.75 us (26%)
  local copies, waits for them, and re-layouts  1.11 us (4%)
    ppermute x4, waiting for transfers between devices, per_device_inner(): arrived.append(lax.ppermute(value, ('ax', 'az'), route))  7.78 us
    pallas_call x6, Pallas kernels, call(): pl.pallas_call(kernel, out_shape=outs, in_specs=[VMEM] * (len(ins) - scal...  4.05 us
    ppermute x4, starting transfers between devices, turned(): lax.ppermute(value, 'az', [(i, (i + by) % sectors) for i in range(sectors)])  3.5 us
    ppermute x4, starting transfers between devices, per_device_inner(): arrived.append(lax.ppermute(value, ('ax', 'az'), route))  3.18 us
    pallas_call x3, Pallas kernels, per_device_inner(): pl.pallas_call(functools.partial(inverse_kernel, n), out_shape=block, in_...  2.75 us
    ppermute x4, waiting for transfers between devices, turned(): lax.ppermute(value, 'az', [(i, (i + by) % sectors) for i in range(sectors)])  2.42 us
    unnamed x12, local copies, waits for them, and re-layouts  1.11 us
    pallas_call x1, Pallas kernels, per_device_inner(): pl.pallas_call(functools.partial(first_kernel, line - 1), out_shape=sent[...  0.96 us
  transfers between devices with their start and end apart: 9, of which 6 were waited for; matrix products, arithmetic and copies ran while one was open for 0% of the time, Pallas kernels for 25%

profile of v6, /device:TPU:2, one launch (start us, length us, event | category | flops | bytes accessed | tf_op | source)
XLA Modules:
  0.0 26.0 jit_solution(7333868261686003787)
XLA Ops:
  0.0 0.0 copy-start
  0.0 1.1 %copy-done = f32[4,5,32,256]{3,2,1,0:T(8,128)S(1)} copy-done((f32[4,5,32,256]{3,2,1,0:T(8,128)S(1)}, f32[4,5,32,256]{3,2,1,0:T(8,128)}, u32[]{:S(2)}) %copy-start) | copy-done | bytes 655384
  1.1 0.3 %shard_map.55 = (f32[4,5,32,256]{3,2,1,0:T(8,128)S(1)}, f32[100,256]{1,0:T(8,128)S(1)}) custom-call(f32[4,5,32,256]{3,2,1,0:T(8,128)S(1)} %copy-done), custom_call_target="tpu_custom_call" | custom-call | tf_op jit(solution)/shard_map/pallas_call | solution.py:354
  1.4 0.1 collective-permute-start
  1.5 0.0 copy-start.1
  1.5 1.6 %collective-permute-start.1 = (f32[100,256]{1,0:T(8,128)S(1)}, f32[100,256]{1,0:T(8,128)S(1)}, u32[]{:S(2)}, u32[]{:S(2)}) collective-permute-start(f32[100,256]{1,0:T(8,128)S(1)} %get-tuple-element.22.own_ref), channel_id=1, source_target_pairs={{0,1},{1,0},{2,3},{3,2},{4,5},{5,4},{6,7},{7,6},{8,9},{9,8},{10,11... | collective-permute-start | bytes 307208 | tf_op jit(solution)/shard_map/ppermute | solution.py:347
  3.1 0.2 shard_map.57
  3.3 0.0 copy-start.2
  3.3 0.0 copy-start.3
  3.3 0.3 %collective-permute-start.7 = (f32[1,5,32,256]{3,2,1,0:T(8,128)S(1)}, f32[1,5,32,256]{3,2,1,0:T(8,128)S(1)}, u32[]{:S(2)}, u32[]{:S(2)}) collective-permute-start(f32[1,5,32,256]{3,2,1,0:T(8,128)S(1)} %get-tuple-element.34.refs_2_), channel_id=1, source_target_pairs={{2,4},{3,5},{6,8},{7,9},{10,12},{11,13},{14,16},{15,17},{18,20},{1... | collective-permute-start | bytes 491528 | tf_op jit(solution)/shard_map/ppermute | solution.py:386
  3.6 1.0 %first.1.refs_0_ = f32[1,5,32,256]{3,2,1,0:T(8,128)S(1)} custom-call(f32[4,5,32,256]{3,2,1,0:T(8,128)} %x_ref.7), custom_call_target="tpu_custom_call" | custom-call | tf_op jit(solution)/shard_map/first/pallas_call | solution.py:371
  4.6 1.5 %collective-permute-start.6 = (f32[1,5,32,256]{3,2,1,0:T(8,128)S(1)}, f32[1,5,32,256]{3,2,1,0:T(8,128)S(1)}, u32[]{:S(2)}, u32[]{:S(2)}) collective-permute-start(f32[1,5,32,256]{3,2,1,0:T(8,128)S(1)} %first.1.refs_0_), channel_id=1, source_target_pairs={{2,4},{3,5},{6,8},{7,9},{10,12},{11,13},{14,16},{15,17},{18,20},{1... | collective-permute-start | bytes 491528 | tf_op jit(solution)/shard_map/ppermute | solution.py:386
  6.1 0.0 copy-start.4
  6.1 0.0 copy-start.5
  6.1 0.3 %collective-permute-start.4 = (f32[1,5,32,256]{3,2,1,0:T(8,128)S(1)}, f32[1,5,32,256]{3,2,1,0:T(8,128)S(1)}, u32[]{:S(2)}, u32[]{:S(2)}) collective-permute-start(f32[1,5,32,256]{3,2,1,0:T(8,128)S(1)} %get-tuple-element.31.refs_0_), channel_id=1, source_target_pairs={{2,4},{3,5},{6,8},{7,9},{10,12},{11,13},{14,16},{15,17},{18,20},{1... | collective-permute-start | bytes 491528 | tf_op jit(solution)/shard_map/ppermute | solution.py:386
  6.4 0.4 %collective-permute-done.1.left_ref.right_ref.across_ref = f32[100,256]{1,0:T(8,128)S(1)} collective-permute-done((f32[100,256]{1,0:T(8,128)S(1)}, f32[100,256]{1,0:T(8,128)S(1)}, u32[]{:S(2)}, u32[]{:S(2)}) %collective-permute-start.1) | collective-permute-done | bytes 102432 | tf_op jit(solution)/shard_map/ppermute | solution.py:347
  6.9 1.0 %collective-permute-start.2 = (f32[1,5,32,256]{3,2,1,0:T(8,128)S(1)}, f32[1,5,32,256]{3,2,1,0:T(8,128)S(1)}, u32[]{:S(2)}, u32[]{:S(2)}) collective-permute-start(f32[1,5,32,256]{3,2,1,0:T(8,128)S(1)} %get-tuple-element.25.refs_0_), channel_id=1, source_target_pairs={{2,4},{3,5},{6,8},{7,9},{10,12},{11,13},{14,16},{15,17},{18,20},{1... | collective-permute-start | bytes 491528 | tf_op jit(solution)/shard_map/ppermute | solution.py:386
  7.9 0.0 collective-permute-done.inner_ref
  7.9 0.0 copy-done.1
  7.9 0.0 copy-done.2
  7.9 0.0 copy-done.3
  7.9 0.0 copy-done.4
  7.9 0.0 copy-done.5
  7.9 2.8 %shard_map.56 = (f32[4,5,32,256]{3,2,1,0:T(8,128)S(1)}, f32[32,128]{1,0:T(8,128)S(1)}, f32[4,32,128]{2,1,0:T(8,128)S(1)}, bf16[2,256,128]{2,1,0:T(8,128)(2,1)S(1)}, bf16[2,128,256]{2,1,0:T(8,128)(2,1)S(1)}) custom-call(f32[4,5,32,256]{3,2,1,0:T(8,128)S(1)} %copy-done.1, f32[4,5,32,256]{3,2,1,0:T(8,128)S(1)} %collective-permute-done.inner_ref, ...), custom_call_target="tpu_custom_call" | custom-call | tf_op jit(solution)/shard_map/pallas_call | solution.py:354
  10.8 0.0 collective-permute-done.7.refs_3_
  10.8 6.1 %collective-permute-done.6.refs_1_ = f32[1,5,32,256]{3,2,1,0:T(8,128)S(1)} collective-permute-done((f32[1,5,32,256]{3,2,1,0:T(8,128)S(1)}, f32[1,5,32,256]{3,2,1,0:T(8,128)S(1)}, u32[]{:S(2)}, u32[]{:S(2)}) %collective-permute-start.6) | collective-permute-done | bytes 163872 | tf_op jit(solution)/shard_map/ppermute | solution.py:386
  16.9 0.3 %shard_map.60 = (f32[2,5,32,256]{3,2,1,0:T(8,128)S(1)}, f32[320,128]{1,0:T(8,128)S(1)}) custom-call(f32[4,5,32,256]{3,2,1,0:T(8,128)S(1)} %get-tuple-element.23.base_ref, bf16[2,256,128]{2,1,0:T(8,128)(2,1)S(1)} %get-tuple-element.24.basis_ref, f32[1,5,32,256]{3,2,1,0:T(8,128)S(1)} %first.1.refs_0_, f32[1,5,32,256]{3,2,1,0:T(8,128)S(1)} %collective-permute-done.6.refs_1_, ...), custom_call_target="tpu_custom_call" | custom-call | tf_op jit(solution)/shard_map/pallas_call | solution.py:354
  17.2 0.6 %collective-permute-start.8 = (f32[320,128]{1,0:T(8,128)S(1)}, f32[320,128]{1,0:T(8,128)S(1)}, u32[]{:S(2)}, u32[]{:S(2)}) collective-permute-start(f32[320,128]{1,0:T(8,128)S(1)} %get-tuple-element.36.mine_ref), channel_id=1, source_target_pairs={{0,1},{1,0},{2,3},{3,2},{4,5},{5,4},{6,7},{7,6},{8,9},{9,8},{10,11... | collective-permute-start | bytes 491528 | tf_op jit(solution)/shard_map/ppermute | solution.py:347
  17.7 0.9 %collective-permute-done.4.refs_1_ = f32[1,5,32,256]{3,2,1,0:T(8,128)S(1)} collective-permute-done((f32[1,5,32,256]{3,2,1,0:T(8,128)S(1)}, f32[1,5,32,256]{3,2,1,0:T(8,128)S(1)}, u32[]{:S(2)}, u32[]{:S(2)}) %collective-permute-start.4) | collective-permute-done | bytes 163872 | tf_op jit(solution)/shard_map/ppermute | solution.py:386
  18.6 0.2 shard_map.59
  18.8 0.7 %collective-permute-start.5 = (f32[160,128]{1,0:T(8,128)S(1)}, f32[160,128]{1,0:T(8,128)S(1)}, u32[]{:S(2)}, u32[]{:S(2)}) collective-permute-start(f32[160,128]{1,0:T(8,128)S(1)} %get-tuple-element.33.mine_ref), channel_id=1, source_target_pairs={{0,1},{1,0},{2,3},{3,2},{4,5},{5,4},{6,7},{7,6},{8,9},{9,8},{10,11... | collective-permute-start | bytes 245768 | tf_op jit(solution)/shard_map/ppermute | solution.py:347
  19.6 0.8 %collective-permute-done.2.refs_1_ = f32[1,5,32,256]{3,2,1,0:T(8,128)S(1)} collective-permute-done((f32[1,5,32,256]{3,2,1,0:T(8,128)S(1)}, f32[1,5,32,256]{3,2,1,0:T(8,128)S(1)}, u32[]{:S(2)}, u32[]{:S(2)}) %collective-permute-start.2) | collective-permute-done | bytes 163872 | tf_op jit(solution)/shard_map/ppermute | solution.py:386
  20.4 0.2 shard_map.58
  20.6 0.6 %collective-permute-start.3 = (f32[160,128]{1,0:T(8,128)S(1)}, f32[160,128]{1,0:T(8,128)S(1)}, u32[]{:S(2)}, u32[]{:S(2)}) collective-permute-start(f32[160,128]{1,0:T(8,128)S(1)} %get-tuple-element.27.mine_ref), channel_id=1, source_target_pairs={{0,1},{1,0},{2,3},{3,2},{4,5},{5,4},{6,7},{7,6},{8,9},{9,8},{10,11... | collective-permute-start | bytes 245768 | tf_op jit(solution)/shard_map/ppermute | solution.py:347
  21.2 1.3 %collective-permute-done.8.other_ref = f32[320,128]{1,0:T(8,128)S(1)} collective-permute-done((f32[320,128]{1,0:T(8,128)S(1)}, f32[320,128]{1,0:T(8,128)S(1)}, u32[]{:S(2)}, u32[]{:S(2)}) %collective-permute-start.8) | collective-permute-done | bytes 163872 | tf_op jit(solution)/shard_map/ppermute | solution.py:347
  22.6 1.0 %shard_map.61.refs_0_ = f32[4,5,32,256]{3,2,1,0:T(8,128)} custom-call(f32[2,5,32,256]{3,2,1,0:T(8,128)S(1)} %get-tuple-element.35.section_ref, f32[320,128]{1,0:T(8,128)S(1)} %get-tuple-element.36.mine_ref, f32[320,128]{1,0:T(8,128)S(1)} %collective-permute-done.8.other_ref, f32[32,128]{1,0:T(8,128)S(1)} %get-tuple-element.28.weight_ref, ...), custom_call_target="tpu_custom_call" | custom-call | tf_op jit(solution)/shard_map/pallas_call | solution.py:414
  23.6 0.0 collective-permute-done.5.other_ref
  23.6 0.9 %shard_map.62.refs_0_ = f32[4,5,32,256]{3,2,1,0:T(8,128)} custom-call(f32[1,5,32,256]{3,2,1,0:T(8,128)S(1)} %get-tuple-element.32.section_ref, f32[160,128]{1,0:T(8,128)S(1)} %get-tuple-element.33.mine_ref, f32[160,128]{1,0:T(8,128)S(1)} %collective-permute-done.5.other_ref, ...), custom_call_target="tpu_custom_call", output_to_operand_aliasing={{}: (6, {})} | custom-call | tf_op jit(solution)/shard_map/pallas_call | solution.py:414
  24.5 0.6 %collective-permute-done.3.other_ref = f32[160,128]{1,0:T(8,128)S(1)} collective-permute-done((f32[160,128]{1,0:T(8,128)S(1)}, f32[160,128]{1,0:T(8,128)S(1)}, u32[]{:S(2)}, u32[]{:S(2)}) %collective-permute-start.3) | collective-permute-done | bytes 81952 | tf_op jit(solution)/shard_map/ppermute | solution.py:347
  25.1 0.9 %shard_map.63 = f32[4,5,32,256]{3,2,1,0:T(8,128)} custom-call(f32[1,5,32,256]{3,2,1,0:T(8,128)S(1)} %get-tuple-element.26.section_ref, f32[160,128]{1,0:T(8,128)S(1)} %get-tuple-element.27.mine_ref, f32[160,128]{1,0:T(8,128)S(1)} %collective-permute-done.3.other_ref, f32[32,128]{1,0:T(8,128)S(1)} %get-tuple-element.28.weight_ref, ...), custom_call_target="tpu_custom_call", output_to_operand_aliasing={{}: (6, {})} | custom-call | tf_op jit(solution)/shard_map/pallas_call | solution.py:414
Async XLA Ops:
  0.0 1.1 %copy-start = (f32[4,5,32,256]{3,2,1,0:T(8,128)S(1)}, f32[4,5,32,256]{3,2,1,0:T(8,128)}, u32[]{:S(2)}) copy-start(f32[4,5,32,256]{3,2,1,0:T(8,128)} %x_ref.7) | copy-start | bytes 1966084
  1.4 6.5 %collective-permute-start = (f32[4,5,32,256]{3,2,1,0:T(8,128)S(1)}, f32[4,5,32,256]{3,2,1,0:T(8,128)S(1)}, u32[]{:S(2)}, u32[]{:S(2)}) collective-permute-start(f32[4,5,32,256]{3,2,1,0:T(8,128)S(1)} %get-tuple-element.21), channel_id=1, source_target_pairs={{0,2},{2,0},{4,6},{6,4},{8,10},{10,8},{12,14},{14,12},{16,18},{18,... | collective-permute-start | bytes 1966088 | tf_op jit(solution)/shard_map/ppermute | solution.py:387
  1.5 6.4 %copy-start.1 = (f32[4,5,32,256]{3,2,1,0:T(8,128)S(1)}, f32[4,5,32,256]{3,2,1,0:T(8,128)}, u32[]{:S(2)}) copy-start(f32[4,5,32,256]{3,2,1,0:T(8,128)} %x_ref.7) | copy-start | bytes 1966084
  1.5 5.4 %collective-permute-start.1 = (f32[100,256]{1,0:T(8,128)S(1)}, f32[100,256]{1,0:T(8,128)S(1)}, u32[]{:S(2)}, u32[]{:S(2)}) collective-permute-start(f32[100,256]{1,0:T(8,128)S(1)} %get-tuple-element.22.own_ref), channel_id=1, source_target_pairs={{0,1},{1,0},{2,3},{3,2},{4,5},{5,4},{6,7},{7,6},{8,9},{9,8},{10,11... | collective-permute-start | bytes 307208 | tf_op jit(solution)/shard_map/ppermute | solution.py:347
  3.3 4.6 %copy-start.2 = (f32[2,256,128]{2,1,0:T(8,128)S(1)}, f32[2,256,128]{2,1,0:T(8,128)}, u32[]{:S(2)}) copy-start(f32[2,256,128]{2,1,0:T(8,128)} %constant.4.clone.table_ref) | copy-start | bytes 786436
  3.3 4.6 %copy-start.3 = (f32[2,128,256]{2,1,0:T(8,128)S(1)}, f32[2,128,256]{2,1,0:T(8,128)}, u32[]{:S(2)}) copy-start(f32[2,128,256]{2,1,0:T(8,128)} %constant.5.clone.back_ref) | copy-start | bytes 786436
  3.3 7.5 %collective-permute-start.7 = (f32[1,5,32,256]{3,2,1,0:T(8,128)S(1)}, f32[1,5,32,256]{3,2,1,0:T(8,128)S(1)}, u32[]{:S(2)}, u32[]{:S(2)}) collective-permute-start(f32[1,5,32,256]{3,2,1,0:T(8,128)S(1)} %get-tuple-element.34.refs_2_), channel_id=1, source_target_pairs={{2,4},{3,5},{6,8},{7,9},{10,12},{11,13},{14,16},{15,17},{18,20},{1... | collective-permute-start | bytes 491528 | tf_op jit(solution)/shard_map/ppermute | solution.py:386
  4.6 12.3 %collective-permute-start.6 = (f32[1,5,32,256]{3,2,1,0:T(8,128)S(1)}, f32[1,5,32,256]{3,2,1,0:T(8,128)S(1)}, u32[]{:S(2)}, u32[]{:S(2)}) collective-permute-start(f32[1,5,32,256]{3,2,1,0:T(8,128)S(1)} %first.1.refs_0_), channel_id=1, source_target_pairs={{2,4},{3,5},{6,8},{7,9},{10,12},{11,13},{14,16},{15,17},{18,20},{1... | collective-permute-start | bytes 491528 | tf_op jit(solution)/shard_map/ppermute | solution.py:386
  6.1 1.8 %copy-start.4 = (s32[32]{0:T(128)S(1)}, s32[32]{0:T(128)}, u32[]{:S(2)}) copy-start(s32[32]{0:T(128)} %modes_ref.1) | copy-start | bytes 388
  6.1 1.8 %copy-start.5 = (s32[4]{0:T(128)S(1)}, s32[4]{0:T(128)}, u32[]{:S(2)}) copy-start(s32[4]{0:T(128)} %limit_ref.1) | copy-start | bytes 52
  6.1 12.5 %collective-permute-start.4 = (f32[1,5,32,256]{3,2,1,0:T(8,128)S(1)}, f32[1,5,32,256]{3,2,1,0:T(8,128)S(1)}, u32[]{:S(2)}, u32[]{:S(2)}) collective-permute-start(f32[1,5,32,256]{3,2,1,0:T(8,128)S(1)} %get-tuple-element.31.refs_0_), channel_id=1, source_target_pairs={{2,4},{3,5},{6,8},{7,9},{10,12},{11,13},{14,16},{15,17},{18,20},{1... | collective-permute-start | bytes 491528 | tf_op jit(solution)/shard_map/ppermute | solution.py:386
  6.9 13.5 %collective-permute-start.2 = (f32[1,5,32,256]{3,2,1,0:T(8,128)S(1)}, f32[1,5,32,256]{3,2,1,0:T(8,128)S(1)}, u32[]{:S(2)}, u32[]{:S(2)}) collective-permute-start(f32[1,5,32,256]{3,2,1,0:T(8,128)S(1)} %get-tuple-element.25.refs_0_), channel_id=1, source_target_pairs={{2,4},{3,5},{6,8},{7,9},{10,12},{11,13},{14,16},{15,17},{18,20},{1... | collective-permute-start | bytes 491528 | tf_op jit(solution)/shard_map/ppermute | solution.py:386
  17.2 5.4 %collective-permute-start.8 = (f32[320,128]{1,0:T(8,128)S(1)}, f32[320,128]{1,0:T(8,128)S(1)}, u32[]{:S(2)}, u32[]{:S(2)}) collective-permute-start(f32[320,128]{1,0:T(8,128)S(1)} %get-tuple-element.36.mine_ref), channel_id=1, source_target_pairs={{0,1},{1,0},{2,3},{3,2},{4,5},{5,4},{6,7},{7,6},{8,9},{9,8},{10,11... | collective-permute-start | bytes 491528 | tf_op jit(solution)/shard_map/ppermute | solution.py:347
  18.8 4.7 %collective-permute-start.5 = (f32[160,128]{1,0:T(8,128)S(1)}, f32[160,128]{1,0:T(8,128)S(1)}, u32[]{:S(2)}, u32[]{:S(2)}) collective-permute-start(f32[160,128]{1,0:T(8,128)S(1)} %get-tuple-element.33.mine_ref), channel_id=1, source_target_pairs={{0,1},{1,0},{2,3},{3,2},{4,5},{5,4},{6,7},{7,6},{8,9},{9,8},{10,11... | collective-permute-start | bytes 245768 | tf_op jit(solution)/shard_map/ppermute | solution.py:347
  20.6 4.5 %collective-permute-start.3 = (f32[160,128]{1,0:T(8,128)S(1)}, f32[160,128]{1,0:T(8,128)S(1)}, u32[]{:S(2)}, u32[]{:S(2)}) collective-permute-start(f32[160,128]{1,0:T(8,128)S(1)} %get-tuple-element.27.mine_ref), channel_id=1, source_target_pairs={{0,1},{1,0},{2,3},{3,2},{4,5},{5,4},{6,7},{7,6},{8,9},{9,8},{10,11... | collective-permute-start | bytes 245768 | tf_op jit(solution)/shard_map/ppermute | solution.py:347
